TPU v7x, 256 devices: a whole 4x4x8 slice. The times are simulated.
256 devices in a mesh: param: 32 (over y, z_hi, core), tm: 8 (over z_lo, x).
Axes of the slice: x: 4, y: 4, z: 8 (z_hi: 4, z_lo: 2; z = z_hi * 2 + z_lo), core: 2. Of those that a mesh axis runs over, the one named last changes fastest.
Arguments:
- params: bfloat16 [32, 128, 16384], P(None, 'tm', 'param'), may hold values from -6 to 6
- kernel: bfloat16 [8, 16384, 600], P(None, 'param'), may hold values from -0.015625 to 0.015625
- lag_offsets: int32 [8], replicated, may hold values from 0 to 11, as said below
- observed: bfloat16 [32, 128, 600], P(None, 'tm'), may hold values from -6 to 6
- diag_inverse: float32 [600, 600], replicated, may hold values from -2 to 2, as said below
- coupling: float32 [3, 600, 600], replicated, may hold values from -26 to 26
Outputs:
- whitened: float32 [32, 128, 600], P(None, 'tm')
Inputs may be any that keep to these rules, and one draw needn't show every extreme that they name: `lag_offsets`: the offsets are distinct and one of them is always 12 - 1. `diag_inverse`: lower triangular with a positive diagonal.
All inputs are finite; a program needn't handle non-finite values.
Results may differ from a plain program's by a relative error of at most 0.0003.
Values may be sent and summed in bfloat16 or wider, within the bound.
No kernel may reach another device: no remote copies, remote signals or barrier semaphores. Data moves between devices by JAX's collectives and lax.ppermute only.
A program may use at most 64 MiB of HBM per device.

v0:
```python
import jax
import jax.numpy as jnp
from jax import lax
from jax.sharding import PartitionSpec as P

REACH = 12


def from_behind(block, axis, distance):
    devices = range(lax.axis_size(axis))
    route = [(i - distance, i) for i in devices if i - distance in devices]
    return lax.ppermute(block, axis, route)


def in_blocks(array, dim, length):
    shape = array.shape
    parts = array.reshape(*shape[:dim], length, shape[dim] // length, *shape[dim + 1 :])
    return jnp.moveaxis(parts, dim, 0)


def summed_on_arrival(array, axis, dim):
    length = lax.axis_size(axis)
    parts = lax.all_to_all(in_blocks(array, dim, length), axis, 0, 0, tiled=True)
    return jnp.sum(parts, axis=0)


def sent_to_all(array, axis):
    length = lax.axis_size(axis)
    return lax.all_to_all(
        jnp.broadcast_to(array[None], (length, *array.shape)), axis, 0, 0, tiled=True
    )


def in_order(parts, dim):
    shape = list(parts.shape[1:])
    shape[dim] *= parts.shape[0]
    return jnp.moveaxis(parts, 0, dim).reshape(shape)


def gather_directly(array, axis, dim):
    parts = sent_to_all(array, axis)
    return in_order(parts, dim)


def solve_block(misfit, incoming, diag_inverse, coupling):

    def advance(history, current):
        balance = current - jnp.einsum(
            "jsn,jmn->sm", history, coupling, precision=lax.Precision.HIGHEST
        )
        solved = jnp.dot(balance, diag_inverse.T, precision=lax.Precision.HIGHEST)
        history = jnp.concatenate([solved[None], history[:-1]], axis=0)
        return (history, solved)

    final_history, solved_all = lax.scan(advance, incoming, jnp.swapaxes(misfit, 0, 1))
    return (jnp.swapaxes(solved_all, 0, 1), final_history)


def per_device(params, kernel, lag_offsets, observed, diag_inverse, coupling):
    samples, step_count, col_count = params.shape
    lag_count, unused_cols, sensors = kernel.shape
    flat_kernel = kernel.reshape(lag_count * col_count, sensors)
    rim = from_behind(params[:, step_count - (REACH - 1) :, :], "tm", 1)
    source = jnp.concatenate([rim, params], axis=1)
    windows = [
        lax.dynamic_slice_in_dim(source, REACH - 1 - lag_offsets[lag_index], step_count, 1)
        for lag_index in range(lag_count)
    ]
    stacked = jnp.stack(windows, axis=2).reshape(samples * step_count, lag_count * col_count)
    product = jnp.dot(stacked, flat_kernel, preferred_element_type=jnp.float32)
    local = product.reshape(samples, step_count, sensors)
    summed = summed_on_arrival(local, "param", 0)
    share = summed.shape[0]
    mine = lax.dynamic_slice_in_dim(observed, lax.axis_index("param") * share, share, 0)
    misfit = mine.astype(jnp.float32) - summed
    local_samples = misfit.shape[0]
    position = lax.axis_index("tm")
    state = jnp.zeros((coupling.shape[0], local_samples, sensors), jnp.float32)
    outputs = jnp.zeros_like(misfit)

    def turn(turn_index, carry):
        solved_now, history = carry
        incoming = from_behind(history, "tm", 1)
        return lax.cond(
            position == turn_index,
            lambda: solve_block(misfit, incoming, diag_inverse, coupling),
            lambda: (solved_now, history),
        )

    outputs, state = lax.fori_loop(0, lax.axis_size("tm"), turn, (outputs, state))
    return gather_directly(outputs, "param", 0)


def solution(mesh):
    in_specs = (P(None, "tm", "param"), P(None, "param", None), P(), P(None, "tm", None), P(), P())
    out_specs = P(None, "tm", None)
    return jax.shard_map(
        per_device, mesh=mesh, in_specs=in_specs, out_specs=out_specs, check_vma=False
    )
```

profile of v0, /device:TPU:39, one launch (start us, length us, event | category | flops | bytes accessed | tf_op | source)
XLA Modules:
  0.0 1202.0 jit_solution(16552093615139092600)
XLA Ops:
  0.0 1.3 slice.30
  1.3 1.3 collective-permute-start.1
  2.6 1.6 fusion.31
  14.3 1.7 collective-permute-done.1
  16.0 1.6 fusion.11
  17.6 1.5 fusion.14
  21.8 4.5 fusion.3
  26.3 11.9 all-to-all-start
  38.8 34.2 %all-to-all-done = f32[32,1,16,600]{3,2,1,0:T(8,128)S(1)} async-done(((f32[32,1,16,600]{3,2,1,0:T(8,128)}), f32[32,1,16,600]{3,2,1,0:T(8,128)S(1)}, u32[]{:S(2)}, u32[]{:S(2)}) %all-to-all-start) | async-done | bytes 1228832 | tf_op jit(solution)/shard_map/all_to_all | solution.py:23
  73.0 0.8 fusion.30
  74.5 1084.0 %while.27 = (s32[]{:T(128)}, f32[1,16,600]{2,0,1:T(1,128)}, f32[3,1,600]{2,1,0:T(1,128)S(1)}, s32[]{:T(128)}, f32[1,16,600]{2,0,1:T(1,128)S(1)}, /*index=5*/f32[...) while((s32[]{:T(128)}, f32[1,16,600]{2,0,1:T(1,128)}, f32[3,1,600]{2,1,0:T(1,128)S(1)}, s32[]{:T(128)}, ...), condition=%wide.region_6.7_spmd, body=%wide.region_1.6_spmd.sunk | while | flops 17282404 | bytes 5861828 | solution.py:90
  74.5 1.3 collective-permute-start
  75.8 3.1 collective-permute-done
  78.9 1.3 collective-permute-start
  80.2 3.1 collective-permute-done
  83.3 1.3 collective-permute-start
  84.6 3.1 collective-permute-done
  87.6 1.3 collective-permute-start
  88.9 3.1 collective-permute-done
  92.0 1.3 collective-permute-start
  93.3 4.5 collective-permute-done
  97.8 1.3 collective-permute-start
  99.1 5.2 collective-permute-done
  104.3 1.3 collective-permute-start
  105.6 5.5 collective-permute-done
  111.1 1.3 collective-permute-start
  112.4 914.1 %collective-permute-done = f32[3,1,600]{2,1,0:T(1,128)S(1)} collective-permute-done((f32[3,1,600]{2,1,0:T(1,128)S(1)}, f32[3,1,600]{2,1,0:T(1,128)S(1)}, u32[]{:S(2)}, u32[]{:S(2)}) %collective-permute-start) | collective-permute-done | bytes 7232 | tf_op jit(solution)/shard_map/while/body/eval_jaxpr/ppermute | solution.py:12
  1026.5 132.0 %conditional.2 = ((f32[1,16,600]{2,0,1:T(1,128)}, f32[3,1,600]{2,1,0:T(1,128)S(1)})) conditional(s32[]{:T(128)} %convert_element_type.15, (f32[1,16,600]{2,0,1:T(1,128)}, f32[3,1,600]{2,1,0:T(1,128)S(1)}) %tuple.57, (f32[1,16,600]{2,0,1:T(1,128)S(1)}, f32[3,600,600]{2,1,0:T(8,128)}, f32[600,600]{1,0:T(8,128)S(1)}, f32[3,1,600]{2,1,0:T(1,128)S(1)}) %tuple.58), branch_computations={%region_2.0_spmd, %region_3.5_spmd} | conditional | flops 17282400 | bytes 5832841 | solution.py:84
  1026.5 131.9 %while.26 = (s32[]{:T(128)}, f32[3,1,600]{2,1,0:T(1,128)S(1)}, f32[16,1,600]{2,1,0:T(1,128)}, f32[16,1,600]{2,1,0:T(1,128)S(1)}, f32[3,600,600]{2,1,0:T(8,128)}, /*index=5*/f32[600,600]{1,0:T(8,128)S(1)}, s32[]{:T(128)}) while((s32[]{:T(128)}, f32[3,1,600]{2,1,0:T(1,128)S(1)}, f32[16,1,600]{2,1,0:T(1,128)}, f32[16,1,600]{2,1,0:T(1,128)S(1)}, ...), condition=%wide.region_5.4_spmd, body=%wide.region_4.3_spmd.sunk | while | flops 17282400 | bytes 5818353 | solution.py:55
  1026.5 6.2 convolution_reduce_fusion.2
  1032.7 2.0 constant_dynamic-update-slice_fusion.2
  1034.7 6.2 convolution_reduce_fusion.2
  1040.9 2.0 constant_dynamic-update-slice_fusion.2
  1043.0 6.2 convolution_reduce_fusion.2
  1049.2 2.0 constant_dynamic-update-slice_fusion.2
  1051.2 6.2 convolution_reduce_fusion.2
  1057.4 2.0 constant_dynamic-update-slice_fusion.2
  1059.5 6.2 convolution_reduce_fusion.2
  1065.7 2.0 constant_dynamic-update-slice_fusion.2
  1067.7 6.2 convolution_reduce_fusion.2
  1073.9 2.0 constant_dynamic-update-slice_fusion.2
  1076.0 6.2 convolution_reduce_fusion.2
  1082.2 2.0 constant_dynamic-update-slice_fusion.2
  1084.2 6.2 convolution_reduce_fusion.2
  1090.4 2.0 constant_dynamic-update-slice_fusion.2
  1092.5 6.2 convolution_reduce_fusion.2
  1098.7 2.0 constant_dynamic-update-slice_fusion.2
  1100.7 6.2 convolution_reduce_fusion.2
  1106.9 2.0 constant_dynamic-update-slice_fusion.2
  1109.0 6.2 convolution_reduce_fusion.2
  1115.2 2.0 constant_dynamic-update-slice_fusion.2
  1117.2 6.2 convolution_reduce_fusion.2
  1123.4 2.0 constant_dynamic-update-slice_fusion.2
  1125.5 6.2 convolution_reduce_fusion.2
  1131.7 2.0 constant_dynamic-update-slice_fusion.2
  1133.7 6.2 convolution_reduce_fusion.2
  1139.9 2.0 constant_dynamic-update-slice_fusion.2
  1142.0 6.2 convolution_reduce_fusion.2
  1148.2 2.0 constant_dynamic-update-slice_fusion.2
  1150.2 6.2 convolution_reduce_fusion.2
  1156.4 2.0 constant_dynamic-update-slice_fusion.2
  1158.4 0.8 copy.18
  1159.3 41.7 %all_to_all.10 = f32[32,1,16,600]{3,2,1,0:T(8,128)S(1)} all-to-all(f32[32,1,16,600]{3,2,1,0:T(8,128)S(1)} %broadcast_in_dim.22), channel_id=1, replica_groups=mesh['param'=32,'tm'=8] {'param'}, dimensions={0} | all-to-all | bytes 2457600 | tf_op jit(solution)/shard_map/all_to_all | solution.py:29
  1201.0 1.1 copy.54
  (111 shorter events, 4.7 us)
Async XLA Ops:
  0.0 38.2 %copy-start = (bf16[32,16,600]{2,1,0:T(8,128)(2,1)S(1)}, bf16[32,16,600]{2,1,0:T(8,128)(2,1)}, u32[]{:S(2)}) copy-start(bf16[32,16,600]{2,1,0:T(8,128)(2,1)} %param.15) | copy-start | bytes 1843204
  0.0 19.1 %copy-start.2 = (bf16[32,16,512]{2,1,0:T(8,128)(2,1)S(1)}, bf16[32,16,512]{2,1,0:T(8,128)(2,1)}, u32[]{:S(2)}) copy-start(bf16[32,16,512]{2,1,0:T(8,128)(2,1)} %param.12) | copy-start | bytes 1572868
  1.3 14.7 %collective-permute-start.1 = (bf16[32,11,512]{2,1,0:T(8,128)(2,1)S(1)}, bf16[32,11,512]{2,1,0:T(8,128)(2,1)S(1)}, u32[]{:S(2)}, u32[]{:S(2)}) collective-permute-start(bf16[32,11,512]{2,1,0:T(8,128)(2,1)S(1)} %slice.30), channel_id=1, source_target_pairs={{0,1},{1,2},{2,3},{3,4},{4,5},{5,6},{6,7},{8,9},{9,10},{10,11},{11... | collective-permute-start | bytes 1081352 | tf_op jit(solution)/shard_map/ppermute | solution.py:12
  16.0 5.7 slice-start
  19.5 2.2 slice-start.1
  21.8 52.7 %copy-start.1 = (f32[600,600]{1,0:T(8,128)S(1)}, f32[600,600]{1,0:T(8,128)}, u32[]{:S(2)}) copy-start(f32[600,600]{1,0:T(8,128)} %param.16) | copy-start | bytes 4320004
  26.3 46.7 %all-to-all-start = ((f32[32,1,16,600]{3,2,1,0:T(8,128)}), f32[32,1,16,600]{3,2,1,0:T(8,128)S(1)}, u32[]{:S(2)}, u32[]{:S(2)}) async-start(f32[32,1,16,600]{3,2,1,0:T(8,128)} %fusion.3), calls=%async_computation | async-start | bytes 2621440 | tf_op jit(solution)/shard_map/all_to_all | solution.py:23
  74.5 4.4 collective-permute-start
  78.9 4.4 collective-permute-start
  83.3 4.4 collective-permute-start
  87.6 4.4 collective-permute-start
  92.0 5.8 collective-permute-start
  97.8 6.5 collective-permute-start
  104.3 6.8 collective-permute-start
  111.1 915.4 %collective-permute-start = (f32[3,1,600]{2,1,0:T(1,128)S(1)}, f32[3,1,600]{2,1,0:T(1,128)S(1)}, u32[]{:S(2)}, u32[]{:S(2)}) collective-permute-start(f32[3,1,600]{2,1,0:T(1,128)S(1)} %get-tuple-element.344), channel_id=1, source_target_pairs={{0,1},{1,2},{2,3},{3,4},{4,5},{5,6},{6,7},{8,9},{9,10},{10,11},{11... | collective-permute-start | bytes 21608 | tf_op jit(solution)/shard_map/while/body/eval_jaxpr/ppermute | solution.py:12
where the time goes:
time: 1200 us
  waiting for transfers between devices  977 us (81%)
  matrix products  135 us (11%)
  blocking collectives  41.7 us (3%)
  starting transfers between devices  23.4 us (2%)
    ppermute x9, waiting for transfers between devices, from_behind(): return lax.ppermute(block, axis, route)  943 us
    dot_general x16, matrix products, advance(): jnp.einsum('jsn,jmn->sm', history, coupling, precision=lax.Precision.HIGH...  98.9 us
    all_to_all x1, blocking collectives, sent_to_all(): lax.all_to_all(jnp.broadcast_to(array[None], (length, *array.shape)), axi...  41.7 us
    all_to_all x1, waiting for transfers between devices, summed_on_arrival(): lax.all_to_all(in_blocks(array, dim, length), axis, 0, 0, tiled=True)  34.2 us
    dot_general x16, matrix products, advance(): solved = jnp.dot(balance, diag_inverse.T, precision=lax.Precision.HIGHEST)  31.7 us
  transfers between devices with their start and end apart: 10, of which 10 were waited for; matrix products, arithmetic and copies ran while one was open for 0% of the time, Pallas kernels for 0%

commit v1 on v0

v1 whole, which is shorter than its diff:
```python
import jax
import jax.numpy as jnp
from jax import lax
from jax.experimental import pallas as pl
from jax.experimental.pallas import tpu as pltpu
from jax.sharding import PartitionSpec as P

REACH = 12
LANES = 128


def from_behind(block, axis, distance):
    devices = range(lax.axis_size(axis))
    route = [(i - distance, i) for i in devices if i - distance in devices]
    return lax.ppermute(block, axis, route)


def sent_to_all(array, axis):
    length = lax.axis_size(axis)
    return lax.all_to_all(
        jnp.broadcast_to(array[None], (length, *array.shape)), axis, 0, 0, tiled=True
    )


def row_chunks(rows):
    return [(start, min(LANES, rows - start)) for start in range(0, rows, LANES)]


def chain_kernel(lags, steps, sensors, factors_ref, forcing_ref, solved_ref, later_ref):
    ahead = lags - 1
    width = factors_ref.shape[2]
    pieces = range(width // LANES)
    later_ref[...] = jnp.zeros_like(later_ref)
    for row in range(ahead):
        solved_ref[row] = jnp.zeros((1, width), jnp.float32)

    def lanes(piece):
        return slice(piece * LANES, (piece + 1) * LANES)

    def step(t, unused):
        diagonal = lax.broadcasted_iota(jnp.int32, (LANES, LANES), 0) == lax.broadcasted_iota(
            jnp.int32, (LANES, LANES), 1
        )
        behind = [
            [
                jnp.broadcast_to(solved_ref[t + ahead - 1 - back, :, lanes(c)], (8, LANES))
                for c in pieces
            ]
            for back in range(ahead)
        ]
        for piece, (start, rows) in enumerate(row_chunks(sensors)):
            sums = []
            for row in range(start, start + rows, 8):
                total = later_ref[row : row + 8, :]
                for c in pieces:
                    total = total + factors_ref[0, row : row + 8, lanes(c)] * behind[0][c]
                sums.append(total)
            column = jnp.sum(jnp.concatenate(sums, axis=0), axis=1, keepdims=True)
            line = jnp.sum(jnp.where(diagonal[:rows], column, 0.0), axis=0, keepdims=True)
            solved_ref[t + ahead, :, lanes(piece)] = line + forcing_ref[t, :, lanes(piece)]
        for start in range(0, sensors, 8):
            total = None
            for back in range(ahead):
                for c in pieces:
                    term = factors_ref[back + 1, start : start + 8, lanes(c)] * behind[back][c]
                    total = term if total is None else total + term
            later_ref[start : start + 8, :] = total
        return unused

    lax.fori_loop(0, steps, step, 0)


def run_chain(factors, forcing):
    lags, sensors, width = factors.shape
    steps = forcing.shape[0]
    solved = pl.pallas_call(
        lambda *refs: chain_kernel(lags, steps, sensors, *refs),
        out_shape=jax.ShapeDtypeStruct((steps + lags - 1, 1, width), jnp.float32),
        in_specs=[pl.BlockSpec(memory_space=pltpu.VMEM)] * 2,
        out_specs=pl.BlockSpec(memory_space=pltpu.VMEM),
        scratch_shapes=[pltpu.VMEM((sensors, LANES), jnp.float32)],
        name="chain",
    )(factors, forcing.reshape(steps, 1, width))
    return solved[lags - 1 :, 0, :]


def per_device(params, kernel, lag_offsets, observed, diag_inverse, coupling):
    samples, step_count, col_count = params.shape
    lag_count, unused_cols, sensors = kernel.shape
    width = -(-sensors // LANES) * LANES
    exact = lax.Precision.HIGHEST
    flat_kernel = kernel.reshape(lag_count * col_count, sensors)
    rim = from_behind(params[:, step_count - (REACH - 1) :, :], "tm", 1)
    source = jnp.concatenate([rim, params], axis=1)
    windows = [
        lax.dynamic_slice_in_dim(source, REACH - 1 - lag_offsets[lag_index], step_count, 1)
        for lag_index in range(lag_count)
    ]
    stacked = jnp.stack(windows, axis=2).reshape(samples * step_count, lag_count * col_count)
    product = jnp.dot(stacked, flat_kernel, preferred_element_type=jnp.float32)
    local = product.reshape(samples, step_count, sensors)
    group = lax.axis_size("param")
    share = samples // group
    parts = lax.all_to_all(
        local.reshape(group, share, step_count, sensors), "param", 0, 0, tiled=True
    )
    summed = jnp.sum(parts, axis=0)
    mine = lax.dynamic_slice_in_dim(observed, lax.axis_index("param") * share, share, 0)
    misfit = mine.astype(jnp.float32) - summed

    factors = -jnp.einsum("mi,jin->jmn", diag_inverse, coupling, precision=exact)
    factors = jnp.pad(factors, ((0, 0), (0, 0), (0, width - sensors)))
    forcing = jnp.einsum("stn,mn->stm", misfit, diag_inverse, precision=exact)
    forcing = jnp.pad(forcing, ((0, 0), (0, 0), (0, width - sensors)))
    every = sent_to_all(forcing, "tm")
    every = jnp.moveaxis(every, 0, 1).reshape(share, -1, width)
    solved = jnp.stack([run_chain(factors, every[s]) for s in range(share)])
    own = lax.dynamic_slice_in_dim(solved, lax.axis_index("tm") * step_count, step_count, 1)
    own = own[:, :, :sensors]
    parts = sent_to_all(own, "param")
    return parts.reshape(samples, step_count, sensors)


def solution(mesh):
    in_specs = (P(None, "tm", "param"), P(None, "param", None), P(), P(None, "tm", None), P(), P())
    out_specs = P(None, "tm", None)
    return jax.shard_map(
        per_device, mesh=mesh, in_specs=in_specs, out_specs=out_specs, check_vma=False
    )
```

time: 1200 us -> 195 us (0.16)
  waiting for transfers between devices: 977 us -> 36.7 us
  matrix products: 135 us -> 21.4 us
  Pallas kernels: 0 us -> 52.6 us
    ppermute x9 -> x1, waiting for transfers between devices: 943 us -> 1.98 us  [from_behind(): return lax.ppermute(block, axis, route)]
    dot_general x32 -> x2, matrix products: 131 us -> 16.9 us  [the longest x1 14.8 us: per_device(): jnp.einsum('mi,jin->jmn', diag_inverse, coupling, precision=exact)]
    pallas_call x0 -> x1, Pallas kernels: none -> 52.6 us  [run_chain(): pl.pallas_call(lambda *refs: chain_kernel(lags, steps, sensors, *refs), o...]
    all_to_all x1 -> x2, waiting for transfers between devices: 34.2 us -> 34.7 us  [the longest x1 34.7 us: per_device(): lax.all_to_all(local.reshape(group, share, step_count, sensors), 'param',...]
  transfers between devices with their start and end apart: 10 -> 3, of which waited for: 10 -> 2; matrix products, arithmetic and copies ran while one was open for 0% -> 10% of each run, Pallas kernels for 0% -> 0%
where the time goes in v1:
time: 195 us
  Pallas kernels  52.6 us (27%)
  blocking collectives  40.6 us (21%)
  waiting for transfers between devices  36.7 us (19%)
  matrix products  21.4 us (11%)
  starting transfers between devices  18.4 us (9%)
  between operations  9.97 us (5%)
  local copies, waits for them, and re-layouts  9.22 us (5%)
  other arithmetic  5.79 us (3%)
    pallas_call x1, Pallas kernels, run_chain(): pl.pallas_call(lambda *refs: chain_kernel(lags, steps, sensors, *refs), o...  52.6 us
    all_to_all x1, blocking collectives, sent_to_all(): lax.all_to_all(jnp.broadcast_to(array[None], (length, *array.shape)), axi...  40.6 us
    all_to_all x1, waiting for transfers between devices, per_device(): lax.all_to_all(local.reshape(group, share, step_count, sensors), 'param',...  34.7 us
    dot_general x1, matrix products, per_device(): jnp.einsum('mi,jin->jmn', diag_inverse, coupling, precision=exact)  14.8 us
    all_to_all x1, starting transfers between devices, per_device(): lax.all_to_all(local.reshape(group, share, step_count, sensors), 'param',...  11.9 us
    unnamed x8, other arithmetic  5.28 us
    all_to_all x1, starting transfers between devices, sent_to_all(): lax.all_to_all(jnp.broadcast_to(array[None], (length, *array.shape)), axi...  5.2 us
    dot_general x1, matrix products, per_device(): product = jnp.dot(stacked, flat_kernel, preferred_element_type=jnp.float32)  4.49 us
  transfers between devices with their start and end apart: 3, of which 2 were waited for; matrix products, arithmetic and copies ran while one was open for 10% of the time, Pallas kernels for 0%

profile of v1, /device:TPU:39, one launch (start us, length us, event | category | flops | bytes accessed | tf_op | source)
XLA Modules:
  0.0 194.8 jit_solution(12898620997486724260)
XLA Ops:
  0.0 0.0 copy-start
  0.0 0.0 copy-start.1
  0.0 1.3 slice.33
  1.3 1.3 collective-permute-start
  2.6 1.6 fusion.34
  14.1 2.0 %collective-permute-done = bf16[32,11,512]{2,1,0:T(8,128)(2,1)S(1)} collective-permute-done((bf16[32,11,512]{2,1,0:T(8,128)(2,1)S(1)}, bf16[32,11,512]{2,1,0:T(8,128)(2,1)S(1)}, u32[]{:S(2)}, u32[]{:S(2)}) %collective-permute-start) | collective-permute-done | bytes 360480 | tf_op jit(solution)/shard_map/ppermute | solution.py:15
  16.0 0.0 slice-start
  16.0 1.6 fusion.11
  17.6 1.5 fusion.14
  19.2 0.0 copy-done.1
  19.2 0.4 fusion.17
  19.6 0.0 slice-start.1
  19.6 0.4 fusion.20
  20.1 0.4 fusion.23
  20.5 0.4 fusion.26
  20.9 0.4 fusion.29
  21.4 0.4 fusion.8
  21.8 0.0 slice-done
  21.8 0.0 slice-done.1
  21.8 4.5 %fusion.3 = f32[32,1,16,600]{3,2,1,0:T(8,128)} fusion(bf16[32,16,8,512]{3,1,2,0:T(8,128)(2,1)S(1)} %fusion.8, bf16[8,512,600]{1,2,0:T(8,128)(2,1)S(1)} %bitcast.92), kind=kOutput, calls=%fused_computation.20 | convolution fusion | flops 2516582400 | bytes 10338304 | tf_op jit(solution)/shard_map/dot_general | solution.py:100
  26.3 11.9 %all-to-all-start = ((f32[32,1,16,600]{3,2,1,0:T(8,128)}), f32[32,1,16,600]{3,2,1,0:T(8,128)S(1)}, u32[]{:S(2)}, u32[]{:S(2)}) async-start(f32[32,1,16,600]{3,2,1,0:T(8,128)} %fusion.3), calls=%async_computation | async-start | bytes 2621440 | tf_op jit(solution)/shard_map/all_to_all | solution.py:104
  38.2 34.7 %all-to-all-done = f32[32,1,16,600]{3,2,1,0:T(8,128)S(1)} async-done(((f32[32,1,16,600]{3,2,1,0:T(8,128)}), f32[32,1,16,600]{3,2,1,0:T(8,128)S(1)}, u32[]{:S(2)}, u32[]{:S(2)}) %all-to-all-start) | async-done | bytes 1228832 | tf_op jit(solution)/shard_map/all_to_all | solution.py:104
  72.9 0.1 reduce_sum.11
  73.0 0.0 copy-done
  73.0 2.1 %convolution_bitcast_fusion = f32[1,16,600]{2,1,0:T(8,128)S(1)} fusion(f32[600,600]{1,0:T(8,128)S(1)} %copy-done, f32[16,600]{1,0:T(8,128)S(1)} %reduce_sum.11, bf16[32,16,600]{2,1,0:T(8,128)(2,1)} %param.9, s32[]{:T(128)S(6)} %select_n.30), kind=kOutput, calls=%fused_computation.21 | convolution fusion | flops 69139200 | bytes 1537284 | tf_op jit(solution)/shard_map/stn,mn->stm/dot_general | solution.py:113
  75.2 0.9 broadcast_in_dim.17
  76.1 5.2 %all-to-all-start.1 = ((f32[8,1,16,640]{3,1,2,0:T(1,128)}), f32[8,1,16,640]{3,1,2,0:T(1,128)S(1)}, u32[]{:S(2)}, u32[]{:S(2)}) async-start(f32[8,1,16,640]{3,1,2,0:T(1,128)} %broadcast_in_dim.17), calls=%async_computation.1 | async-start | bytes 655360 | tf_op jit(solution)/shard_map/all_to_all | solution.py:20
  81.3 14.8 %negate_bitcast_fusion = f32[3,600,600]{2,1,0:T(8,128)S(1)} fusion(f32[3,600,600]{2,1,0:T(8,128)} %param.11, f32[600,600]{1,0:T(8,128)S(1)} %copy-done), kind=kOutput, calls=%fused_computation.2 | convolution fusion | flops 7777080320 | bytes 10080000 | tf_op jit(solution)/shard_map/mi,jin->jmn/dot_general | solution.py:111
  96.1 2.4 %pad.8.refs_0_ = f32[3,600,640]{2,1,0:T(8,128)} pad(f32[3,600,600]{2,1,0:T(8,128)S(1)} %negate_bitcast_fusion, f32[]{:T(128)} %constant.39.clone.1), padding=0_0x0_0x0_40 | pad | bytes 8928004 | tf_op jit(solution)/shard_map/jit(_pad)/pad | solution.py:112
  98.5 0.0 all-to-all-done.1
  98.5 0.0 copy-start.2
  98.5 0.7 copy-done.2
  99.2 52.6 %chain.1 = f32[130,1,640]{2,1,0:T(1,128)} custom-call(f32[3,600,640]{2,1,0:T(8,128)} %pad.8.refs_0_, f32[128,1,640]{2,1,0:T(1,128)} %bitcast.88), custom_call_target="tpu_custom_call" | custom-call | tf_op jit(solution)/shard_map/chain/pallas_call | solution.py:76
  151.9 1.1 slice.44
  153.0 0.1 broadcast_in_dim.19
  153.1 40.6 %all_to_all.15 = f32[32,1,16,600]{3,2,1,0:T(8,128)S(1)} all-to-all(f32[32,1,16,600]{3,2,1,0:T(8,128)S(1)} %broadcast_in_dim.19), channel_id=1, replica_groups=mesh['param'=32,'tm'=8] {'param'}, dimensions={0} | all-to-all | bytes 2457600 | tf_op jit(solution)/shard_map/all_to_all | solution.py:20
  193.7 1.1 copy.20
  (4 shorter events, 0.0 us)
Async XLA Ops:
  0.0 73.0 %copy-start = (f32[600,600]{1,0:T(8,128)S(1)}, f32[600,600]{1,0:T(8,128)}, u32[]{:S(2)}) copy-start(f32[600,600]{1,0:T(8,128)} %param.10) | copy-start | bytes 4320004
  0.0 19.2 %copy-start.1 = (bf16[32,16,512]{2,1,0:T(8,128)(2,1)S(1)}, bf16[32,16,512]{2,1,0:T(8,128)(2,1)}, u32[]{:S(2)}) copy-start(bf16[32,16,512]{2,1,0:T(8,128)(2,1)} %param.6) | copy-start | bytes 1572868
  1.3 14.7 %collective-permute-start = (bf16[32,11,512]{2,1,0:T(8,128)(2,1)S(1)}, bf16[32,11,512]{2,1,0:T(8,128)(2,1)S(1)}, u32[]{:S(2)}, u32[]{:S(2)}) collective-permute-start(bf16[32,11,512]{2,1,0:T(8,128)(2,1)S(1)} %slice.33), channel_id=1, source_target_pairs={{0,1},{1,2},{2,3},{3,4},{4,5},{5,6},{6,7},{8,9},{9,10},{10,11},{11... | collective-permute-start | bytes 1081352 | tf_op jit(solution)/shard_map/ppermute | solution.py:15
  16.0 5.8 %slice-start = ((s8[4915200]{0:T(1024)(128)(4,1)}), s8[4194304]{0:T(1024)(128)(4,1)S(1)}, s32[]{:S(2)}) async-start(s8[4915200]{0:T(1024)(128)(4,1)} %bitcast.91), calls=%async_computation.3 | async-start | bytes 8388608
  19.6 2.2 %slice-start.1 = ((s8[4915200]{0:T(1024)(128)(4,1)}), s8[720896]{0:T(1024)(128)(4,1)S(1)}, s32[]{:S(2)}) async-start(s8[4915200]{0:T(1024)(128)(4,1)} %bitcast.91), calls=%async_computation.4 | async-start | bytes 1441792
  26.3 46.6 %all-to-all-start = ((f32[32,1,16,600]{3,2,1,0:T(8,128)}), f32[32,1,16,600]{3,2,1,0:T(8,128)S(1)}, u32[]{:S(2)}, u32[]{:S(2)}) async-start(f32[32,1,16,600]{3,2,1,0:T(8,128)} %fusion.3), calls=%async_computation | async-start | bytes 2621440 | tf_op jit(solution)/shard_map/all_to_all | solution.py:104
  76.1 22.4 %all-to-all-start.1 = ((f32[8,1,16,640]{3,1,2,0:T(1,128)}), f32[8,1,16,640]{3,1,2,0:T(1,128)S(1)}, u32[]{:S(2)}, u32[]{:S(2)}) async-start(f32[8,1,16,640]{3,1,2,0:T(1,128)} %broadcast_in_dim.17), calls=%async_computation.1 | async-start | bytes 655360 | tf_op jit(solution)/shard_map/all_to_all | solution.py:20
  98.5 0.7 copy-start.2

commit v2 on v1

v2 whole, which is shorter than its diff:
```python
import functools

import jax
import jax.numpy as jnp
from jax import lax
from jax.experimental import pallas as pl
from jax.experimental.pallas import tpu as pltpu
from jax.sharding import PartitionSpec as P

REACH = 12
LANES = 128
LEVELS = 32700.0
OCTAVE = 64.0
TINY = 1e-37


def from_behind(block, axis, distance):
    devices = range(lax.axis_size(axis))
    route = [(i - distance, i) for i in devices if i - distance in devices]
    return lax.ppermute(block, axis, route)


def sent_to_all(array, axis):
    length = lax.axis_size(axis)
    return lax.all_to_all(
        jnp.broadcast_to(array[None], (length, *array.shape)), axis, 0, 0, tiled=True
    )


def grade_of(rows):
    largest = jnp.maximum(jnp.max(jnp.abs(rows), axis=-1, keepdims=True), TINY)
    return jnp.ceil(jnp.log2(largest) * OCTAVE)


def coded(rows, grade):
    return jnp.round(rows * (LEVELS * jnp.exp2(grade * (-1.0 / OCTAVE))))


def scale_of(grade):
    return jnp.exp2(grade * (1.0 / OCTAVE)) * (1.0 / LEVELS)


def row_chunks(rows):
    return [(start, min(LANES, rows - start)) for start in range(0, rows, LANES)]


def chain_kernel(
    block, sensors, near_ref, two_hi, two_lo, three_hi, three_lo, forcing_ref,
    code_ref, solved_ref, later_ref, carry_ref, even_ref, odd_ref, far_ref,
):
    width = near_ref.shape[2]
    pieces = list(range(width // LANES))
    reach = two_hi.shape[0]
    rest = [c for c in pieces if c * LANES >= reach]
    for ref in (later_ref, carry_ref, even_ref, odd_ref):
        ref[...] = jnp.zeros_like(ref)
    dot = functools.partial(jnp.dot, preferred_element_type=jnp.float32)

    def lanes(piece):
        return slice(piece * LANES, (piece + 1) * LANES)

    def wide(row):
        return jnp.broadcast_to(row, (8, LANES))

    def pair(turn, unused):
        diagonal = lax.broadcasted_iota(jnp.int32, (LANES, LANES), 0) == lax.broadcasted_iota(
            jnp.int32, (LANES, LANES), 1
        )
        row_id = lax.broadcasted_iota(jnp.int32, (16, LANES), 0)
        split = []
        for c in pieces:
            older = jnp.concatenate([even_ref[:, lanes(c)]] * 2, axis=0)
            newer = jnp.concatenate([odd_ref[:, lanes(c)]] * 2, axis=0)
            both = jnp.where(row_id < 2, older, jnp.where(row_id < 4, newer, 0.0))
            high = both.astype(jnp.bfloat16).astype(jnp.float32)
            split.append(
                jnp.where((row_id == 0) | (row_id == 2), high, both - high).astype(jnp.bfloat16)
            )
        operand = jnp.concatenate(split, axis=1)
        front = operand[:, :reach]
        far_ref[0] = dot(front, two_hi[...]) + dot(front, two_lo[...])
        far_ref[1] = dot(operand, three_hi[...]) + dot(operand, three_lo[...])

        for half in range(2):
            t = 2 * turn + half
            prev_ref, new_ref = ((odd_ref, even_ref), (even_ref, odd_ref))[half]
            behind = [prev_ref[:, lanes(c)] for c in pieces]
            for piece, (start, rows) in enumerate(row_chunks(sensors)):
                sums = []
                for row in range(start, start + rows, 8):
                    total = later_ref[row : row + 8, :]
                    for c in pieces:
                        total = total + near_ref[0, row : row + 8, lanes(c)] * behind[c]
                    sums.append(total)
                column = jnp.sum(jnp.concatenate(sums, axis=0), axis=1, keepdims=True)
                line = jnp.sum(jnp.where(diagonal[:rows], column, 0.0), axis=0, keepdims=True)
                base = wide(forcing_ref[t, :, lanes(piece)])
                if half == 0:
                    base = base + wide(carry_ref[0:1, lanes(piece)])
                else:
                    base = base + (
                        wide(far_ref[1, 0:1, lanes(piece)]) + wide(far_ref[1, 1:2, lanes(piece)])
                    )
                base = base + (
                    wide(far_ref[0, 2 * half : 2 * half + 1, lanes(piece)])
                    + wide(far_ref[0, 2 * half + 1 : 2 * half + 2, lanes(piece)])
                )
                solved = wide(line) + base
                new_ref[:, lanes(piece)] = solved
                solved_ref[lax.rem(t, block), :, lanes(piece)] = solved[0:1]
            behind = {c: prev_ref[:, lanes(c)] for c in rest}
            for start in range(0, sensors, 8):
                total = None
                for c in rest:
                    term = near_ref[1, start : start + 8, lanes(c)] * behind[c]
                    total = term if total is None else total + term
                later_ref[start : start + 8, :] = total
        carry_ref[0:1, :] = far_ref[1, 2:3] + far_ref[1, 3:4]
        return unused

    turns = (lax.axis_index("tm") + 1) * (block // 2)
    lax.fori_loop(0, turns, pair, 0)
    own = jnp.concatenate([solved_ref[row] for row in range(block)], axis=0)
    grade = grade_of(own)
    place = lax.broadcasted_iota(jnp.int32, own.shape, 1)
    code = jnp.where(place == sensors, grade, coded(own, grade))
    code_ref[...] = code.astype(jnp.int32).astype(jnp.int16)


def run_chain(block, near, two_hi, two_lo, three_hi, three_lo, forcing):
    unused_lags, sensors, width = near.shape
    steps = forcing.shape[0]
    code, unused_rows = pl.pallas_call(
        functools.partial(chain_kernel, block, sensors),
        out_shape=(
            jax.ShapeDtypeStruct((block, width), jnp.int16),
            jax.ShapeDtypeStruct((block, 1, width), jnp.float32),
        ),
        in_specs=[pl.BlockSpec(memory_space=pltpu.VMEM)] * 6,
        out_specs=[pl.BlockSpec(memory_space=pltpu.VMEM)] * 2,
        scratch_shapes=[
            pltpu.VMEM((sensors, LANES), jnp.float32),
            pltpu.VMEM((8, width), jnp.float32),
            pltpu.VMEM((8, width), jnp.float32),
            pltpu.VMEM((8, width), jnp.float32),
            pltpu.VMEM((2, 16, width), jnp.float32),
        ],
        name="chain",
    )(near, two_hi, two_lo, three_hi, three_lo, forcing.reshape(steps, 1, width))
    return code


def high_low(array):
    high = array.astype(jnp.bfloat16).astype(jnp.float32)
    return high.astype(jnp.bfloat16), (array - high).astype(jnp.bfloat16)


def factor(diag_ref, coupling_ref, lag):
    sensors = diag_ref.shape[0]
    lines = []
    for start in range(0, sensors, 2 * LANES):
        end = min(start + 2 * LANES, sensors)
        lines.append(
            -jnp.dot(
                diag_ref[start:end, :end],
                coupling_ref[lag, :end, :],
                precision=lax.Precision.HIGHEST,
                preferred_element_type=jnp.float32,
            )
        )
    return jnp.concatenate(lines, axis=0)


def turned(square_ref, high_ref, low_ref):
    for row in range(0, high_ref.shape[0], LANES):
        for column in range(0, high_ref.shape[1], LANES):
            tile = square_ref[column : column + LANES, row : row + LANES].T
            high, low = high_low(tile)
            high_ref[row : row + LANES, column : column + LANES] = high
            low_ref[row : row + LANES, column : column + LANES] = low


def near_kernel(diag_ref, coupling_ref, near_ref, high_ref, low_ref, square_ref):
    sensors = diag_ref.shape[0]
    near_ref[...] = jnp.zeros_like(near_ref)
    square_ref[...] = jnp.zeros_like(square_ref)
    near_ref[0, :, :sensors] = factor(diag_ref, coupling_ref, 0)
    second = factor(diag_ref, coupling_ref, 1)
    near_ref[1, :, :sensors] = second
    square_ref[:sensors, :sensors] = second
    turned(square_ref, high_ref, low_ref)


def far_kernel(diag_ref, coupling_ref, high_ref, low_ref, square_ref):
    sensors = diag_ref.shape[0]
    square_ref[...] = jnp.zeros_like(square_ref)
    square_ref[:sensors, :sensors] = factor(diag_ref, coupling_ref, 0)
    turned(square_ref, high_ref, low_ref)


def prepare_near(diag_inverse, coupling, width):
    sensors = diag_inverse.shape[0]
    part = jax.ShapeDtypeStruct((2 * LANES, width), jnp.bfloat16)
    return pl.pallas_call(
        near_kernel,
        out_shape=(jax.ShapeDtypeStruct((2, sensors, width), jnp.float32), part, part),
        in_specs=[
            pl.BlockSpec((sensors, sensors), lambda _: (0, 0)),
            pl.BlockSpec((2, sensors, sensors), lambda _: (0, 0, 0)),
        ],
        out_specs=[
            pl.BlockSpec((2, sensors, width), lambda _: (0, 0, 0)),
            pl.BlockSpec((2 * LANES, width), lambda _: (0, 0)),
            pl.BlockSpec((2 * LANES, width), lambda _: (0, 0)),
        ],
        grid=(1,),
        scratch_shapes=[pltpu.VMEM((width, width), jnp.float32)],
        cost_estimate=pl.CostEstimate(
            flops=12 * 2 * sensors**3, bytes_accessed=16 * sensors**2, transcendentals=0
        ),
        name="near_factors",
    )(diag_inverse, coupling)


def prepare_far(diag_inverse, coupling, width):
    sensors = diag_inverse.shape[0]
    part = jax.ShapeDtypeStruct((width, width), jnp.bfloat16)
    return pl.pallas_call(
        far_kernel,
        out_shape=(part, part),
        in_specs=[
            pl.BlockSpec((sensors, sensors), lambda _: (0, 0)),
            pl.BlockSpec((1, sensors, sensors), lambda _: (2, 0, 0)),
        ],
        out_specs=[pl.BlockSpec((width, width), lambda _: (0, 0))] * 2,
        grid=(1,),
        scratch_shapes=[pltpu.VMEM((width, width), jnp.float32)],
        cost_estimate=pl.CostEstimate(
            flops=12 * sensors**3, bytes_accessed=12 * sensors**2, transcendentals=0
        ),
        name="far_factors",
    )(diag_inverse, coupling)


def predict_kernel(offsets_ref, source_ref, kernel_ref, code_ref, total_ref):
    steps, samples, cols = code_ref.shape[0], source_ref.shape[1], source_ref.shape[2]
    sensors = kernel_ref.shape[2]
    lag = pl.program_id(0)
    window = source_ref[pl.ds(REACH - 1 - offsets_ref[lag], steps)]
    product = jnp.dot(
        window.reshape(steps * samples, cols), kernel_ref[0], preferred_element_type=jnp.float32
    )

    @pl.when(lag == 0)
    def first():
        total_ref[...] = product

    @pl.when(lag > 0)
    def later():
        total_ref[...] = total_ref[...] + product

    @pl.when(lag == pl.num_programs(0) - 1)
    def last():
        for step in range(steps):
            rows = total_ref[step * samples : (step + 1) * samples, :]
            grade = grade_of(rows)
            code = coded(rows, grade)
            code_ref[step, :, :sensors] = code.astype(jnp.int32).astype(jnp.int16)
            code_ref[step, :, sensors : sensors + 1] = grade.astype(jnp.int32).astype(jnp.int16)


def predict(source, kernel, lag_offsets):
    lag_count, cols, sensors = kernel.shape
    span, samples, unused_cols = source.shape
    steps = span - (REACH - 1)
    return pl.pallas_call(
        predict_kernel,
        out_shape=jax.ShapeDtypeStruct((steps, samples, sensors + 1), jnp.int16),
        in_specs=[
            pl.BlockSpec(memory_space=pltpu.SMEM),
            pl.BlockSpec((span, samples, cols), lambda lag: (0, 0, 0)),
            pl.BlockSpec((1, cols, sensors), lambda lag: (lag, 0, 0)),
        ],
        out_specs=pl.BlockSpec((steps, samples, sensors + 1), lambda lag: (0, 0, 0)),
        grid=(lag_count,),
        scratch_shapes=[pltpu.VMEM((steps * samples, sensors), jnp.float32)],
        cost_estimate=pl.CostEstimate(
            flops=2 * steps * samples * lag_count * cols * sensors,
            bytes_accessed=2 * lag_count * cols * sensors,
            transcendentals=0,
        ),
        name="predict",
    )(lag_offsets, source, kernel)


def per_device(params, kernel, lag_offsets, observed, diag_inverse, coupling):
    samples, step_count, col_count = params.shape
    lag_count, unused_cols, sensors = kernel.shape
    width = -(-sensors // LANES) * LANES
    exact = lax.Precision.HIGHEST
    group = lax.axis_size("param")
    share = samples // group
    by_step = jnp.swapaxes(params, 0, 1)
    rim = from_behind(by_step[step_count - (REACH - 1) :], "tm", 1)
    near = prepare_near(diag_inverse, coupling, width)
    rim, near = lax.optimization_barrier((rim, near))
    code = predict(jnp.concatenate([rim, by_step], axis=0), kernel, lag_offsets)
    code = jnp.swapaxes(code, 0, 1).reshape(group, share, step_count, sensors + 1)
    code = lax.all_to_all(code, "param", 0, 0, tiled=True)
    far = prepare_far(diag_inverse, coupling, width)
    code, far = lax.optimization_barrier((code, far))
    factors = (*near, *far)
    grade = code[..., sensors:].astype(jnp.float32)
    summed = jnp.sum(code[..., :sensors].astype(jnp.float32) * scale_of(grade), axis=0)
    mine = lax.dynamic_slice_in_dim(observed, lax.axis_index("param") * share, share, 0)
    misfit = mine.astype(jnp.float32) - summed

    forcing = jnp.einsum("stn,mn->stm", misfit, diag_inverse, precision=exact)
    forcing = jnp.pad(forcing, ((0, 0), (0, 0), (0, width - sensors)))
    every = sent_to_all(forcing, "tm")
    every = jnp.moveaxis(every, 0, 1).reshape(share, -1, width)
    code = jnp.stack([run_chain(step_count, *factors, every[s]) for s in range(share)])
    code = sent_to_all(code, "param").reshape(samples, step_count, width)
    grade = code[..., sensors : sensors + 1].astype(jnp.float32)
    return code[..., :sensors].astype(jnp.float32) * scale_of(grade)


def solution(mesh):
    in_specs = (P(None, "tm", "param"), P(None, "param", None), P(), P(None, "tm", None), P(), P())
    out_specs = P(None, "tm", None)
    return jax.shard_map(
        per_device, mesh=mesh, in_specs=in_specs, out_specs=out_specs, check_vma=False
    )
```

time: 195 us -> 149 us (0.76)
  waiting for transfers between devices: 36.7 us -> 12.7 us
  matrix products: 21.4 us -> 2.79 us
  Pallas kernels: 52.6 us -> 64.8 us
  between operations: 9.97 us -> 0.09 us
  starting transfers between devices: 18.4 us -> 12.3 us
  local copies, waits for them, and re-layouts: 9.22 us -> 14.9 us
  other arithmetic: 5.79 us -> 2.74 us
  blocking collectives: 40.6 us -> 38 us
    all_to_all x2 -> x1, waiting for transfers between devices: 34.7 us -> 12.7 us  [per_device(): code = lax.all_to_all(code, 'param', 0, 0, tiled=True)]
    dot_general x2 -> x0, matrix products: 19.3 us -> none  [the longest x1 14.8 us: per_device(): jnp.einsum('mi,jin->jmn', diag_inverse, coupling, precision=exact)]
    pallas_call x1 -> x4, Pallas kernels: 52.6 us -> 64.8 us  [the longest x1 39.4 us: run_chain(): pl.pallas_call(functools.partial(chain_kernel, block, sensors), out_shape...]
    unnamed x12 -> x2, local copies, waits for them, and re-layouts: 1.82 us -> 9.08 us
    all_to_all x2 -> x1, starting transfers between devices: 17.1 us -> 11 us  [per_device(): code = lax.all_to_all(code, 'param', 0, 0, tiled=True)]
    unnamed x8 -> x0, other arithmetic: 5.28 us -> none
    slice x3 -> x1, local copies, waits for them, and re-layouts: 3.99 us -> 0.03 us  [per_device(): rim = from_behind(by_step[step_count - (REACH - 1):], 'tm', 1)]
    all_to_all x1 -> x2, blocking collectives: 40.6 us -> 38 us  [sent_to_all(): lax.all_to_all(jnp.broadcast_to(array[None], (length, *array.shape)), axi...]
  transfers between devices with their start and end apart: 3 -> 2, of which waited for: 2 -> 1; matrix products, arithmetic and copies ran while one was open for 10% -> 5% of each run, Pallas kernels for 0% -> 11%
where the time goes in v2:
time: 149 us; the launch traced here: 148 us
  Pallas kernels  64.8 us (43%)
  blocking collectives  38 us (26%)
  local copies, waits for them, and re-layouts  14.9 us (10%)
  waiting for transfers between devices  12.7 us (9%)
  starting transfers between devices  12.3 us (8%)
  matrix products  2.79 us (2%)
  other arithmetic  2.74 us (2%)
    pallas_call x1, Pallas kernels, run_chain(): pl.pallas_call(functools.partial(chain_kernel, block, sensors), out_shape...  39.4 us
    all_to_all x2, blocking collectives, sent_to_all(): lax.all_to_all(jnp.broadcast_to(array[None], (length, *array.shape)), axi...  38 us
    all_to_all x1, waiting for transfers between devices, per_device(): code = lax.all_to_all(code, 'param', 0, 0, tiled=True)  12.7 us
    all_to_all x1, starting transfers between devices, per_device(): code = lax.all_to_all(code, 'param', 0, 0, tiled=True)  11 us
    pallas_call x1, Pallas kernels, prepare_near(): pl.pallas_call(near_kernel, out_shape=(jax.ShapeDtypeStruct((2, sensors,...  9.7 us
    pallas_call x1, Pallas kernels, predict(): pl.pallas_call(predict_kernel, out_shape=jax.ShapeDtypeStruct((steps, sam...  9.53 us
    unnamed x2, local copies, waits for them, and re-layouts  9.08 us
    pallas_call x1, Pallas kernels, prepare_far(): pl.pallas_call(far_kernel, out_shape=(part, part), in_specs=[pl.BlockSpec...  6.13 us
  transfers between devices with their start and end apart: 2, of which 1 were waited for; matrix products, arithmetic and copies ran while one was open for 5% of the time, Pallas kernels for 11%

profile of v2, /device:TPU:39, one launch (start us, length us, event | category | flops | bytes accessed | tf_op | source)
XLA Modules:
  0.0 148.3 jit_solution(3530947970346493869)
XLA Ops:
  0.0 1.3 copy.29
  1.4 1.3 collective-permute-start
  2.7 7.8 %copy.21.kernel_ref = bf16[8,512,600]{2,1,0:T(8,128)(2,1)} copy(bf16[8,512,600]{1,2,0:T(8,128)(2,1)} %param.7) | data formatting | bytes 9830400 | tf_op args[1]
  10.4 9.7 %near_factors.1 = (f32[2,600,640]{2,1,0:T(8,128)}, bf16[256,640]{1,0:T(8,128)(2,1)}, bf16[256,640]{1,0:T(8,128)(2,1)}) custom-call(f32[600,600]{1,0:T(8,128)} %diag_ref.3, f32[3,600,600]{2,1,0:T(8,128)} %coupling_ref.3), custom_call_target="tpu_custom_call" | custom-call | flops 5184000000 | bytes 5760000 | tf_op jit(solution)/shard_map/near_factors/pallas_call | solution.py:204
  20.1 0.0 collective-permute-done
  20.1 1.0 pad_maximum_fusion.source_ref
  21.1 9.5 %predict.1 = s16[16,32,601]{2,1,0:T(8,128)(2,1)} custom-call(s32[8]{0:T(128)} %offsets_ref.1, bf16[27,32,512]{2,1,0:T(8,128)(2,1)} %pad_maximum_fusion.source_ref, bf16[8,512,600]{2,1,0:T(8,128)(2,1)} %copy.21.kernel_ref), custom_call_target="tpu_custom_call" | custom-call | flops 2516582400 | bytes 4915200 | tf_op jit(solution)/shard_map/predict/pallas_call | solution.py:276
  30.6 2.1 %copy.22 = s16[32,1,16,601]{3,2,1,0:T(8,128)(2,1)} copy(s16[32,1,16,601]{3,0,2,1:T(8,128)(2,1)} %bitcast.30) | data formatting | bytes 1230848 | tf_op jit(solution)/shard_map/reshape | solution.py:308
  32.8 11.0 %all-to-all-start = ((s16[32,1,16,601]{3,2,1,0:T(8,128)(2,1)}), s16[32,1,16,601]{3,2,1,0:T(8,128)(2,1)S(1)}, u32[]{:S(2)}, u32[]{:S(2)}) async-start(s16[32,1,16,601]{3,2,1,0:T(8,128)(2,1)} %copy.22), calls=%async_computation | async-start | bytes 1310720 | tf_op jit(solution)/shard_map/all_to_all | solution.py:309
  43.8 6.1 %far_factors.1 = (bf16[640,640]{1,0:T(8,128)(2,1)}, bf16[640,640]{1,0:T(8,128)(2,1)}) custom-call(f32[600,600]{1,0:T(8,128)} %diag_ref.3, f32[3,600,600]{2,1,0:T(8,128)} %coupling_ref.3), custom_call_target="tpu_custom_call" | custom-call | flops 2592000000 | bytes 4320000 | tf_op jit(solution)/shard_map/far_factors/pallas_call | solution.py:228
  50.0 12.7 %all-to-all-done = s16[32,1,16,601]{3,2,1,0:T(8,128)(2,1)S(1)} async-done(((s16[32,1,16,601]{3,2,1,0:T(8,128)(2,1)}), s16[32,1,16,601]{3,2,1,0:T(8,128)(2,1)S(1)}, u32[]{:S(2)}, u32[]{:S(2)}) %all-to-all-start) | async-done | bytes 615456 | tf_op jit(solution)/shard_map/all_to_all | solution.py:309
  62.7 2.4 %copy.23 = s16[32,1,16,601]{0,2,3,1:T(8,128)(2,1)S(1)} copy(s16[32,1,16,601]{3,2,1,0:T(8,128)(2,1)S(1)} %all-to-all-done) | data formatting | bytes 1230848 | tf_op jit(solution)/shard_map/optimization_barrier | solution.py:311
  65.1 0.1 copy.24
  65.2 0.3 multiply_reduce_fusion
  65.5 2.8 %convolution_bitcast_fusion = f32[1,16,600]{2,1,0:T(8,128)S(1)} fusion(f32[600,600]{1,0:T(8,128)} %diag_ref.3, f32[16,600]{1,0:T(8,128)S(1)} %multiply_reduce_fusion, bf16[32,16,600]{2,1,0:T(8,128)(2,1)} %param.9, s32[]{:T(128)S(6)} %select_n.3), kind=kOutput, calls=%fused_computation.2 | convolution fusion | flops 69139200 | bytes 1633284 | tf_op jit(solution)/shard_map/stn,mn->stm/dot_general | solution.py:318
  68.3 0.2 broadcast_in_dim.14
  68.5 15.5 %all_to_all.15 = f32[8,1,16,640]{3,1,2,0:T(1,128)} all-to-all(f32[8,1,16,640]{3,1,2,0:T(1,128)S(1)} %broadcast_in_dim.14), channel_id=1, replica_groups=mesh['param'=32,'tm'=8] {'tm'}, dimensions={0} | all-to-all | bytes 655360 | tf_op jit(solution)/shard_map/all_to_all | solution.py:25
  83.9 39.4 %chain.1 = (s16[16,640]{1,0:T(8,128)(2,1)}, f32[16,1,640]{2,1,0:T(1,128)}) custom-call(f32[2,600,640]{2,1,0:T(8,128)} %get-tuple-element.21.near_ref, bf16[256,640]{1,0:T(8,128)(2,1)} %get-tuple-element.22.two_hi, bf16[256,640]{1,0:T(8,128)(2,1)} %get-tuple-element.23.two_lo, bf16[640,640]{1,0:T(8,128)(2,1)} %get-tuple-element.27.three_hi, ...), custom_call_target="tpu_custom_call" | custom-call | tf_op jit(solution)/shard_map/chain/pallas_call | solution.py:133
  123.3 0.8 broadcast_in_dim.15
  124.1 22.5 %all_to_all.16 = s16[32,1,16,640]{3,2,1,0:T(8,128)(2,1)S(1)} all-to-all(s16[32,1,16,640]{3,2,1,0:T(8,128)(2,1)S(1)} %broadcast_in_dim.15), channel_id=1, replica_groups=mesh['param'=32,'tm'=8] {'param'}, dimensions={0} | all-to-all | bytes 1310720 | tf_op jit(solution)/shard_map/all_to_all | solution.py:25
  146.6 0.1 exponential_multiply_fusion
  146.8 0.2 copy.27
  147.0 1.3 convert_multiply_fusion
  (3 shorter events, 0.1 us)
Async XLA Ops:
  1.4 18.8 %collective-permute-start = (bf16[11,32,512]{2,1,0:T(8,128)(2,1)S(1)}, bf16[11,32,512]{2,1,0:T(8,128)(2,1)S(1)}, u32[]{:S(2)}, u32[]{:S(2)}) collective-permute-start(bf16[11,32,512]{2,1,0:T(8,128)(2,1)S(1)} %slice.20), channel_id=1, source_target_pairs={{0,1},{1,2},{2,3},{3,4},{4,5},{5,6},{6,7},{8,9},{9,10},{10,11},{11... | collective-permute-start | bytes 1081352 | tf_op jit(solution)/shard_map/ppermute | solution.py:20
  32.8 29.9 %all-to-all-start = ((s16[32,1,16,601]{3,2,1,0:T(8,128)(2,1)}), s16[32,1,16,601]{3,2,1,0:T(8,128)(2,1)S(1)}, u32[]{:S(2)}, u32[]{:S(2)}) async-start(s16[32,1,16,601]{3,2,1,0:T(8,128)(2,1)} %copy.22), calls=%async_computation | async-start | bytes 1310720 | tf_op jit(solution)/shard_map/all_to_all | solution.py:309

commit v3 on v2

--- a/solution.py
+++ b/solution.py
@@ -108,7 +108,8 @@
                 solved = wide(line) + base
                 new_ref[:, lanes(piece)] = solved
                 solved_ref[lax.rem(t, block), :, lanes(piece)] = solved[0:1]
-            behind = {c: prev_ref[:, lanes(c)] for c in rest}
+            gate = jnp.minimum(jnp.abs(sums[-1]), 0.0)
+            behind = {c: prev_ref[:, lanes(c)] + gate for c in rest}
             for start in range(0, sensors, 8):
                 total = None
                 for c in rest:
@@ -119,7 +120,12 @@
         return unused
 
     turns = (lax.axis_index("tm") + 1) * (block // 2)
-    lax.fori_loop(0, turns, pair, 0)
+    def several(group, unused):
+        for member in range(4):
+            unused = pair(4 * group + member, unused)
+        return unused
+
+    lax.fori_loop(0, turns // 4, several, 0)
     own = jnp.concatenate([solved_ref[row] for row in range(block)], axis=0)
     grade = grade_of(own)
     place = lax.broadcasted_iota(jnp.int32, own.shape, 1)
@@ -244,11 +250,14 @@
 
 def predict_kernel(offsets_ref, source_ref, kernel_ref, code_ref, total_ref):
     steps, samples, cols = code_ref.shape[0], source_ref.shape[1], source_ref.shape[2]
-    sensors = kernel_ref.shape[2]
+    sensors = kernel_ref.shape[1]
     lag = pl.program_id(0)
     window = source_ref[pl.ds(REACH - 1 - offsets_ref[lag], steps)]
-    product = jnp.dot(
-        window.reshape(steps * samples, cols), kernel_ref[0], preferred_element_type=jnp.float32
+    product = lax.dot_general(
+        window.reshape(steps * samples, cols),
+        kernel_ref[0],
+        (((1,), (1,)), ((), ())),
+        preferred_element_type=jnp.float32,
     )
 
     @pl.when(lag == 0)
@@ -270,7 +279,7 @@
 
 
 def predict(source, kernel, lag_offsets):
-    lag_count, cols, sensors = kernel.shape
+    lag_count, sensors, cols = kernel.shape
     span, samples, unused_cols = source.shape
     steps = span - (REACH - 1)
     return pl.pallas_call(
@@ -279,7 +288,7 @@
         in_specs=[
             pl.BlockSpec(memory_space=pltpu.SMEM),
             pl.BlockSpec((span, samples, cols), lambda lag: (0, 0, 0)),
-            pl.BlockSpec((1, cols, sensors), lambda lag: (lag, 0, 0)),
+            pl.BlockSpec((1, sensors, cols), lambda lag: (lag, 0, 0)),
         ],
         out_specs=pl.BlockSpec((steps, samples, sensors + 1), lambda lag: (0, 0, 0)),
         grid=(lag_count,),
@@ -293,31 +302,60 @@
     )(lag_offsets, source, kernel)
 
 
+def forcing_kernel(code_ref, observed_ref, diag_ref, forcing_ref):
+    sensors = diag_ref.shape[0]
+    total = None
+    for part in range(code_ref.shape[0]):
+        code = code_ref[part].astype(jnp.int32).astype(jnp.float32)
+        term = code * scale_of(code[:, sensors : sensors + 1])
+        total = term if total is None else total + term
+    misfit = observed_ref[...] - total[:, :sensors]
+    rows = lax.dot_general(
+        misfit,
+        diag_ref[...],
+        (((1,), (1,)), ((), ())),
+        precision=lax.Precision.HIGHEST,
+        preferred_element_type=jnp.float32,
+    )
+    for copy in range(forcing_ref.shape[0]):
+        forcing_ref[copy] = jnp.zeros(forcing_ref.shape[1:], jnp.float32)
+        forcing_ref[copy, :, :sensors] = rows
+
+
+def force(code, observed, diag_inverse, copies, width):
+    steps = code.shape[1]
+    return pl.pallas_call(
+        forcing_kernel,
+        out_shape=jax.ShapeDtypeStruct((copies, steps, width), jnp.float32),
+        in_specs=[pl.BlockSpec(memory_space=pltpu.VMEM)] * 3,
+        out_specs=pl.BlockSpec(memory_space=pltpu.VMEM),
+        name="forcing",
+    )(code, observed, diag_inverse)
+
+
 def per_device(params, kernel, lag_offsets, observed, diag_inverse, coupling):
     samples, step_count, col_count = params.shape
     lag_count, unused_cols, sensors = kernel.shape
     width = -(-sensors // LANES) * LANES
-    exact = lax.Precision.HIGHEST
     group = lax.axis_size("param")
     share = samples // group
     by_step = jnp.swapaxes(params, 0, 1)
     rim = from_behind(by_step[step_count - (REACH - 1) :], "tm", 1)
     near = prepare_near(diag_inverse, coupling, width)
     rim, near = lax.optimization_barrier((rim, near))
-    code = predict(jnp.concatenate([rim, by_step], axis=0), kernel, lag_offsets)
+    code = predict(
+        jnp.concatenate([rim, by_step], axis=0), jnp.swapaxes(kernel, 1, 2), lag_offsets
+    )
     code = jnp.swapaxes(code, 0, 1).reshape(group, share, step_count, sensors + 1)
     code = lax.all_to_all(code, "param", 0, 0, tiled=True)
     far = prepare_far(diag_inverse, coupling, width)
     code, far = lax.optimization_barrier((code, far))
     factors = (*near, *far)
-    grade = code[..., sensors:].astype(jnp.float32)
-    summed = jnp.sum(code[..., :sensors].astype(jnp.float32) * scale_of(grade), axis=0)
     mine = lax.dynamic_slice_in_dim(observed, lax.axis_index("param") * share, share, 0)
-    misfit = mine.astype(jnp.float32) - summed
-
-    forcing = jnp.einsum("stn,mn->stm", misfit, diag_inverse, precision=exact)
-    forcing = jnp.pad(forcing, ((0, 0), (0, 0), (0, width - sensors)))
-    every = sent_to_all(forcing, "tm")
+    mine = mine.astype(jnp.float32)
+    blocks = lax.axis_size("tm")
+    every = [force(code[:, s], mine[s], diag_inverse, blocks, width) for s in range(share)]
+    every = lax.all_to_all(jnp.stack(every, axis=1), "tm", 0, 0, tiled=True)
     every = jnp.moveaxis(every, 0, 1).reshape(share, -1, width)
     code = jnp.stack([run_chain(step_count, *factors, every[s]) for s in range(share)])
     code = sent_to_all(code, "param").reshape(samples, step_count, width)

time: 149 us -> 137 us (0.919)
  local copies, waits for them, and re-layouts: 14.9 us -> 6.36 us
  matrix products: 2.79 us -> 0 us
    all_to_all x2 -> x1, blocking collectives: 38 us -> 22.4 us  [sent_to_all(): lax.all_to_all(jnp.broadcast_to(array[None], (length, *array.shape)), axi...]
    all_to_all x0 -> x1, blocking collectives: none -> 14.6 us  [per_device(): every = lax.all_to_all(jnp.stack(every, axis=1), 'tm', 0, 0, tiled=True)]
    unnamed x2 -> x3, local copies, waits for them, and re-layouts: 9.08 us -> 2.16 us
    pallas_call x1, Pallas kernels: 39.4 us -> 34.8 us  [run_chain(): pl.pallas_call(functools.partial(chain_kernel, block, sensors), out_shape...]
    pallas_call x0 -> x1, Pallas kernels: none -> 3.87 us  [force(): pl.pallas_call(forcing_kernel, out_shape=jax.ShapeDtypeStruct((copies, st...]
    dot_general x1 -> x0, matrix products: 2.79 us -> none  [per_device(): forcing = jnp.einsum('stn,mn->stm', misfit, diag_inverse, precision=exact)]
    optimization_barrier x1 -> x0, local copies, waits for them, and re-layouts: 2.37 us -> none  [per_device(): code, far = lax.optimization_barrier((code, far))]
  transfers between devices with their start and end apart: 2 -> 2, of which waited for: 1 -> 2; matrix products, arithmetic and copies ran while one was open for 5% -> 1% of each run, Pallas kernels for 11% -> 12%
where the time goes in v3:
time: 137 us; the launch traced here: 136 us
  Pallas kernels  64 us (47%)
  blocking collectives  37 us (27%)
  starting transfers between devices  13.2 us (10%)
  waiting for transfers between devices  11.6 us (8%)
  local copies, waits for them, and re-layouts  6.36 us (5%)
  other arithmetic  3.8 us (3%)
    pallas_call x1, Pallas kernels, run_chain(): pl.pallas_call(functools.partial(chain_kernel, block, sensors), out_shape...  34.8 us
    all_to_all x1, blocking collectives, sent_to_all(): lax.all_to_all(jnp.broadcast_to(array[None], (length, *array.shape)), axi...  22.4 us
    all_to_all x1, blocking collectives, per_device(): every = lax.all_to_all(jnp.stack(every, axis=1), 'tm', 0, 0, tiled=True)  14.6 us
    all_to_all x1, starting transfers between devices, per_device(): code = lax.all_to_all(code, 'param', 0, 0, tiled=True)  11.9 us
    all_to_all x1, waiting for transfers between devices, per_device(): code = lax.all_to_all(code, 'param', 0, 0, tiled=True)  11.4 us
    pallas_call x1, Pallas kernels, prepare_near(): pl.pallas_call(near_kernel, out_shape=(jax.ShapeDtypeStruct((2, sensors,...  9.7 us
    pallas_call x1, Pallas kernels, predict(): pl.pallas_call(predict_kernel, out_shape=jax.ShapeDtypeStruct((steps, sam...  9.56 us
    pallas_call x1, Pallas kernels, prepare_far(): pl.pallas_call(far_kernel, out_shape=(part, part), in_specs=[pl.BlockSpec...  6.11 us
  transfers between devices with their start and end apart: 2, of which 2 were waited for; matrix products, arithmetic and copies ran while one was open for 1% of the time, Pallas kernels for 12%

profile of v3, /device:TPU:39, one launch (start us, length us, event | category | flops | bytes accessed | tf_op | source)
XLA Modules:
  0.0 136.0 jit_solution(6686747801489417281)
XLA Ops:
  0.0 1.3 copy.25
  1.4 1.3 collective-permute-start
  2.7 9.7 %near_factors.1 = (f32[2,600,640]{2,1,0:T(8,128)}, bf16[256,640]{1,0:T(8,128)(2,1)}, bf16[256,640]{1,0:T(8,128)(2,1)}) custom-call(f32[600,600]{1,0:T(8,128)} %diag_ref.5, f32[3,600,600]{2,1,0:T(8,128)} %coupling_ref.3), custom_call_target="tpu_custom_call" | custom-call | flops 5184000000 | bytes 5760000 | tf_op jit(solution)/shard_map/near_factors/pallas_call | solution.py:210
  12.4 0.2 collective-permute-done
  12.6 1.0 pad_maximum_fusion.source_ref
  13.5 9.6 %predict.1 = s16[16,32,601]{2,1,0:T(8,128)(2,1)} custom-call(s32[8]{0:T(128)} %offsets_ref.1, bf16[27,32,512]{2,1,0:T(8,128)(2,1)} %pad_maximum_fusion.source_ref, bf16[8,600,512]{2,1,0:T(8,128)(2,1)} %bitcast.27), custom_call_target="tpu_custom_call" | custom-call | flops 2516582400 | bytes 4915200 | tf_op jit(solution)/shard_map/predict/pallas_call | solution.py:285
  23.1 2.1 %copy.19 = s16[32,1,16,601]{3,2,1,0:T(8,128)(2,1)} copy(s16[32,1,16,601]{3,0,2,1:T(8,128)(2,1)} %bitcast.25) | data formatting | bytes 1230848 | tf_op jit(solution)/shard_map/reshape | solution.py:349
  25.2 11.9 %all-to-all-start = ((s16[32,1,16,601]{3,2,1,0:T(8,128)(2,1)}), s16[32,1,16,601]{3,2,1,0:T(8,128)(2,1)S(1)}, u32[]{:S(2)}, u32[]{:S(2)}) async-start(s16[32,1,16,601]{3,2,1,0:T(8,128)(2,1)} %copy.19), calls=%async_computation | async-start | bytes 1310720 | tf_op jit(solution)/shard_map/all_to_all | solution.py:350
  37.1 1.4 bitcast_convert_fusion.observed_ref
  38.5 6.1 %far_factors.1 = (bf16[640,640]{1,0:T(8,128)(2,1)}, bf16[640,640]{1,0:T(8,128)(2,1)}) custom-call(f32[600,600]{1,0:T(8,128)} %diag_ref.5, f32[3,600,600]{2,1,0:T(8,128)} %coupling_ref.3), custom_call_target="tpu_custom_call" | custom-call | flops 2592000000 | bytes 4320000 | tf_op jit(solution)/shard_map/far_factors/pallas_call | solution.py:234
  44.6 11.4 %all-to-all-done = s16[32,1,16,601]{3,2,1,0:T(8,128)(2,1)S(1)} async-done(((s16[32,1,16,601]{3,2,1,0:T(8,128)(2,1)}), s16[32,1,16,601]{3,2,1,0:T(8,128)(2,1)S(1)}, u32[]{:S(2)}, u32[]{:S(2)}) %all-to-all-start) | async-done | bytes 615456 | tf_op jit(solution)/shard_map/all_to_all | solution.py:350
  56.0 0.0 copy-start
  56.0 0.8 copy-done
  56.8 3.9 %forcing.1 = f32[8,16,640]{2,1,0:T(8,128)} custom-call(s16[32,16,601]{2,1,0:T(8,128)(2,1)} %bitcast.23, f32[16,600]{1,0:T(8,128)} %bitcast_convert_fusion.observed_ref, f32[600,600]{1,0:T(8,128)} %diag_ref.5), custom_call_target="tpu_custom_call" | custom-call | tf_op jit(solution)/shard_map/forcing/pallas_call | solution.py:327
  60.7 14.6 %all_to_all.15 = f32[8,1,16,640]{3,2,1,0:T(8,128)S(1)} all-to-all(f32[8,1,16,640]{3,2,1,0:T(8,128)} %bitcast.24), channel_id=1, replica_groups=mesh['param'=32,'tm'=8] {'tm'}, dimensions={0} | all-to-all | bytes 655360 | tf_op jit(solution)/shard_map/all_to_all | solution.py:358
  75.3 1.0 reshape_squeeze_reshape_transpose.3.forcing_ref
  76.3 34.8 %chain.1 = (s16[16,640]{1,0:T(8,128)(2,1)}, f32[16,1,640]{2,1,0:T(1,128)}) custom-call(f32[2,600,640]{2,1,0:T(8,128)} %get-tuple-element.21.near_ref, bf16[256,640]{1,0:T(8,128)(2,1)} %get-tuple-element.22.two_hi, bf16[256,640]{1,0:T(8,128)(2,1)} %get-tuple-element.23.two_lo, bf16[640,640]{1,0:T(8,128)(2,1)} %get-tuple-element.27.three_hi, ...), custom_call_target="tpu_custom_call" | custom-call | tf_op jit(solution)/shard_map/chain/pallas_call | solution.py:139
  111.1 0.8 broadcast_in_dim.2
  111.9 22.4 %all_to_all.16 = s16[32,1,16,640]{3,2,1,0:T(8,128)(2,1)S(1)} all-to-all(s16[32,1,16,640]{3,2,1,0:T(8,128)(2,1)S(1)} %broadcast_in_dim.2), channel_id=1, replica_groups=mesh['param'=32,'tm'=8] {'param'}, dimensions={0} | all-to-all | bytes 1310720 | tf_op jit(solution)/shard_map/all_to_all | solution.py:25
  134.3 0.1 exponential_multiply_fusion
  134.5 0.2 copy.23
  134.7 1.3 convert_multiply_fusion
  (1 shorter events, 0.0 us)
Async XLA Ops:
  1.4 11.2 %collective-permute-start = (bf16[11,32,512]{2,1,0:T(8,128)(2,1)S(1)}, bf16[11,32,512]{2,1,0:T(8,128)(2,1)S(1)}, u32[]{:S(2)}, u32[]{:S(2)}) collective-permute-start(bf16[11,32,512]{2,1,0:T(8,128)(2,1)S(1)} %slice.12), channel_id=1, source_target_pairs={{0,1},{1,2},{2,3},{3,4},{4,5},{5,6},{6,7},{8,9},{9,10},{10,11},{11... | collective-permute-start | bytes 1081352 | tf_op jit(solution)/shard_map/ppermute | solution.py:20
  25.2 30.8 %all-to-all-start = ((s16[32,1,16,601]{3,2,1,0:T(8,128)(2,1)}), s16[32,1,16,601]{3,2,1,0:T(8,128)(2,1)S(1)}, u32[]{:S(2)}, u32[]{:S(2)}) async-start(s16[32,1,16,601]{3,2,1,0:T(8,128)(2,1)} %copy.19), calls=%async_computation | async-start | bytes 1310720 | tf_op jit(solution)/shard_map/all_to_all | solution.py:350
  56.0 0.8 copy-start

commit v4 on v3

--- a/solution.py
+++ b/solution.py
@@ -20,13 +20,6 @@
     return lax.ppermute(block, axis, route)
 
 
-def sent_to_all(array, axis):
-    length = lax.axis_size(axis)
-    return lax.all_to_all(
-        jnp.broadcast_to(array[None], (length, *array.shape)), axis, 0, 0, tiled=True
-    )
-
-
 def grade_of(rows):
     largest = jnp.maximum(jnp.max(jnp.abs(rows), axis=-1, keepdims=True), TINY)
     return jnp.ceil(jnp.log2(largest) * OCTAVE)
@@ -38,6 +31,13 @@
 
 def scale_of(grade):
     return jnp.exp2(grade * (1.0 / OCTAVE)) * (1.0 / LEVELS)
+
+
+def coded_with_grade(rows, place):
+    grade = grade_of(rows)
+    lane = lax.broadcasted_iota(jnp.int32, rows.shape, 1)
+    code = jnp.where(lane == place, grade, coded(rows, grade))
+    return code.astype(jnp.int32).astype(jnp.int16)
 
 
 def row_chunks(rows):
@@ -127,19 +127,18 @@
 
     lax.fori_loop(0, turns // 4, several, 0)
     own = jnp.concatenate([solved_ref[row] for row in range(block)], axis=0)
-    grade = grade_of(own)
-    place = lax.broadcasted_iota(jnp.int32, own.shape, 1)
-    code = jnp.where(place == sensors, grade, coded(own, grade))
-    code_ref[...] = code.astype(jnp.int32).astype(jnp.int16)
-
-
-def run_chain(block, near, two_hi, two_lo, three_hi, three_lo, forcing):
+    code = coded_with_grade(own, sensors)
+    for copy in range(code_ref.shape[0]):
+        code_ref[copy] = code
+
+
+def run_chain(block, copies, near, two_hi, two_lo, three_hi, three_lo, forcing):
     unused_lags, sensors, width = near.shape
     steps = forcing.shape[0]
     code, unused_rows = pl.pallas_call(
         functools.partial(chain_kernel, block, sensors),
         out_shape=(
-            jax.ShapeDtypeStruct((block, width), jnp.int16),
+            jax.ShapeDtypeStruct((copies, block, width), jnp.int16),
             jax.ShapeDtypeStruct((block, 1, width), jnp.float32),
         ),
         in_specs=[pl.BlockSpec(memory_space=pltpu.VMEM)] * 6,
@@ -152,7 +151,7 @@
             pltpu.VMEM((2, 16, width), jnp.float32),
         ],
         name="chain",
-    )(near, two_hi, two_lo, three_hi, three_lo, forcing.reshape(steps, 1, width))
+    )(near, two_hi, two_lo, three_hi, three_lo, forcing)
     return code
 
 
@@ -249,50 +248,63 @@
 
 
 def predict_kernel(offsets_ref, source_ref, kernel_ref, code_ref, total_ref):
-    steps, samples, cols = code_ref.shape[0], source_ref.shape[1], source_ref.shape[2]
+    steps, samples, cols = code_ref.shape[1], source_ref.shape[1], source_ref.shape[2]
     sensors = kernel_ref.shape[1]
     lag = pl.program_id(0)
     window = source_ref[pl.ds(REACH - 1 - offsets_ref[lag], steps)]
-    product = lax.dot_general(
-        window.reshape(steps * samples, cols),
-        kernel_ref[0],
-        (((1,), (1,)), ((), ())),
-        preferred_element_type=jnp.float32,
-    )
+    window = window.reshape(steps * samples, cols)
 
     @pl.when(lag == 0)
     def first():
-        total_ref[...] = product
-
-    @pl.when(lag > 0)
-    def later():
-        total_ref[...] = total_ref[...] + product
+        total_ref[...] = jnp.zeros_like(total_ref)
+
+    for start in range(0, sensors, 2 * LANES):
+        end = min(start + 2 * LANES, sensors)
+        product = lax.dot_general(
+            window,
+            kernel_ref[0, start:end, :],
+            (((1,), (1,)), ((), ())),
+            preferred_element_type=jnp.float32,
+        )
+        for at in range(start, end, LANES):
+            size = min(LANES, end - at)
+            piece = product[:, at - start : at - start + size]
+            total_ref[at // LANES, :, :size] = total_ref[at // LANES, :, :size] + piece
 
     @pl.when(lag == pl.num_programs(0) - 1)
     def last():
-        for step in range(steps):
-            rows = total_ref[step * samples : (step + 1) * samples, :]
-            grade = grade_of(rows)
-            code = coded(rows, grade)
-            code_ref[step, :, :sensors] = code.astype(jnp.int32).astype(jnp.int16)
-            code_ref[step, :, sensors : sensors + 1] = grade.astype(jnp.int32).astype(jnp.int16)
+        def several(group, unused):
+            for member in range(4):
+                sample = 4 * group + member
+                rows = jnp.concatenate(
+                    [
+                        total_ref[c, pl.ds(sample, steps, stride=samples), :]
+                        for c in range(total_ref.shape[0])
+                    ],
+                    axis=1,
+                )
+                code_ref[sample] = coded_with_grade(rows, sensors)
+            return unused
+
+        lax.fori_loop(0, samples // 4, several, 0)
 
 
 def predict(source, kernel, lag_offsets):
     lag_count, sensors, cols = kernel.shape
     span, samples, unused_cols = source.shape
     steps = span - (REACH - 1)
+    width = -(-sensors // LANES) * LANES
     return pl.pallas_call(
         predict_kernel,
-        out_shape=jax.ShapeDtypeStruct((steps, samples, sensors + 1), jnp.int16),
+        out_shape=jax.ShapeDtypeStruct((samples, steps, width), jnp.int16),
         in_specs=[
             pl.BlockSpec(memory_space=pltpu.SMEM),
             pl.BlockSpec((span, samples, cols), lambda lag: (0, 0, 0)),
             pl.BlockSpec((1, sensors, cols), lambda lag: (lag, 0, 0)),
         ],
-        out_specs=pl.BlockSpec((steps, samples, sensors + 1), lambda lag: (0, 0, 0)),
+        out_specs=pl.BlockSpec((samples, steps, width), lambda lag: (0, 0, 0)),
         grid=(lag_count,),
-        scratch_shapes=[pltpu.VMEM((steps * samples, sensors), jnp.float32)],
+        scratch_shapes=[pltpu.VMEM((width // LANES, steps * samples, LANES), jnp.float32)],
         cost_estimate=pl.CostEstimate(
             flops=2 * steps * samples * lag_count * cols * sensors,
             bytes_accessed=2 * lag_count * cols * sensors,
@@ -302,14 +314,15 @@
     )(lag_offsets, source, kernel)
 
 
-def forcing_kernel(code_ref, observed_ref, diag_ref, forcing_ref):
+def forcing_kernel(place_ref, code_ref, observed_ref, diag_ref, forcing_ref):
     sensors = diag_ref.shape[0]
+    copies, steps, unused, width = forcing_ref.shape
     total = None
     for part in range(code_ref.shape[0]):
         code = code_ref[part].astype(jnp.int32).astype(jnp.float32)
         term = code * scale_of(code[:, sensors : sensors + 1])
         total = term if total is None else total + term
-    misfit = observed_ref[...] - total[:, :sensors]
+    misfit = observed_ref[0].astype(jnp.float32) - total[:, :sensors]
     rows = lax.dot_general(
         misfit,
         diag_ref[...],
@@ -317,20 +330,30 @@
         precision=lax.Precision.HIGHEST,
         preferred_element_type=jnp.float32,
     )
-    for copy in range(forcing_ref.shape[0]):
-        forcing_ref[copy] = jnp.zeros(forcing_ref.shape[1:], jnp.float32)
-        forcing_ref[copy, :, :sensors] = rows
-
-
-def force(code, observed, diag_inverse, copies, width):
-    steps = code.shape[1]
+    rows = jnp.concatenate([rows, jnp.zeros((steps, width - sensors), jnp.float32)], axis=1)
+    for copy in range(copies):
+        for step in range(steps):
+            forcing_ref[copy, step] = rows[step : step + 1]
+
+
+def force(code, observed, diag_inverse, place, copies, width):
+    parts, steps, wide = code.shape
+    sensors = diag_inverse.shape[0]
     return pl.pallas_call(
         forcing_kernel,
-        out_shape=jax.ShapeDtypeStruct((copies, steps, width), jnp.float32),
-        in_specs=[pl.BlockSpec(memory_space=pltpu.VMEM)] * 3,
-        out_specs=pl.BlockSpec(memory_space=pltpu.VMEM),
+        out_shape=jax.ShapeDtypeStruct((copies, steps, 1, width), jnp.float32),
+        grid_spec=pltpu.PrefetchScalarGridSpec(
+            num_scalar_prefetch=1,
+            grid=(1,),
+            in_specs=[
+                pl.BlockSpec((parts, steps, wide), lambda i, place: (0, 0, 0)),
+                pl.BlockSpec((1, steps, sensors), lambda i, place: (place[0], 0, 0)),
+                pl.BlockSpec((sensors, sensors), lambda i, place: (0, 0)),
+            ],
+            out_specs=pl.BlockSpec((copies, steps, 1, width), lambda i, place: (0, 0, 0, 0)),
+        ),
         name="forcing",
-    )(code, observed, diag_inverse)
+    )(place, code, observed, diag_inverse)
 
 
 def per_device(params, kernel, lag_offsets, observed, diag_inverse, coupling):
@@ -346,19 +369,21 @@
     code = predict(
         jnp.concatenate([rim, by_step], axis=0), jnp.swapaxes(kernel, 1, 2), lag_offsets
     )
-    code = jnp.swapaxes(code, 0, 1).reshape(group, share, step_count, sensors + 1)
+    code = code.reshape(group, share, step_count, width)
     code = lax.all_to_all(code, "param", 0, 0, tiled=True)
-    far = prepare_far(diag_inverse, coupling, width)
-    code, far = lax.optimization_barrier((code, far))
-    factors = (*near, *far)
-    mine = lax.dynamic_slice_in_dim(observed, lax.axis_index("param") * share, share, 0)
-    mine = mine.astype(jnp.float32)
     blocks = lax.axis_size("tm")
-    every = [force(code[:, s], mine[s], diag_inverse, blocks, width) for s in range(share)]
-    every = lax.all_to_all(jnp.stack(every, axis=1), "tm", 0, 0, tiled=True)
-    every = jnp.moveaxis(every, 0, 1).reshape(share, -1, width)
-    code = jnp.stack([run_chain(step_count, *factors, every[s]) for s in range(share)])
-    code = sent_to_all(code, "param").reshape(samples, step_count, width)
+    first = lax.axis_index("param").astype(jnp.int32) * share
+    forced = [
+        force(code[:, s], observed, diag_inverse, (first + s).reshape(1), blocks, width)
+        for s in range(share)
+    ]
+    forced, coupling = lax.optimization_barrier((jnp.stack(forced, axis=1), coupling))
+    every = lax.all_to_all(forced, "tm", 0, 0, tiled=True)
+    factors = (*near, *prepare_far(diag_inverse, coupling, width))
+    every = jnp.moveaxis(every, 0, 1).reshape(share, -1, 1, width)
+    code = [run_chain(step_count, group, *factors, every[s]) for s in range(share)]
+    code = lax.all_to_all(jnp.stack(code, axis=1), "param", 0, 0, tiled=True)
+    code = code.reshape(samples, step_count, width)
     grade = code[..., sensors : sensors + 1].astype(jnp.float32)
     return code[..., :sensors].astype(jnp.float32) * scale_of(grade)
 

time: 137 us -> 136 us (level)
  blocking collectives: 37 us -> 23.1 us
  starting transfers between devices: 13.2 us -> 21.6 us
  waiting for transfers between devices: 11.6 us -> 19.1 us
  local copies, waits for them, and re-layouts: 6.36 us -> 3.16 us
  Pallas kernels: 64 us -> 65.4 us
    all_to_all x2 -> x1, blocking collectives: 37 us -> 23.1 us  [per_device(): code = lax.all_to_all(jnp.stack(code, axis=1), 'param', 0, 0, tiled=True)]
    all_to_all x0 -> x1, starting transfers between devices: none -> 8.46 us  [per_device(): every = lax.all_to_all(forced, 'tm', 0, 0, tiled=True)]
    all_to_all x1, waiting for transfers between devices: 11.4 us -> 18.9 us  [per_device(): code = lax.all_to_all(code, 'param', 0, 0, tiled=True)]
    reshape x1 -> x0, local copies, waits for them, and re-layouts: 2.12 us -> none  [per_device(): jnp.swapaxes(code, 0, 1).reshape(group, share, step_count, sensors + 1)]
    unnamed x3 -> x5, local copies, waits for them, and re-layouts: 2.16 us -> 2.9 us
  transfers between devices with their start and end apart: 2 -> 3, of which waited for: 2 -> 2; matrix products, arithmetic and copies ran while one was open for 1% -> 0% of each run, Pallas kernels for 12% -> 12%
where the time goes in v4:
time: 136 us; the launch traced here: 135 us
  Pallas kernels  65.4 us (48%)
  blocking collectives  23.1 us (17%)
  starting transfers between devices  21.6 us (16%)
  waiting for transfers between devices  19.1 us (14%)
  local copies, waits for them, and re-layouts  3.16 us (2%)
  other arithmetic  2.45 us (2%)
    pallas_call x1, Pallas kernels, run_chain(): pl.pallas_call(functools.partial(chain_kernel, block, sensors), out_shape...  35.1 us
    all_to_all x1, blocking collectives, per_device(): code = lax.all_to_all(jnp.stack(code, axis=1), 'param', 0, 0, tiled=True)  23.1 us
    all_to_all x1, waiting for transfers between devices, per_device(): code = lax.all_to_all(code, 'param', 0, 0, tiled=True)  18.9 us
    all_to_all x1, starting transfers between devices, per_device(): code = lax.all_to_all(code, 'param', 0, 0, tiled=True)  11.9 us
    pallas_call x1, Pallas kernels, predict(): pl.pallas_call(predict_kernel, out_shape=jax.ShapeDtypeStruct((samples, s...  10.7 us
    pallas_call x1, Pallas kernels, prepare_near(): pl.pallas_call(near_kernel, out_shape=(jax.ShapeDtypeStruct((2, sensors,...  9.68 us
    all_to_all x1, starting transfers between devices, per_device(): every = lax.all_to_all(forced, 'tm', 0, 0, tiled=True)  8.46 us
    pallas_call x1, Pallas kernels, prepare_far(): pl.pallas_call(far_kernel, out_shape=(part, part), in_specs=[pl.BlockSpec...  6.11 us
  transfers between devices with their start and end apart: 3, of which 2 were waited for; matrix products, arithmetic and copies ran while one was open for 0% of the time, Pallas kernels for 12%

profile of v4, /device:TPU:39, one launch (start us, length us, event | category | flops | bytes accessed | tf_op | source)
XLA Modules:
  0.0 134.9 jit_solution(14946297037407588407)
XLA Ops:
  0.0 1.3 copy.23
  1.4 1.3 collective-permute-start
  2.7 9.7 %near_factors.1 = (f32[2,600,640]{2,1,0:T(8,128)}, bf16[256,640]{1,0:T(8,128)(2,1)}, bf16[256,640]{1,0:T(8,128)(2,1)}) custom-call(f32[600,600]{1,0:T(8,128)} %diag_ref.5, f32[3,600,600]{2,1,0:T(8,128)} %coupling_ref.2), custom_call_target="tpu_custom_call" | custom-call | flops 5184000000 | bytes 5760000 | tf_op jit(solution)/shard_map/near_factors/pallas_call | solution.py:209
  12.4 0.2 collective-permute-done
  12.6 1.0 pad_maximum_fusion.source_ref
  13.5 10.7 %predict.1 = s16[32,16,640]{2,1,0:T(8,128)(2,1)} custom-call(s32[8]{0:T(128)} %offsets_ref.1, bf16[27,32,512]{2,1,0:T(8,128)(2,1)} %pad_maximum_fusion.source_ref, bf16[8,600,512]{2,1,0:T(8,128)(2,1)} %bitcast.27), custom_call_target="tpu_custom_call" | custom-call | flops 2516582400 | bytes 4915200 | tf_op jit(solution)/shard_map/predict/pallas_call | solution.py:297
  24.2 11.9 %all-to-all-start = ((s16[32,1,16,640]{3,2,1,0:T(8,128)(2,1)}), s16[32,1,16,640]{3,2,1,0:T(8,128)(2,1)S(1)}, u32[]{:S(2)}, u32[]{:S(2)}) async-start(s16[32,1,16,640]{3,2,1,0:T(8,128)(2,1)} %bitcast.24), calls=%async_computation | async-start | bytes 1310720 | tf_op jit(solution)/shard_map/all_to_all | solution.py:373
  36.1 18.9 %all-to-all-done = s16[32,1,16,640]{3,2,1,0:T(8,128)(2,1)S(1)} async-done(((s16[32,1,16,640]{3,2,1,0:T(8,128)(2,1)}), s16[32,1,16,640]{3,2,1,0:T(8,128)(2,1)S(1)}, u32[]{:S(2)}, u32[]{:S(2)}) %all-to-all-start) | async-done | bytes 655392 | tf_op jit(solution)/shard_map/all_to_all | solution.py:373
  55.0 0.0 copy-start
  55.0 0.8 copy-done
  55.8 3.9 %forcing.1 = f32[8,16,1,640]{3,2,1,0:T(1,128)} custom-call(s32[1]{0:T(128)} %bitcast.1.place_ref, s16[32,16,640]{2,1,0:T(8,128)(2,1)} %bitcast.21, bf16[32,16,600]{2,1,0:T(8,128)(2,1)} %observed_ref.1, f32[600,600]{1,0:T(8,128)} %diag_ref.5), custom_call_target="tpu_custom_call" | custom-call | tf_op jit(solution)/shard_map/forcing/pallas_call | solution.py:342
  59.7 8.5 %all-to-all-start.1 = ((f32[8,1,16,1,640]{4,3,2,1,0:T(1,128)}), f32[8,1,16,1,640]{4,3,2,1,0:T(1,128)S(1)}, u32[]{:S(2)}, u32[]{:S(2)}) async-start(f32[8,1,16,1,640]{4,3,2,1,0:T(1,128)} %bitcast.23), calls=%async_computation.1 | async-start | bytes 655360 | tf_op jit(solution)/shard_map/all_to_all | solution.py:381
  68.2 6.1 %far_factors.1 = (bf16[640,640]{1,0:T(8,128)(2,1)}, bf16[640,640]{1,0:T(8,128)(2,1)}) custom-call(f32[600,600]{1,0:T(8,128)} %diag_ref.5, f32[3,600,600]{2,1,0:T(8,128)} %coupling_ref.2), custom_call_target="tpu_custom_call" | custom-call | flops 2592000000 | bytes 4320000 | tf_op jit(solution)/shard_map/far_factors/pallas_call | solution.py:233
  74.3 0.0 all-to-all-done.1
  74.3 0.0 copy-start.1
  74.3 0.7 copy-done.1
  75.0 35.1 %chain.1 = (s16[32,16,640]{2,1,0:T(8,128)(2,1)}, f32[16,1,640]{2,1,0:T(1,128)}) custom-call(f32[2,600,640]{2,1,0:T(8,128)} %get-tuple-element.20.near_ref, bf16[256,640]{1,0:T(8,128)(2,1)} %get-tuple-element.21.two_hi, bf16[256,640]{1,0:T(8,128)(2,1)} %get-tuple-element.22.two_lo, bf16[640,640]{1,0:T(8,128)(2,1)} %get-tuple-element.25.three_hi, ...), custom_call_target="tpu_custom_call" | custom-call | tf_op jit(solution)/shard_map/chain/pallas_call | solution.py:138
  110.1 23.1 %all_to_all.15 = s16[32,1,16,640]{3,2,1,0:T(8,128)(2,1)S(1)} all-to-all(s16[32,1,16,640]{3,2,1,0:T(8,128)(2,1)} %bitcast.25), channel_id=1, replica_groups=mesh['param'=32,'tm'=8] {'param'}, dimensions={0} | all-to-all | bytes 1310720 | tf_op jit(solution)/shard_map/all_to_all | solution.py:385
  133.2 0.1 exponential_multiply_fusion
  133.3 0.2 copy.21
  133.6 1.3 convert_multiply_fusion
  (1 shorter events, 0.0 us)
Async XLA Ops:
  1.4 11.2 %collective-permute-start = (bf16[11,32,512]{2,1,0:T(8,128)(2,1)S(1)}, bf16[11,32,512]{2,1,0:T(8,128)(2,1)S(1)}, u32[]{:S(2)}, u32[]{:S(2)}) collective-permute-start(bf16[11,32,512]{2,1,0:T(8,128)(2,1)S(1)} %slice.12), channel_id=1, source_target_pairs={{0,1},{1,2},{2,3},{3,4},{4,5},{5,6},{6,7},{8,9},{9,10},{10,11},{11... | collective-permute-start | bytes 1081352 | tf_op jit(solution)/shard_map/ppermute | solution.py:20
  24.2 30.8 %all-to-all-start = ((s16[32,1,16,640]{3,2,1,0:T(8,128)(2,1)}), s16[32,1,16,640]{3,2,1,0:T(8,128)(2,1)S(1)}, u32[]{:S(2)}, u32[]{:S(2)}) async-start(s16[32,1,16,640]{3,2,1,0:T(8,128)(2,1)} %bitcast.24), calls=%async_computation | async-start | bytes 1310720 | tf_op jit(solution)/shard_map/all_to_all | solution.py:373
  55.0 0.8 copy-start
  59.7 14.6 %all-to-all-start.1 = ((f32[8,1,16,1,640]{4,3,2,1,0:T(1,128)}), f32[8,1,16,1,640]{4,3,2,1,0:T(1,128)S(1)}, u32[]{:S(2)}, u32[]{:S(2)}) async-start(f32[8,1,16,1,640]{4,3,2,1,0:T(1,128)} %bitcast.23), calls=%async_computation.1 | async-start | bytes 655360 | tf_op jit(solution)/shard_map/all_to_all | solution.py:381
  74.3 0.7 copy-start.1

commit v5 on v4

--- a/solution.py
+++ b/solution.py
@@ -247,46 +247,52 @@
     )(diag_inverse, coupling)
 
 
-def predict_kernel(offsets_ref, source_ref, kernel_ref, code_ref, total_ref):
-    steps, samples, cols = code_ref.shape[1], source_ref.shape[1], source_ref.shape[2]
-    sensors = kernel_ref.shape[1]
-    lag = pl.program_id(0)
-    window = source_ref[pl.ds(REACH - 1 - offsets_ref[lag], steps)]
-    window = window.reshape(steps * samples, cols)
-
-    @pl.when(lag == 0)
-    def first():
-        total_ref[...] = jnp.zeros_like(total_ref)
-
-    for start in range(0, sensors, 2 * LANES):
-        end = min(start + 2 * LANES, sensors)
-        product = lax.dot_general(
-            window,
-            kernel_ref[0, start:end, :],
-            (((1,), (1,)), ((), ())),
-            preferred_element_type=jnp.float32,
-        )
-        for at in range(start, end, LANES):
-            size = min(LANES, end - at)
-            piece = product[:, at - start : at - start + size]
-            total_ref[at // LANES, :, :size] = total_ref[at // LANES, :, :size] + piece
-
-    @pl.when(lag == pl.num_programs(0) - 1)
-    def last():
-        def several(group, unused):
-            for member in range(4):
-                sample = 4 * group + member
-                rows = jnp.concatenate(
-                    [
-                        total_ref[c, pl.ds(sample, steps, stride=samples), :]
-                        for c in range(total_ref.shape[0])
-                    ],
-                    axis=1,
-                )
-                code_ref[sample] = coded_with_grade(rows, sensors)
-            return unused
-
-        lax.fori_loop(0, samples // 4, several, 0)
+def predict_kernel(offsets_ref, source_ref, kernel_hbm, code_ref, kernel_ref, total_ref, arrived):
+    samples, cols = source_ref.shape[1:]
+    steps = code_ref.shape[1]
+    lag_count, sensors, unused = kernel_ref.shape
+
+    def fetch(lag):
+        return pltpu.make_async_copy(kernel_hbm.at[lag], kernel_ref.at[lag], arrived.at[lag])
+
+    for lag in range(lag_count):
+        fetch(lag).start()
+    total_ref[...] = jnp.zeros_like(total_ref)
+
+    def add(lag, unused):
+        fetch(lag).wait()
+        window = source_ref[pl.ds(REACH - 1 - offsets_ref[lag], steps)]
+        window = window.reshape(steps * samples, cols)
+        for start in range(0, sensors, 2 * LANES):
+            end = min(start + 2 * LANES, sensors)
+            product = lax.dot_general(
+                window,
+                kernel_ref[lag, start:end, :],
+                (((1,), (1,)), ((), ())),
+                preferred_element_type=jnp.float32,
+            )
+            for at in range(start, end, LANES):
+                size = min(LANES, end - at)
+                piece = product[:, at - start : at - start + size]
+                total_ref[at // LANES, :, :size] = total_ref[at // LANES, :, :size] + piece
+        return unused
+
+    lax.fori_loop(0, lag_count, add, 0)
+
+    def several(group, unused):
+        for member in range(4):
+            sample = 4 * group + member
+            rows = jnp.concatenate(
+                [
+                    total_ref[c, pl.ds(sample, steps, stride=samples), :]
+                    for c in range(total_ref.shape[0])
+                ],
+                axis=1,
+            )
+            code_ref[sample] = coded_with_grade(rows, sensors)
+        return unused
+
+    lax.fori_loop(0, samples // 4, several, 0)
 
 
 def predict(source, kernel, lag_offsets):
@@ -299,12 +305,15 @@
         out_shape=jax.ShapeDtypeStruct((samples, steps, width), jnp.int16),
         in_specs=[
             pl.BlockSpec(memory_space=pltpu.SMEM),
-            pl.BlockSpec((span, samples, cols), lambda lag: (0, 0, 0)),
-            pl.BlockSpec((1, sensors, cols), lambda lag: (lag, 0, 0)),
-        ],
-        out_specs=pl.BlockSpec((samples, steps, width), lambda lag: (0, 0, 0)),
-        grid=(lag_count,),
-        scratch_shapes=[pltpu.VMEM((width // LANES, steps * samples, LANES), jnp.float32)],
+            pl.BlockSpec(memory_space=pltpu.VMEM),
+            pl.BlockSpec(memory_space=pl.ANY),
+        ],
+        out_specs=pl.BlockSpec(memory_space=pltpu.VMEM),
+        scratch_shapes=[
+            pltpu.VMEM((lag_count, sensors, cols), jnp.bfloat16),
+            pltpu.VMEM((width // LANES, steps * samples, LANES), jnp.float32),
+            pltpu.SemaphoreType.DMA((lag_count,)),
+        ],
         cost_estimate=pl.CostEstimate(
             flops=2 * steps * samples * lag_count * cols * sensors,
             bytes_accessed=2 * lag_count * cols * sensors,
@@ -370,9 +379,10 @@
         jnp.concatenate([rim, by_step], axis=0), jnp.swapaxes(kernel, 1, 2), lag_offsets
     )
     code = code.reshape(group, share, step_count, width)
+    first = lax.axis_index("param").astype(jnp.int32) * share
+    code, first = lax.optimization_barrier((code, first))
     code = lax.all_to_all(code, "param", 0, 0, tiled=True)
     blocks = lax.axis_size("tm")
-    first = lax.axis_index("param").astype(jnp.int32) * share
     forced = [
         force(code[:, s], observed, diag_inverse, (first + s).reshape(1), blocks, width)
         for s in range(share)

time: 136 us -> 134 us (0.985)
  blocking collectives: 23.1 us -> 53.8 us
  waiting for transfers between devices: 19.1 us -> 0.19 us
  starting transfers between devices: 21.6 us -> 9.94 us
    all_to_all x0 -> x1, blocking collectives: none -> 30.9 us  [per_device(): code = lax.all_to_all(code, 'param', 0, 0, tiled=True)]
    all_to_all x1 -> x0, waiting for transfers between devices: 18.9 us -> none  [per_device(): code = lax.all_to_all(code, 'param', 0, 0, tiled=True)]
    all_to_all x1 -> x0, starting transfers between devices: 11.9 us -> none  [per_device(): code = lax.all_to_all(code, 'param', 0, 0, tiled=True)]
    unnamed x5 -> x3, local copies, waits for them, and re-layouts: 2.9 us -> 2.08 us
  transfers between devices with their start and end apart: 3 -> 2, of which waited for: 2 -> 1; matrix products, arithmetic and copies ran while one was open for 0% -> 0% of each run, Pallas kernels for 12% -> 12%
where the time goes in v5:
time: 134 us; the launch traced here: 133 us
  Pallas kernels  64.5 us (48%)
  blocking collectives  53.8 us (40%)
  starting transfers between devices  9.94 us (7%)
  other arithmetic  2.45 us (2%)
  local copies, waits for them, and re-layouts  2.34 us (2%)
    pallas_call x1, Pallas kernels, run_chain(): pl.pallas_call(functools.partial(chain_kernel, block, sensors), out_shape...  35.1 us
    all_to_all x1, blocking collectives, per_device(): code = lax.all_to_all(code, 'param', 0, 0, tiled=True)  30.9 us
    all_to_all x1, blocking collectives, per_device(): code = lax.all_to_all(jnp.stack(code, axis=1), 'param', 0, 0, tiled=True)  23 us
    pallas_call x1, Pallas kernels, predict(): pl.pallas_call(predict_kernel, out_shape=jax.ShapeDtypeStruct((samples, s...  9.73 us
    pallas_call x1, Pallas kernels, prepare_near(): pl.pallas_call(near_kernel, out_shape=(jax.ShapeDtypeStruct((2, sensors,...  9.7 us
    all_to_all x1, starting transfers between devices, per_device(): every = lax.all_to_all(forced, 'tm', 0, 0, tiled=True)  8.65 us
    pallas_call x1, Pallas kernels, prepare_far(): pl.pallas_call(far_kernel, out_shape=(part, part), in_specs=[pl.BlockSpec...  6.1 us
    pallas_call x1, Pallas kernels, force(): pl.pallas_call(forcing_kernel, out_shape=jax.ShapeDtypeStruct((copies, st...  3.87 us
  transfers between devices with their start and end apart: 2, of which 1 were waited for; matrix products, arithmetic and copies ran while one was open for 0% of the time, Pallas kernels for 12%

profile of v5, /device:TPU:39, one launch (start us, length us, event | category | flops | bytes accessed | tf_op | source)
XLA Modules:
  0.0 133.3 jit_solution(15412931430999072083)
XLA Ops:
  0.0 1.3 %copy.23 = bf16[32,16,512]{2,0,1:T(8,128)(2,1)S(1)} copy(bf16[32,16,512]{2,1,0:T(8,128)(2,1)} %param.6) | data formatting | bytes 1048576 | tf_op args[0]
  1.4 1.3 collective-permute-start
  2.7 9.7 %near_factors.1 = (f32[2,600,640]{2,1,0:T(8,128)}, bf16[256,640]{1,0:T(8,128)(2,1)}, bf16[256,640]{1,0:T(8,128)(2,1)}) custom-call(f32[600,600]{1,0:T(8,128)} %diag_ref.5, f32[3,600,600]{2,1,0:T(8,128)} %coupling_ref.2), custom_call_target="tpu_custom_call" | custom-call | flops 5184000000 | bytes 5760000 | tf_op jit(solution)/shard_map/near_factors/pallas_call | solution.py:209
  12.4 0.2 collective-permute-done
  12.6 1.0 pad_maximum_fusion.source_ref
  13.5 9.7 %predict.1 = s16[32,16,640]{2,1,0:T(8,128)(2,1)} custom-call(s32[8]{0:T(128)} %offsets_ref.1, bf16[27,32,512]{2,1,0:T(8,128)(2,1)} %pad_maximum_fusion.source_ref, bf16[8,600,512]{2,1,0:T(8,128)(2,1)} %bitcast.26), custom_call_target="tpu_custom_call" | custom-call | flops 2516582400 | bytes 4915200 | tf_op jit(solution)/shard_map/predict/pallas_call | solution.py:303
  23.3 30.9 %all_to_all.15 = s16[32,1,16,640]{3,2,1,0:T(8,128)(2,1)} all-to-all(s16[32,1,16,640]{3,2,1,0:T(8,128)(2,1)} %bitcast.24), channel_id=1, replica_groups=mesh['param'=32,'tm'=8] {'param'}, dimensions={0} | all-to-all | bytes 1310720 | tf_op jit(solution)/shard_map/all_to_all | solution.py:384
  54.2 3.9 %forcing.1 = f32[8,16,1,640]{3,2,1,0:T(1,128)} custom-call(s32[1]{0:T(128)} %bitcast.3.place_ref, s16[32,16,640]{2,1,0:T(8,128)(2,1)} %bitcast.20, bf16[32,16,600]{2,1,0:T(8,128)(2,1)} %observed_ref.1, f32[600,600]{1,0:T(8,128)} %diag_ref.5), custom_call_target="tpu_custom_call" | custom-call | tf_op jit(solution)/shard_map/forcing/pallas_call | solution.py:351
  58.0 8.7 %all-to-all-start.1 = ((f32[8,1,16,1,640]{4,3,2,1,0:T(1,128)}), f32[8,1,16,1,640]{4,3,2,1,0:T(1,128)S(1)}, u32[]{:S(2)}, u32[]{:S(2)}) async-start(f32[8,1,16,1,640]{4,3,2,1,0:T(1,128)} %bitcast.22), calls=%async_computation.1 | async-start | bytes 655360 | tf_op jit(solution)/shard_map/all_to_all | solution.py:391
  66.7 6.1 %far_factors.1 = (bf16[640,640]{1,0:T(8,128)(2,1)}, bf16[640,640]{1,0:T(8,128)(2,1)}) custom-call(f32[600,600]{1,0:T(8,128)} %diag_ref.5, f32[3,600,600]{2,1,0:T(8,128)} %coupling_ref.2), custom_call_target="tpu_custom_call" | custom-call | flops 2592000000 | bytes 4320000 | tf_op jit(solution)/shard_map/far_factors/pallas_call | solution.py:233
  72.8 0.0 all-to-all-done.1
  72.8 0.0 copy-start
  72.8 0.7 copy-done
  73.5 35.1 %chain.1 = (s16[32,16,640]{2,1,0:T(8,128)(2,1)}, f32[16,1,640]{2,1,0:T(1,128)}) custom-call(f32[2,600,640]{2,1,0:T(8,128)} %get-tuple-element.22.near_ref, bf16[256,640]{1,0:T(8,128)(2,1)} %get-tuple-element.23.two_hi, bf16[256,640]{1,0:T(8,128)(2,1)} %get-tuple-element.24.two_lo, bf16[640,640]{1,0:T(8,128)(2,1)} %get-tuple-element.29.three_hi, ...), custom_call_target="tpu_custom_call" | custom-call | tf_op jit(solution)/shard_map/chain/pallas_call | solution.py:138
  108.6 23.0 %all_to_all.16 = s16[32,1,16,640]{3,2,1,0:T(8,128)(2,1)S(1)} all-to-all(s16[32,1,16,640]{3,2,1,0:T(8,128)(2,1)} %bitcast.23), channel_id=1, replica_groups=mesh['param'=32,'tm'=8] {'param'}, dimensions={0} | all-to-all | bytes 1310720 | tf_op jit(solution)/shard_map/all_to_all | solution.py:395
  131.6 0.1 exponential_multiply_fusion
  131.7 0.2 copy.21
  131.9 1.3 convert_multiply_fusion
  (1 shorter events, 0.0 us)
Async XLA Ops:
  1.4 11.2 %collective-permute-start = (bf16[11,32,512]{2,1,0:T(8,128)(2,1)S(1)}, bf16[11,32,512]{2,1,0:T(8,128)(2,1)S(1)}, u32[]{:S(2)}, u32[]{:S(2)}) collective-permute-start(bf16[11,32,512]{2,1,0:T(8,128)(2,1)S(1)} %slice.12), channel_id=1, source_target_pairs={{0,1},{1,2},{2,3},{3,4},{4,5},{5,6},{6,7},{8,9},{9,10},{10,11},{11... | collective-permute-start | bytes 1081352 | tf_op jit(solution)/shard_map/ppermute | solution.py:20
  58.0 14.8 %all-to-all-start.1 = ((f32[8,1,16,1,640]{4,3,2,1,0:T(1,128)}), f32[8,1,16,1,640]{4,3,2,1,0:T(1,128)S(1)}, u32[]{:S(2)}, u32[]{:S(2)}) async-start(f32[8,1,16,1,640]{4,3,2,1,0:T(1,128)} %bitcast.22), calls=%async_computation.1 | async-start | bytes 655360 | tf_op jit(solution)/shard_map/all_to_all | solution.py:391
  72.8 0.7 copy-start

commit v6 on v5

--- a/solution.py
+++ b/solution.py
@@ -247,7 +247,9 @@
     )(diag_inverse, coupling)
 
 
-def predict_kernel(offsets_ref, source_ref, kernel_hbm, code_ref, kernel_ref, total_ref, arrived):
+def predict_kernel(
+    offsets_ref, source_ref, kernel_hbm, code_ref, own_ref, kernel_ref, total_ref, arrived
+):
     samples, cols = source_ref.shape[1:]
     steps = code_ref.shape[1]
     lag_count, sensors, unused = kernel_ref.shape
@@ -279,20 +281,25 @@
 
     lax.fori_loop(0, lag_count, add, 0)
 
+    core = lax.rem(lax.axis_index("param"), 2)
+
+    def rows_of(sample):
+        return jnp.concatenate(
+            [
+                total_ref[c, pl.ds(sample, steps, stride=samples), :]
+                for c in range(total_ref.shape[0])
+            ],
+            axis=1,
+        )
+
     def several(group, unused):
         for member in range(4):
-            sample = 4 * group + member
-            rows = jnp.concatenate(
-                [
-                    total_ref[c, pl.ds(sample, steps, stride=samples), :]
-                    for c in range(total_ref.shape[0])
-                ],
-                axis=1,
-            )
-            code_ref[sample] = coded_with_grade(rows, sensors)
-        return unused
-
-    lax.fori_loop(0, samples // 4, several, 0)
+            pair = 4 * group + member
+            code_ref[pair] = coded_with_grade(rows_of(2 * pair + 1 - core), sensors)
+            own_ref[pair] = rows_of(2 * pair + core)
+        return unused
+
+    lax.fori_loop(0, samples // 8, several, 0)
 
 
 def predict(source, kernel, lag_offsets):
@@ -302,13 +309,16 @@
     width = -(-sensors // LANES) * LANES
     return pl.pallas_call(
         predict_kernel,
-        out_shape=jax.ShapeDtypeStruct((samples, steps, width), jnp.int16),
+        out_shape=(
+            jax.ShapeDtypeStruct((samples // 2, steps, width), jnp.int16),
+            jax.ShapeDtypeStruct((samples // 2, steps, width), jnp.float32),
+        ),
         in_specs=[
             pl.BlockSpec(memory_space=pltpu.SMEM),
             pl.BlockSpec(memory_space=pltpu.VMEM),
             pl.BlockSpec(memory_space=pl.ANY),
         ],
-        out_specs=pl.BlockSpec(memory_space=pltpu.VMEM),
+        out_specs=[pl.BlockSpec(memory_space=pltpu.VMEM)] * 2,
         scratch_shapes=[
             pltpu.VMEM((lag_count, sensors, cols), jnp.bfloat16),
             pltpu.VMEM((width // LANES, steps * samples, LANES), jnp.float32),
@@ -321,6 +331,58 @@
         ),
         name="predict",
     )(lag_offsets, source, kernel)
+
+
+def decoded(code, sensors):
+    values = code.astype(jnp.int32).astype(jnp.float32)
+    return values * scale_of(values[:, sensors : sensors + 1])
+
+
+def merge_kernel(sensors, own_ref, code_ref, merged_ref):
+    lane = lax.broadcasted_iota(jnp.int32, own_ref.shape[1:], 1)
+
+    def several(group, unused):
+        for member in range(4):
+            pair = 4 * group + member
+            other = jnp.where(lane < sensors, decoded(code_ref[pair], sensors), 0.0)
+            merged_ref[pair] = coded_with_grade(own_ref[pair] + other, sensors)
+        return unused
+
+    lax.fori_loop(0, own_ref.shape[0] // 4, several, 0)
+
+
+def merge(own, code, sensors):
+    return pl.pallas_call(
+        functools.partial(merge_kernel, sensors),
+        out_shape=jax.ShapeDtypeStruct(code.shape, code.dtype),
+        in_specs=[pl.BlockSpec(memory_space=pltpu.VMEM)] * 2,
+        out_specs=pl.BlockSpec(memory_space=pltpu.VMEM),
+        name="merge",
+    )(own, code)
+
+
+def decode_kernel(own_ref, other_ref, out_ref):
+    sensors = out_ref.shape[3]
+    core = lax.rem(lax.axis_index("param"), 2)
+
+    def one(pair, unused):
+        out_ref[pair, core] = decoded(own_ref[pair], sensors)[:, :sensors]
+        out_ref[pair, 1 - core] = decoded(other_ref[pair], sensors)[:, :sensors]
+        return unused
+
+    lax.fori_loop(0, own_ref.shape[0], one, 0, unroll=4)
+
+
+def decode(own, other, sensors):
+    pairs, steps, unused = own.shape
+    out = pl.pallas_call(
+        decode_kernel,
+        out_shape=jax.ShapeDtypeStruct((pairs, 2, steps, sensors), jnp.float32),
+        in_specs=[pl.BlockSpec(memory_space=pltpu.VMEM)] * 2,
+        out_specs=pl.BlockSpec(memory_space=pltpu.VMEM),
+        name="decode",
+    )(own, other)
+    return out.reshape(2 * pairs, steps, sensors)
 
 
 def forcing_kernel(place_ref, code_ref, observed_ref, diag_ref, forcing_ref):
@@ -375,27 +437,24 @@
     rim = from_behind(by_step[step_count - (REACH - 1) :], "tm", 1)
     near = prepare_near(diag_inverse, coupling, width)
     rim, near = lax.optimization_barrier((rim, near))
-    code = predict(
+    assert share == 1
+    chips = [list(range(core, group, 2)) for core in range(2)]
+    partner = [(i, i ^ 1) for i in range(group)]
+    code, own = predict(
         jnp.concatenate([rim, by_step], axis=0), jnp.swapaxes(kernel, 1, 2), lag_offsets
     )
-    code = code.reshape(group, share, step_count, width)
-    first = lax.axis_index("param").astype(jnp.int32) * share
-    code, first = lax.optimization_barrier((code, first))
-    code = lax.all_to_all(code, "param", 0, 0, tiled=True)
+    code = merge(own, lax.ppermute(code, "param", partner), sensors)
+    place = lax.axis_index("param").astype(jnp.int32).reshape(1)
+    code, place = lax.optimization_barrier((code, place))
+    code = lax.all_to_all(code, "param", 0, 0, tiled=True, axis_index_groups=chips)
     blocks = lax.axis_size("tm")
-    forced = [
-        force(code[:, s], observed, diag_inverse, (first + s).reshape(1), blocks, width)
-        for s in range(share)
-    ]
-    forced, coupling = lax.optimization_barrier((jnp.stack(forced, axis=1), coupling))
+    forced = force(code, observed, diag_inverse, place, blocks, width)
+    forced, coupling = lax.optimization_barrier((forced, coupling))
     every = lax.all_to_all(forced, "tm", 0, 0, tiled=True)
     factors = (*near, *prepare_far(diag_inverse, coupling, width))
-    every = jnp.moveaxis(every, 0, 1).reshape(share, -1, 1, width)
-    code = [run_chain(step_count, group, *factors, every[s]) for s in range(share)]
-    code = lax.all_to_all(jnp.stack(code, axis=1), "param", 0, 0, tiled=True)
-    code = code.reshape(samples, step_count, width)
-    grade = code[..., sensors : sensors + 1].astype(jnp.float32)
-    return code[..., :sensors].astype(jnp.float32) * scale_of(grade)
+    code = run_chain(step_count, group // 2, *factors, every.reshape(-1, 1, width))
+    code = lax.all_to_all(code, "param", 0, 0, tiled=True, axis_index_groups=chips)
+    return decode(code, lax.ppermute(code, "param", partner), sensors)
 
 
 def solution(mesh):

time: 134 us -> 128 us (0.955)
  blocking collectives: 53.8 us -> 37.3 us
  Pallas kernels: 64.5 us -> 69.3 us
  starting transfers between devices: 9.94 us -> 13.2 us
  waiting for transfers between devices: 0.19 us -> 2.93 us
  other arithmetic: 2.45 us -> 0.99 us
    all_to_all x2, blocking collectives: 53.8 us -> 37.3 us  [per_device(): lax.all_to_all(code, 'param', 0, 0, tiled=True, axis_index_groups=chips)]
    pallas_call x1 -> x3, Pallas kernels: 9.73 us -> 14.8 us  [the longest x1 9.53 us: predict(): pl.pallas_call(predict_kernel, out_shape=(jax.ShapeDtypeStruct((samples /...]
    ppermute x0 -> x2, starting transfers between devices: none -> 4.99 us  [the longest x1 3.37 us: per_device(): return decode(code, lax.ppermute(code, 'param', partner), sensors)]
    ppermute x0 -> x2, waiting for transfers between devices: none -> 2.72 us  [the longest x1 1.47 us: per_device(): code = merge(own, lax.ppermute(code, 'param', partner), sensors)]
    all_to_all x1, starting transfers between devices: 8.65 us -> 6.94 us  [per_device(): every = lax.all_to_all(forced, 'tm', 0, 0, tiled=True)]
    mul x2 -> x0, other arithmetic: 1.46 us -> none  [the longest x1 1.31 us: per_device(): return code[..., :sensors].astype(jnp.float32) * scale_of(grade)]
    unnamed x3 -> x9, local copies, waits for them, and re-layouts: 2.08 us -> 3.53 us
  transfers between devices with their start and end apart: 2 -> 4, of which waited for: 1 -> 3; matrix products, arithmetic and copies ran while one was open for 0% -> 0% of each run, Pallas kernels for 12% -> 12%
where the time goes in v6:
time: 128 us; the launch traced here: 127 us
  Pallas kernels  69.3 us (54%)
  blocking collectives  37.3 us (29%)
  starting transfers between devices  13.2 us (10%)
  local copies, waits for them, and re-layouts  3.55 us (3%)
  waiting for transfers between devices  2.93 us (2%)
    all_to_all x2, blocking collectives, per_device(): lax.all_to_all(code, 'param', 0, 0, tiled=True, axis_index_groups=chips)  37.3 us
    pallas_call x1, Pallas kernels, run_chain(): pl.pallas_call(functools.partial(chain_kernel, block, sensors), out_shape...  34.9 us
    pallas_call x1, Pallas kernels, prepare_near(): pl.pallas_call(near_kernel, out_shape=(jax.ShapeDtypeStruct((2, sensors,...  9.69 us
    pallas_call x1, Pallas kernels, predict(): pl.pallas_call(predict_kernel, out_shape=(jax.ShapeDtypeStruct((samples /...  9.53 us
    all_to_all x1, starting transfers between devices, per_device(): every = lax.all_to_all(forced, 'tm', 0, 0, tiled=True)  6.94 us
    pallas_call x1, Pallas kernels, prepare_far(): pl.pallas_call(far_kernel, out_shape=(part, part), in_specs=[pl.BlockSpec...  6.13 us
    pallas_call x1, Pallas kernels, force(): pl.pallas_call(forcing_kernel, out_shape=jax.ShapeDtypeStruct((copies, st...  3.72 us
    unnamed x9, local copies, waits for them, and re-layouts  3.53 us
  transfers between devices with their start and end apart: 4, of which 3 were waited for; matrix products, arithmetic and copies ran while one was open for 0% of the time, Pallas kernels for 12%

profile of v6, /device:TPU:39, one launch (start us, length us, event | category | flops | bytes accessed | tf_op | source)
XLA Modules:
  0.0 127.4 jit_solution(7499523174021274758)
XLA Ops:
  0.0 1.3 %copy.9 = bf16[32,16,512]{2,0,1:T(8,128)(2,1)S(1)} copy(bf16[32,16,512]{2,1,0:T(8,128)(2,1)} %param.6) | data formatting | bytes 1048576 | tf_op args[0]
  1.4 1.3 %collective-permute-start = (bf16[11,32,512]{2,1,0:T(8,128)(2,1)S(1)}, bf16[11,32,512]{2,1,0:T(8,128)(2,1)S(1)}, u32[]{:S(2)}, u32[]{:S(2)}) collective-permute-start(bf16[11,32,512]{2,1,0:T(8,128)(2,1)S(1)} %slice.4), channel_id=1, source_target_pairs={{0,1},{1,2},{2,3},{3,4},{4,5},{5,6},{6,7},{8,9},{9,10},{10,11},{11... | collective-permute-start | bytes 1081352 | tf_op jit(solution)/shard_map/ppermute | solution.py:20
  2.7 9.7 %near_factors.1 = (f32[2,600,640]{2,1,0:T(8,128)}, bf16[256,640]{1,0:T(8,128)(2,1)}, bf16[256,640]{1,0:T(8,128)(2,1)}) custom-call(f32[600,600]{1,0:T(8,128)} %diag_ref.5, f32[3,600,600]{2,1,0:T(8,128)} %coupling_ref.2), custom_call_target="tpu_custom_call" | custom-call | flops 5184000000 | bytes 5760000 | tf_op jit(solution)/shard_map/near_factors/pallas_call | solution.py:209
  12.4 0.2 collective-permute-done
  12.6 1.0 pad_maximum_fusion.source_ref
  13.5 9.5 %predict.1 = (s16[16,16,640]{2,1,0:T(8,128)(2,1)}, f32[16,16,640]{2,1,0:T(8,128)}) custom-call(s32[8]{0:T(128)} %offsets_ref.1, bf16[27,32,512]{2,1,0:T(8,128)(2,1)} %pad_maximum_fusion.source_ref, bf16[8,600,512]{2,1,0:T(8,128)(2,1)} %bitcast.10), custom_call_target="tpu_custom_call" | custom-call | flops 2516582400 | bytes 4915200 | tf_op jit(solution)/shard_map/predict/pallas_call | solution.py:310
  23.1 1.6 %collective-permute-start.1 = (s16[16,16,640]{2,1,0:T(8,128)(2,1)}, s16[16,16,640]{2,1,0:T(8,128)(2,1)S(1)}, u32[]{:S(2)}, u32[]{:S(2)}) collective-permute-start(s16[16,16,640]{2,1,0:T(8,128)(2,1)} %get-tuple-element.29), channel_id=1, source_target_pairs={{0,8},{8,0},{16,24},{24,16},{32,40},{40,32},{48,56},{56,48},{64,72... | collective-permute-start | bytes 983048 | tf_op jit(solution)/shard_map/ppermute | solution.py:446
  24.7 1.5 %collective-permute-done.1.code_ref = s16[16,16,640]{2,1,0:T(8,128)(2,1)S(1)} collective-permute-done((s16[16,16,640]{2,1,0:T(8,128)(2,1)}, s16[16,16,640]{2,1,0:T(8,128)(2,1)S(1)}, u32[]{:S(2)}, u32[]{:S(2)}) %collective-permute-start.1) | collective-permute-done | bytes 327712 | tf_op jit(solution)/shard_map/ppermute | solution.py:446
  26.2 0.0 copy-start.2
  26.2 0.7 copy-done.2
  26.9 2.7 %merge.1 = s16[16,16,640]{2,1,0:T(8,128)(2,1)} custom-call(f32[16,16,640]{2,1,0:T(8,128)} %get-tuple-element.28.own_ref, s16[16,16,640]{2,1,0:T(8,128)(2,1)} %copy-done.2), custom_call_target="tpu_custom_call" | custom-call | tf_op jit(solution)/shard_map/merge/pallas_call | solution.py:355
  29.6 22.9 %all_to_all.15.code_ref = s16[16,16,640]{2,1,0:T(8,128)(2,1)} all-to-all(s16[16,16,640]{2,1,0:T(8,128)(2,1)} %merge.1), channel_id=1, replica_groups={{0,16,32,48,64,80,96,112,128,144,160,176,192,208,224,240},{8,24,40,56,7..., dimensions={0} | all-to-all | bytes 655360 | tf_op jit(solution)/shard_map/all_to_all | solution.py:449
  52.5 3.7 %forcing.1 = f32[8,16,1,640]{3,2,1,0:T(1,128)} custom-call(s32[1]{0:T(128)} %bitcast.2.place_ref, s16[16,16,640]{2,1,0:T(8,128)(2,1)} %all_to_all.15.code_ref, bf16[32,16,600]{2,1,0:T(8,128)(2,1)} %observed_ref.1, f32[600,600]{1,0:T(8,128)} %diag_ref.5), custom_call_target="tpu_custom_call" | custom-call | tf_op jit(solution)/shard_map/forcing/pallas_call | solution.py:413
  56.2 6.9 %all-to-all-start.1 = ((f32[8,16,1,640]{3,2,1,0:T(1,128)}), f32[8,16,1,640]{3,2,1,0:T(1,128)S(1)}, u32[]{:S(2)}, u32[]{:S(2)}) async-start(f32[8,16,1,640]{3,2,1,0:T(1,128)} %forcing.1), calls=%async_computation.1 | async-start | bytes 655360 | tf_op jit(solution)/shard_map/all_to_all | solution.py:453
  63.2 6.1 %far_factors.1 = (bf16[640,640]{1,0:T(8,128)(2,1)}, bf16[640,640]{1,0:T(8,128)(2,1)}) custom-call(f32[600,600]{1,0:T(8,128)} %diag_ref.5, f32[3,600,600]{2,1,0:T(8,128)} %coupling_ref.2), custom_call_target="tpu_custom_call" | custom-call | flops 2592000000 | bytes 4320000 | tf_op jit(solution)/shard_map/far_factors/pallas_call | solution.py:233
  69.3 0.0 all-to-all-done.1
  69.3 0.0 copy-start
  69.3 0.7 copy-done
  70.1 34.9 %chain.1 = (s16[16,16,640]{2,1,0:T(8,128)(2,1)}, f32[16,1,640]{2,1,0:T(1,128)}) custom-call(f32[2,600,640]{2,1,0:T(8,128)} %get-tuple-element.24.near_ref, bf16[256,640]{1,0:T(8,128)(2,1)} %get-tuple-element.25.two_hi, bf16[256,640]{1,0:T(8,128)(2,1)} %get-tuple-element.26.two_lo, bf16[640,640]{1,0:T(8,128)(2,1)} %get-tuple-element.33.three_hi, ...), custom_call_target="tpu_custom_call" | custom-call | tf_op jit(solution)/shard_map/chain/pallas_call | solution.py:138
  105.0 14.5 %all_to_all.16.own_ref = s16[16,16,640]{2,1,0:T(8,128)(2,1)S(1)} all-to-all(s16[16,16,640]{2,1,0:T(8,128)(2,1)} %get-tuple-element.36), channel_id=1, replica_groups={{0,16,32,48,64,80,96,112,128,144,160,176,192,208,224,240},{8,24,40,56,7..., dimensions={0} | all-to-all | bytes 655360 | tf_op jit(solution)/shard_map/all_to_all | solution.py:456
  119.5 0.0 copy-start.1
  119.5 3.4 %collective-permute-start.2 = (s16[16,16,640]{2,1,0:T(8,128)(2,1)S(1)}, s16[16,16,640]{2,1,0:T(8,128)(2,1)S(1)}, u32[]{:S(2)}, u32[]{:S(2)}) collective-permute-start(s16[16,16,640]{2,1,0:T(8,128)(2,1)S(1)} %all_to_all.16.own_ref), channel_id=1, source_target_pairs={{0,8},{8,0},{16,24},{24,16},{32,40},{40,32},{48,56},{56,48},{64,72... | collective-permute-start | bytes 983048 | tf_op jit(solution)/shard_map/ppermute | solution.py:457
  122.8 1.3 collective-permute-done.2.other_ref
  124.1 0.0 copy-done.1
  124.1 0.0 copy-start.3
  124.1 0.7 copy-done.3
  124.8 2.5 %decode.1 = f32[16,2,16,600]{3,2,1,0:T(8,128)} custom-call(s16[16,16,640]{2,1,0:T(8,128)(2,1)} %copy-done.1, s16[16,16,640]{2,1,0:T(8,128)(2,1)} %copy-done.3), custom_call_target="tpu_custom_call" | custom-call | tf_op jit(solution)/shard_map/decode/pallas_call | solution.py:378
  (1 shorter events, 0.0 us)
Async XLA Ops:
  1.4 11.2 %collective-permute-start = (bf16[11,32,512]{2,1,0:T(8,128)(2,1)S(1)}, bf16[11,32,512]{2,1,0:T(8,128)(2,1)S(1)}, u32[]{:S(2)}, u32[]{:S(2)}) collective-permute-start(bf16[11,32,512]{2,1,0:T(8,128)(2,1)S(1)} %slice.4), channel_id=1, source_target_pairs={{0,1},{1,2},{2,3},{3,4},{4,5},{5,6},{6,7},{8,9},{9,10},{10,11},{11... | collective-permute-start | bytes 1081352 | tf_op jit(solution)/shard_map/ppermute | solution.py:20
  23.1 3.1 %collective-permute-start.1 = (s16[16,16,640]{2,1,0:T(8,128)(2,1)}, s16[16,16,640]{2,1,0:T(8,128)(2,1)S(1)}, u32[]{:S(2)}, u32[]{:S(2)}) collective-permute-start(s16[16,16,640]{2,1,0:T(8,128)(2,1)} %get-tuple-element.29), channel_id=1, source_target_pairs={{0,8},{8,0},{16,24},{24,16},{32,40},{40,32},{48,56},{56,48},{64,72... | collective-permute-start | bytes 983048 | tf_op jit(solution)/shard_map/ppermute | solution.py:446
  26.2 0.7 copy-start.2
  56.2 13.1 %all-to-all-start.1 = ((f32[8,16,1,640]{3,2,1,0:T(1,128)}), f32[8,16,1,640]{3,2,1,0:T(1,128)S(1)}, u32[]{:S(2)}, u32[]{:S(2)}) async-start(f32[8,16,1,640]{3,2,1,0:T(1,128)} %forcing.1), calls=%async_computation.1 | async-start | bytes 655360 | tf_op jit(solution)/shard_map/all_to_all | solution.py:453
  69.3 0.7 copy-start
  119.5 4.6 %copy-start.1 = (s16[16,16,640]{2,1,0:T(8,128)(2,1)}, s16[16,16,640]{2,1,0:T(8,128)(2,1)S(1)}, u32[]{:S(2)}) copy-start(s16[16,16,640]{2,1,0:T(8,128)(2,1)S(1)} %all_to_all.16.own_ref) | copy-start | bytes 983044
  119.5 4.6 %collective-permute-start.2 = (s16[16,16,640]{2,1,0:T(8,128)(2,1)S(1)}, s16[16,16,640]{2,1,0:T(8,128)(2,1)S(1)}, u32[]{:S(2)}, u32[]{:S(2)}) collective-permute-start(s16[16,16,640]{2,1,0:T(8,128)(2,1)S(1)} %all_to_all.16.own_ref), channel_id=1, source_target_pairs={{0,8},{8,0},{16,24},{24,16},{32,40},{40,32},{48,56},{56,48},{64,72... | collective-permute-start | bytes 983048 | tf_op jit(solution)/shard_map/ppermute | solution.py:457
  124.1 0.7 copy-start.3

commit v7 on v6

--- a/solution.py
+++ b/solution.py
@@ -8,6 +8,7 @@
 from jax.sharding import PartitionSpec as P
 
 REACH = 12
+AHEAD = 3
 LANES = 128
 LEVELS = 32700.0
 OCTAVE = 64.0
@@ -248,7 +249,8 @@
 
 
 def predict_kernel(
-    offsets_ref, source_ref, kernel_hbm, code_ref, own_ref, kernel_ref, total_ref, arrived
+    offsets_ref, rim_hbm, steps_hbm, kernel_hbm, code_ref, own_ref,
+    source_ref, kernel_ref, total_ref, arrived, here,
 ):
     samples, cols = source_ref.shape[1:]
     steps = code_ref.shape[1]
@@ -257,12 +259,26 @@
     def fetch(lag):
         return pltpu.make_async_copy(kernel_hbm.at[lag], kernel_ref.at[lag], arrived.at[lag])
 
-    for lag in range(lag_count):
+    rim_rows = rim_hbm.shape[0]
+    inputs = [
+        pltpu.make_async_copy(steps_hbm, source_ref.at[rim_rows:], here.at[0]),
+        pltpu.make_async_copy(rim_hbm, source_ref.at[:rim_rows], here.at[1]),
+    ]
+    for copy in inputs:
+        copy.start()
+    for lag in range(AHEAD):
         fetch(lag).start()
     total_ref[...] = jnp.zeros_like(total_ref)
+    for copy in inputs:
+        copy.wait()
 
     def add(lag, unused):
         fetch(lag).wait()
+
+        @pl.when(lag + AHEAD < lag_count)
+        def more():
+            fetch(lag + AHEAD).start()
+
         window = source_ref[pl.ds(REACH - 1 - offsets_ref[lag], steps)]
         window = window.reshape(steps * samples, cols)
         for start in range(0, sensors, 2 * LANES):
@@ -302,10 +318,9 @@
     lax.fori_loop(0, samples // 8, several, 0)
 
 
-def predict(source, kernel, lag_offsets):
+def predict(rim, by_step, kernel, lag_offsets):
     lag_count, sensors, cols = kernel.shape
-    span, samples, unused_cols = source.shape
-    steps = span - (REACH - 1)
+    steps, samples, unused_cols = by_step.shape
     width = -(-sensors // LANES) * LANES
     return pl.pallas_call(
         predict_kernel,
@@ -315,14 +330,17 @@
         ),
         in_specs=[
             pl.BlockSpec(memory_space=pltpu.SMEM),
-            pl.BlockSpec(memory_space=pltpu.VMEM),
+            pl.BlockSpec(memory_space=pl.ANY),
+            pl.BlockSpec(memory_space=pl.ANY),
             pl.BlockSpec(memory_space=pl.ANY),
         ],
         out_specs=[pl.BlockSpec(memory_space=pltpu.VMEM)] * 2,
         scratch_shapes=[
+            pltpu.VMEM((rim.shape[0] + steps, samples, cols), jnp.bfloat16),
             pltpu.VMEM((lag_count, sensors, cols), jnp.bfloat16),
             pltpu.VMEM((width // LANES, steps * samples, LANES), jnp.float32),
             pltpu.SemaphoreType.DMA((lag_count,)),
+            pltpu.SemaphoreType.DMA((2,)),
         ],
         cost_estimate=pl.CostEstimate(
             flops=2 * steps * samples * lag_count * cols * sensors,
@@ -330,7 +348,7 @@
             transcendentals=0,
         ),
         name="predict",
-    )(lag_offsets, source, kernel)
+    )(lag_offsets, rim, by_step, kernel)
 
 
 def decoded(code, sensors):
@@ -341,22 +359,18 @@
 def merge_kernel(sensors, own_ref, code_ref, merged_ref):
     lane = lax.broadcasted_iota(jnp.int32, own_ref.shape[1:], 1)
 
-    def several(group, unused):
-        for member in range(4):
-            pair = 4 * group + member
-            other = jnp.where(lane < sensors, decoded(code_ref[pair], sensors), 0.0)
-            merged_ref[pair] = coded_with_grade(own_ref[pair] + other, sensors)
-        return unused
-
-    lax.fori_loop(0, own_ref.shape[0] // 4, several, 0)
+    for pair in range(own_ref.shape[0]):
+        other = jnp.where(lane < sensors, decoded(code_ref[pair], sensors), 0.0)
+        merged_ref[pair] = coded_with_grade(own_ref[pair] + other, sensors)
 
 
 def merge(own, code, sensors):
     return pl.pallas_call(
         functools.partial(merge_kernel, sensors),
         out_shape=jax.ShapeDtypeStruct(code.shape, code.dtype),
-        in_specs=[pl.BlockSpec(memory_space=pltpu.VMEM)] * 2,
-        out_specs=pl.BlockSpec(memory_space=pltpu.VMEM),
+        in_specs=[pl.BlockSpec((4, *own.shape[1:]), lambda i: (i, 0, 0))] * 2,
+        out_specs=pl.BlockSpec((4, *own.shape[1:]), lambda i: (i, 0, 0)),
+        grid=(own.shape[0] // 4,),
         name="merge",
     )(own, code)
 
@@ -365,12 +379,9 @@
     sensors = out_ref.shape[3]
     core = lax.rem(lax.axis_index("param"), 2)
 
-    def one(pair, unused):
+    for pair in range(own_ref.shape[0]):
         out_ref[pair, core] = decoded(own_ref[pair], sensors)[:, :sensors]
         out_ref[pair, 1 - core] = decoded(other_ref[pair], sensors)[:, :sensors]
-        return unused
-
-    lax.fori_loop(0, own_ref.shape[0], one, 0, unroll=4)
 
 
 def decode(own, other, sensors):
@@ -378,8 +389,9 @@
     out = pl.pallas_call(
         decode_kernel,
         out_shape=jax.ShapeDtypeStruct((pairs, 2, steps, sensors), jnp.float32),
-        in_specs=[pl.BlockSpec(memory_space=pltpu.VMEM)] * 2,
-        out_specs=pl.BlockSpec(memory_space=pltpu.VMEM),
+        in_specs=[pl.BlockSpec((4, *own.shape[1:]), lambda i: (i, 0, 0))] * 2,
+        out_specs=pl.BlockSpec((4, 2, steps, sensors), lambda i: (i, 0, 0, 0)),
+        grid=(pairs // 4,),
         name="decode",
     )(own, other)
     return out.reshape(2 * pairs, steps, sensors)
@@ -440,9 +452,7 @@
     assert share == 1
     chips = [list(range(core, group, 2)) for core in range(2)]
     partner = [(i, i ^ 1) for i in range(group)]
-    code, own = predict(
-        jnp.concatenate([rim, by_step], axis=0), jnp.swapaxes(kernel, 1, 2), lag_offsets
-    )
+    code, own = predict(rim, by_step, jnp.swapaxes(kernel, 1, 2), lag_offsets)
     code = merge(own, lax.ppermute(code, "param", partner), sensors)
     place = lax.axis_index("param").astype(jnp.int32).reshape(1)
     code, place = lax.optimization_barrier((code, place))

time: 128 us -> 130 us (1.016)
  Pallas kernels: 69.3 us -> 71 us
    unnamed x9 -> x13, local copies, waits for them, and re-layouts: 3.53 us -> 4.3 us
where the time goes in v7:
time: 130 us; the launch traced here: 129 us
  Pallas kernels  71 us (55%)
  blocking collectives  37.3 us (29%)
  starting transfers between devices  13.2 us (10%)
  local copies, waits for them, and re-layouts  4.32 us (3%)
  waiting for transfers between devices  2.94 us (2%)
    all_to_all x2, blocking collectives, per_device(): lax.all_to_all(code, 'param', 0, 0, tiled=True, axis_index_groups=chips)  37.3 us
    pallas_call x1, Pallas kernels, run_chain(): pl.pallas_call(functools.partial(chain_kernel, block, sensors), out_shape...  34.9 us
    pallas_call x1, Pallas kernels, prepare_near(): pl.pallas_call(near_kernel, out_shape=(jax.ShapeDtypeStruct((2, sensors,...  9.68 us
    pallas_call x1, Pallas kernels, predict(): pl.pallas_call(predict_kernel, out_shape=(jax.ShapeDtypeStruct((samples /...  9.46 us
    all_to_all x1, starting transfers between devices, per_device(): every = lax.all_to_all(forced, 'tm', 0, 0, tiled=True)  6.94 us
    pallas_call x1, Pallas kernels, prepare_far(): pl.pallas_call(far_kernel, out_shape=(part, part), in_specs=[pl.BlockSpec...  6.13 us
    unnamed x13, local copies, waits for them, and re-layouts  4.3 us
    pallas_call x1, Pallas kernels, force(): pl.pallas_call(forcing_kernel, out_shape=jax.ShapeDtypeStruct((copies, st...  3.71 us
  transfers between devices with their start and end apart: 4, of which 3 were waited for; matrix products, arithmetic and copies ran while one was open for 0% of the time, Pallas kernels for 12%

profile of v7, /device:TPU:39, one launch (start us, length us, event | category | flops | bytes accessed | tf_op | source)
XLA Modules:
  0.0 128.9 jit_solution(6793020995574585162)
XLA Ops:
  0.0 1.3 %copy.9 = bf16[32,16,512]{2,0,1:T(8,128)(2,1)S(1)} copy(bf16[32,16,512]{2,1,0:T(8,128)(2,1)} %param.6) | data formatting | bytes 1048576 | tf_op args[0]
  1.3 0.0 copy-start
  1.4 1.3 %collective-permute-start = (bf16[11,32,512]{2,1,0:T(8,128)(2,1)S(1)}, bf16[11,32,512]{2,1,0:T(8,128)(2,1)S(1)}, u32[]{:S(2)}, u32[]{:S(2)}) collective-permute-start(bf16[11,32,512]{2,1,0:T(8,128)(2,1)S(1)} %slice.4), channel_id=1, source_target_pairs={{0,1},{1,2},{2,3},{3,4},{4,5},{5,6},{6,7},{8,9},{9,10},{10,11},{11... | collective-permute-start | bytes 1081352 | tf_op jit(solution)/shard_map/ppermute | solution.py:21
  2.7 9.7 %near_factors.1 = (f32[2,600,640]{2,1,0:T(8,128)}, bf16[256,640]{1,0:T(8,128)(2,1)}, bf16[256,640]{1,0:T(8,128)(2,1)}) custom-call(f32[600,600]{1,0:T(8,128)} %diag_ref.5, f32[3,600,600]{2,1,0:T(8,128)} %coupling_ref.2), custom_call_target="tpu_custom_call" | custom-call | flops 5184000000 | bytes 5760000 | tf_op jit(solution)/shard_map/near_factors/pallas_call | solution.py:210
  12.4 0.0 copy-done
  12.4 0.2 collective-permute-done.rim_hbm
  12.6 0.0 copy-start.5
  12.6 0.8 copy-done.5
  13.3 9.5 %predict.1 = (s16[16,16,640]{2,1,0:T(8,128)(2,1)}, f32[16,16,640]{2,1,0:T(8,128)}) custom-call(s32[8]{0:T(128)} %offsets_ref.1, bf16[11,32,512]{2,1,0:T(8,128)(2,1)} %copy-done.5, bf16[16,32,512]{2,1,0:T(8,128)(2,1)} %bitcast.8, bf16[8,600,512]{2,1,0:T(8,128)(2,1)} %bitcast.10), custom_call_target="tpu_custom_call" | custom-call | flops 2516582400 | bytes 4915200 | tf_op jit(solution)/shard_map/predict/pallas_call | solution.py:325
  22.8 1.6 %collective-permute-start.1 = (s16[16,16,640]{2,1,0:T(8,128)(2,1)}, s16[16,16,640]{2,1,0:T(8,128)(2,1)S(1)}, u32[]{:S(2)}, u32[]{:S(2)}) collective-permute-start(s16[16,16,640]{2,1,0:T(8,128)(2,1)} %get-tuple-element.29), channel_id=1, source_target_pairs={{0,8},{8,0},{16,24},{24,16},{32,40},{40,32},{48,56},{56,48},{64,72... | collective-permute-start | bytes 983048 | tf_op jit(solution)/shard_map/ppermute | solution.py:456
  24.4 1.5 %collective-permute-done.1.code_ref = s16[16,16,640]{2,1,0:T(8,128)(2,1)S(1)} collective-permute-done((s16[16,16,640]{2,1,0:T(8,128)(2,1)}, s16[16,16,640]{2,1,0:T(8,128)(2,1)S(1)}, u32[]{:S(2)}, u32[]{:S(2)}) %collective-permute-start.1) | collective-permute-done | bytes 327712 | tf_op jit(solution)/shard_map/ppermute | solution.py:456
  25.9 0.0 copy-start.3
  25.9 0.7 copy-done.3
  26.6 3.6 %merge.1 = s16[16,16,640]{2,1,0:T(8,128)(2,1)} custom-call(f32[16,16,640]{2,1,0:T(8,128)} %get-tuple-element.28.own_ref, s16[16,16,640]{2,1,0:T(8,128)(2,1)} %copy-done.3), custom_call_target="tpu_custom_call" | custom-call | tf_op jit(solution)/shard_map/merge/pallas_call | solution.py:368
  30.2 22.9 %all_to_all.15.code_ref = s16[16,16,640]{2,1,0:T(8,128)(2,1)} all-to-all(s16[16,16,640]{2,1,0:T(8,128)(2,1)} %merge.1), channel_id=1, replica_groups={{0,16,32,48,64,80,96,112,128,144,160,176,192,208,224,240},{8,24,40,56,7..., dimensions={0} | all-to-all | bytes 655360 | tf_op jit(solution)/shard_map/all_to_all | solution.py:459
  53.1 3.7 %forcing.1 = f32[8,16,1,640]{3,2,1,0:T(1,128)} custom-call(s32[1]{0:T(128)} %bitcast.2.place_ref, s16[16,16,640]{2,1,0:T(8,128)(2,1)} %all_to_all.15.code_ref, bf16[32,16,600]{2,1,0:T(8,128)(2,1)} %observed_ref.1, f32[600,600]{1,0:T(8,128)} %diag_ref.5), custom_call_target="tpu_custom_call" | custom-call | tf_op jit(solution)/shard_map/forcing/pallas_call | solution.py:425
  56.8 6.9 %all-to-all-start.1 = ((f32[8,16,1,640]{3,2,1,0:T(1,128)}), f32[8,16,1,640]{3,2,1,0:T(1,128)S(1)}, u32[]{:S(2)}, u32[]{:S(2)}) async-start(f32[8,16,1,640]{3,2,1,0:T(1,128)} %forcing.1), calls=%async_computation.1 | async-start | bytes 655360 | tf_op jit(solution)/shard_map/all_to_all | solution.py:463
  63.8 6.1 %far_factors.1 = (bf16[640,640]{1,0:T(8,128)(2,1)}, bf16[640,640]{1,0:T(8,128)(2,1)}) custom-call(f32[600,600]{1,0:T(8,128)} %diag_ref.5, f32[3,600,600]{2,1,0:T(8,128)} %coupling_ref.2), custom_call_target="tpu_custom_call" | custom-call | flops 2592000000 | bytes 4320000 | tf_op jit(solution)/shard_map/far_factors/pallas_call | solution.py:234
  69.9 0.0 all-to-all-done.1
  69.9 0.0 copy-start.1
  69.9 0.7 copy-done.1
  70.6 34.9 %chain.1 = (s16[16,16,640]{2,1,0:T(8,128)(2,1)}, f32[16,1,640]{2,1,0:T(1,128)}) custom-call(f32[2,600,640]{2,1,0:T(8,128)} %get-tuple-element.24.near_ref, bf16[256,640]{1,0:T(8,128)(2,1)} %get-tuple-element.25.two_hi, bf16[256,640]{1,0:T(8,128)(2,1)} %get-tuple-element.26.two_lo, bf16[640,640]{1,0:T(8,128)(2,1)} %get-tuple-element.33.three_hi, ...), custom_call_target="tpu_custom_call" | custom-call | tf_op jit(solution)/shard_map/chain/pallas_call | solution.py:139
  105.5 14.5 %all_to_all.16.own_ref = s16[16,16,640]{2,1,0:T(8,128)(2,1)S(1)} all-to-all(s16[16,16,640]{2,1,0:T(8,128)(2,1)} %get-tuple-element.36), channel_id=1, replica_groups={{0,16,32,48,64,80,96,112,128,144,160,176,192,208,224,240},{8,24,40,56,7..., dimensions={0} | all-to-all | bytes 655360 | tf_op jit(solution)/shard_map/all_to_all | solution.py:466
  120.0 0.0 copy-start.2
  120.0 3.4 %collective-permute-start.2 = (s16[16,16,640]{2,1,0:T(8,128)(2,1)S(1)}, s16[16,16,640]{2,1,0:T(8,128)(2,1)S(1)}, u32[]{:S(2)}, u32[]{:S(2)}) collective-permute-start(s16[16,16,640]{2,1,0:T(8,128)(2,1)S(1)} %all_to_all.16.own_ref), channel_id=1, source_target_pairs={{0,8},{8,0},{16,24},{24,16},{32,40},{40,32},{48,56},{56,48},{64,72... | collective-permute-start | bytes 983048 | tf_op jit(solution)/shard_map/ppermute | solution.py:467
  123.4 1.3 collective-permute-done.2.other_ref
  124.6 0.0 copy-done.2
  124.6 0.0 copy-start.4
  124.7 0.7 copy-done.4
  125.4 3.5 %decode.1 = f32[16,2,16,600]{3,2,1,0:T(8,128)} custom-call(s16[16,16,640]{2,1,0:T(8,128)(2,1)} %copy-done.2, s16[16,16,640]{2,1,0:T(8,128)(2,1)} %copy-done.4), custom_call_target="tpu_custom_call" | custom-call | tf_op jit(solution)/shard_map/decode/pallas_call | solution.py:389
  (1 shorter events, 0.0 us)
Async XLA Ops:
  1.3 11.0 %copy-start = (bf16[32,16,512]{2,0,1:T(8,128)(2,1)}, bf16[32,16,512]{2,0,1:T(8,128)(2,1)S(1)}, u32[]{:S(2)}) copy-start(bf16[32,16,512]{2,0,1:T(8,128)(2,1)S(1)} %copy.9) | copy-start | bytes 1572868
  1.4 11.2 %collective-permute-start = (bf16[11,32,512]{2,1,0:T(8,128)(2,1)S(1)}, bf16[11,32,512]{2,1,0:T(8,128)(2,1)S(1)}, u32[]{:S(2)}, u32[]{:S(2)}) collective-permute-start(bf16[11,32,512]{2,1,0:T(8,128)(2,1)S(1)} %slice.4), channel_id=1, source_target_pairs={{0,1},{1,2},{2,3},{3,4},{4,5},{5,6},{6,7},{8,9},{9,10},{10,11},{11... | collective-permute-start | bytes 1081352 | tf_op jit(solution)/shard_map/ppermute | solution.py:21
  12.6 0.8 copy-start.5
  22.8 3.1 %collective-permute-start.1 = (s16[16,16,640]{2,1,0:T(8,128)(2,1)}, s16[16,16,640]{2,1,0:T(8,128)(2,1)S(1)}, u32[]{:S(2)}, u32[]{:S(2)}) collective-permute-start(s16[16,16,640]{2,1,0:T(8,128)(2,1)} %get-tuple-element.29), channel_id=1, source_target_pairs={{0,8},{8,0},{16,24},{24,16},{32,40},{40,32},{48,56},{56,48},{64,72... | collective-permute-start | bytes 983048 | tf_op jit(solution)/shard_map/ppermute | solution.py:456
  25.9 0.7 copy-start.3
  56.8 13.1 %all-to-all-start.1 = ((f32[8,16,1,640]{3,2,1,0:T(1,128)}), f32[8,16,1,640]{3,2,1,0:T(1,128)S(1)}, u32[]{:S(2)}, u32[]{:S(2)}) async-start(f32[8,16,1,640]{3,2,1,0:T(1,128)} %forcing.1), calls=%async_computation.1 | async-start | bytes 655360 | tf_op jit(solution)/shard_map/all_to_all | solution.py:463
  69.9 0.7 copy-start.1
  120.0 4.6 %copy-start.2 = (s16[16,16,640]{2,1,0:T(8,128)(2,1)}, s16[16,16,640]{2,1,0:T(8,128)(2,1)S(1)}, u32[]{:S(2)}) copy-start(s16[16,16,640]{2,1,0:T(8,128)(2,1)S(1)} %all_to_all.16.own_ref) | copy-start | bytes 983044
  120.0 4.6 %collective-permute-start.2 = (s16[16,16,640]{2,1,0:T(8,128)(2,1)S(1)}, s16[16,16,640]{2,1,0:T(8,128)(2,1)S(1)}, u32[]{:S(2)}, u32[]{:S(2)}) collective-permute-start(s16[16,16,640]{2,1,0:T(8,128)(2,1)S(1)} %all_to_all.16.own_ref), channel_id=1, source_target_pairs={{0,8},{8,0},{16,24},{24,16},{32,40},{40,32},{48,56},{56,48},{64,72... | collective-permute-start | bytes 983048 | tf_op jit(solution)/shard_map/ppermute | solution.py:467
  124.6 0.7 copy-start.4

commit v8 on v6

--- a/solution.py
+++ b/solution.py
@@ -151,6 +151,7 @@
             pltpu.VMEM((2, 16, width), jnp.float32),
         ],
         name="chain",
+        compiler_params=pltpu.CompilerParams(vmem_limit_bytes=12 << 20),
     )(near, two_hi, two_lo, three_hi, three_lo, forcing)
     return code
 
@@ -224,6 +225,7 @@
             flops=12 * 2 * sensors**3, bytes_accessed=16 * sensors**2, transcendentals=0
         ),
         name="near_factors",
+        compiler_params=pltpu.CompilerParams(vmem_limit_bytes=18 << 20),
     )(diag_inverse, coupling)
 
 
@@ -244,6 +246,7 @@
             flops=12 * sensors**3, bytes_accessed=12 * sensors**2, transcendentals=0
         ),
         name="far_factors",
+        compiler_params=pltpu.CompilerParams(vmem_limit_bytes=14 << 20),
     )(diag_inverse, coupling)
 
 
@@ -330,6 +333,7 @@
             transcendentals=0,
         ),
         name="predict",
+        compiler_params=pltpu.CompilerParams(vmem_limit_bytes=14 << 20),
     )(lag_offsets, source, kernel)
 
 
@@ -358,6 +362,7 @@
         in_specs=[pl.BlockSpec(memory_space=pltpu.VMEM)] * 2,
         out_specs=pl.BlockSpec(memory_space=pltpu.VMEM),
         name="merge",
+        compiler_params=pltpu.CompilerParams(vmem_limit_bytes=4 << 20),
     )(own, code)
 
 
@@ -381,6 +386,7 @@
         in_specs=[pl.BlockSpec(memory_space=pltpu.VMEM)] * 2,
         out_specs=pl.BlockSpec(memory_space=pltpu.VMEM),
         name="decode",
+        compiler_params=pltpu.CompilerParams(vmem_limit_bytes=6 << 20),
     )(own, other)
     return out.reshape(2 * pairs, steps, sensors)
 
@@ -424,6 +430,7 @@
             out_specs=pl.BlockSpec((copies, steps, 1, width), lambda i, place: (0, 0, 0, 0)),
         ),
         name="forcing",
+        compiler_params=pltpu.CompilerParams(vmem_limit_bytes=6 << 20),
     )(place, code, observed, diag_inverse)
 
 

time: 128 us -> 131 us (1.023)
  local copies, waits for them, and re-layouts: 3.55 us -> 19.9 us
  Pallas kernels: 69.3 us -> 57.2 us
    unnamed x9 -> x39, local copies, waits for them, and re-layouts: 3.53 us -> 19.9 us
    pallas_call x1, Pallas kernels: 9.69 us -> 5.87 us  [prepare_near(): pl.pallas_call(near_kernel, out_shape=(jax.ShapeDtypeStruct((2, sensors,...]
    pallas_call x1, Pallas kernels: 6.13 us -> 3.19 us  [prepare_far(): pl.pallas_call(far_kernel, out_shape=(part, part), in_specs=[pl.BlockSpec...]
    pallas_call x1, Pallas kernels: 3.72 us -> 1.46 us  [force(): pl.pallas_call(forcing_kernel, out_shape=jax.ShapeDtypeStruct((copies, st...]
    pallas_call x1, Pallas kernels: 2.74 us -> 0.82 us  [merge(): pl.pallas_call(functools.partial(merge_kernel, sensors), out_shape=jax.Sh...]
  transfers between devices with their start and end apart: 4 -> 4, of which waited for: 3 -> 3; matrix products, arithmetic and copies ran while one was open for 0% -> 0% of each run, Pallas kernels for 12% -> 7%
where the time goes in v8:
time: 131 us; the launch traced here: 130 us
  Pallas kernels  57.2 us (44%)
  blocking collectives  36.5 us (28%)
  local copies, waits for them, and re-layouts  19.9 us (15%)
  starting transfers between devices  13 us (10%)
  waiting for transfers between devices  3.01 us (2%)
    all_to_all x2, blocking collectives, per_device(): lax.all_to_all(code, 'param', 0, 0, tiled=True, axis_index_groups=chips)  36.5 us
    pallas_call x1, Pallas kernels, run_chain(): pl.pallas_call(functools.partial(chain_kernel, block, sensors), out_shape...  35.4 us
    unnamed x39, local copies, waits for them, and re-layouts  19.9 us
    pallas_call x1, Pallas kernels, predict(): pl.pallas_call(predict_kernel, out_shape=(jax.ShapeDtypeStruct((samples /...  8.99 us
    all_to_all x1, starting transfers between devices, per_device(): every = lax.all_to_all(forced, 'tm', 0, 0, tiled=True)  6.72 us
    pallas_call x1, Pallas kernels, prepare_near(): pl.pallas_call(near_kernel, out_shape=(jax.ShapeDtypeStruct((2, sensors,...  5.87 us
    ppermute x1, starting transfers between devices, per_device(): return decode(code, lax.ppermute(code, 'param', partner), sensors)  3.47 us
    pallas_call x1, Pallas kernels, prepare_far(): pl.pallas_call(far_kernel, out_shape=(part, part), in_specs=[pl.BlockSpec...  3.19 us
  transfers between devices with their start and end apart: 4, of which 3 were waited for; matrix products, arithmetic and copies ran while one was open for 0% of the time, Pallas kernels for 7%

profile of v8, /device:TPU:39, one launch (start us, length us, event | category | flops | bytes accessed | tf_op | source)
XLA Modules:
  0.0 129.9 jit_solution(4396185020684153929)
XLA Ops:
  0.0 1.3 %copy.9 = bf16[32,16,512]{2,0,1:T(8,128)(2,1)S(1)} copy(bf16[32,16,512]{2,1,0:T(8,128)(2,1)} %param.6) | data formatting | bytes 1048576 | tf_op args[0]
  1.4 1.3 collective-permute-start
  2.7 0.0 copy-start
  2.7 1.4 %copy-done = f32[600,600]{1,0:T(8,128)S(1)} copy-done((f32[600,600]{1,0:T(8,128)S(1)}, f32[600,600]{1,0:T(8,128)}, u32[]{:S(2)}) %copy-start) | copy-done | bytes 1440024
  4.1 0.0 copy-start.16
  4.1 2.3 %copy-done.16 = f32[3,600,600]{2,1,0:T(8,128)S(1)} copy-done((f32[3,600,600]{2,1,0:T(8,128)S(1)}, f32[3,600,600]{2,1,0:T(8,128)}, u32[]{:S(2)}) %copy-start.16) | copy-done | bytes 4320024
  6.4 0.0 copy-start.15
  6.4 0.0 copy-start.18
  6.4 5.9 %near_factors.1 = (f32[2,600,640]{2,1,0:T(8,128)S(1)}, bf16[256,640]{1,0:T(8,128)(2,1)S(1)}, bf16[256,640]{1,0:T(8,128)(2,1)S(1)}) custom-call(f32[600,600]{1,0:T(8,128)S(1)} %copy-done, f32[3,600,600]{2,1,0:T(8,128)S(1)} %copy-done.16), custom_call_target="tpu_custom_call" | custom-call | flops 5184000000 | bytes 5760000 | tf_op jit(solution)/shard_map/near_factors/pallas_call | solution.py:210
  12.3 0.0 copy-start.11
  12.3 0.0 copy-start.13
  12.3 0.3 collective-permute-done
  12.6 0.1 pad_maximum_fusion.source_ref
  12.6 0.0 copy-done.15
  12.7 0.0 copy-done.18
  12.7 9.0 %predict.1 = (s16[16,16,640]{2,1,0:T(8,128)(2,1)}, f32[16,16,640]{2,1,0:T(8,128)S(1)}) custom-call(s32[8]{0:T(128)S(1)} %copy-done.18, bf16[27,32,512]{2,1,0:T(8,128)(2,1)S(1)} %pad_maximum_fusion.source_ref, bf16[8,600,512]{2,1,0:T(8,128)(2,1)S(1)} %bitcast.8), custom_call_target="tpu_custom_call" | custom-call | flops 2516582400 | bytes 4915200 | tf_op jit(solution)/shard_map/predict/pallas_call | solution.py:313
  21.7 0.0 copy-done.11
  21.7 0.0 copy-done.13
  21.7 0.0 copy-start.8
  21.7 0.8 copy-done.8
  22.5 1.5 %collective-permute-start.1 = (s16[16,16,640]{2,1,0:T(8,128)(2,1)}, s16[16,16,640]{2,1,0:T(8,128)(2,1)S(1)}, u32[]{:S(2)}, u32[]{:S(2)}) collective-permute-start(s16[16,16,640]{2,1,0:T(8,128)(2,1)} %get-tuple-element.29), channel_id=1, source_target_pairs={{0,8},{8,0},{16,24},{24,16},{32,40},{40,32},{48,56},{56,48},{64,72... | collective-permute-start | bytes 983048 | tf_op jit(solution)/shard_map/ppermute | solution.py:453
  24.0 1.5 %collective-permute-done.1.code_ref = s16[16,16,640]{2,1,0:T(8,128)(2,1)S(1)} collective-permute-done((s16[16,16,640]{2,1,0:T(8,128)(2,1)}, s16[16,16,640]{2,1,0:T(8,128)(2,1)S(1)}, u32[]{:S(2)}, u32[]{:S(2)}) %collective-permute-start.1) | collective-permute-done | bytes 327712 | tf_op jit(solution)/shard_map/ppermute | solution.py:453
  25.5 0.0 copy-start.9
  25.5 1.1 copy-done.9
  26.6 0.8 merge.1
  27.4 22.7 %all_to_all.15.code_ref = s16[16,16,640]{2,1,0:T(8,128)(2,1)S(1)} all-to-all(s16[16,16,640]{2,1,0:T(8,128)(2,1)S(1)} %merge.1), channel_id=1, replica_groups={{0,16,32,48,64,80,96,112,128,144,160,176,192,208,224,240},{8,24,40,56,7..., dimensions={0} | all-to-all | bytes 655360 | tf_op jit(solution)/shard_map/all_to_all | solution.py:456
  50.1 0.0 copy-start.1
  50.1 1.4 %copy-done.1 = f32[600,600]{1,0:T(8,128)S(1)} copy-done((f32[600,600]{1,0:T(8,128)S(1)}, f32[600,600]{1,0:T(8,128)}, u32[]{:S(2)}) %copy-start.1) | copy-done | bytes 1440024
  51.5 0.0 copy-start.10
  51.5 1.1 copy-done.10
  52.6 1.5 %forcing.1 = f32[8,16,1,640]{3,2,1,0:T(1,128)S(1)} custom-call(s32[1]{0:T(128)} %bitcast.2.place_ref, s16[16,16,640]{2,1,0:T(8,128)(2,1)S(1)} %all_to_all.15.code_ref, bf16[32,16,600]{2,1,0:T(8,128)(2,1)S(1)} %copy-done.10, f32[600,600]{1,0:T(8,128)S(1)} %copy-done.1), custom_call_target="tpu_custom_call" | custom-call | tf_op jit(solution)/shard_map/forcing/pallas_call | solution.py:419
  54.1 0.0 copy-start.3
  54.1 0.7 copy-done.3
  54.8 6.7 %all-to-all-start.1 = ((f32[8,16,1,640]{3,2,1,0:T(1,128)}), f32[8,16,1,640]{3,2,1,0:T(1,128)S(1)}, u32[]{:S(2)}, u32[]{:S(2)}) async-start(f32[8,16,1,640]{3,2,1,0:T(1,128)} %copy-done.3), calls=%async_computation.1 | async-start | bytes 655360 | tf_op jit(solution)/shard_map/all_to_all | solution.py:460
  61.5 0.0 copy-start.2
  61.5 1.4 %copy-done.2 = f32[600,600]{1,0:T(8,128)S(1)} copy-done((f32[600,600]{1,0:T(8,128)S(1)}, f32[600,600]{1,0:T(8,128)}, u32[]{:S(2)}) %copy-start.2) | copy-done | bytes 1440024
  62.9 0.0 copy-start.17
  62.9 2.3 %copy-done.17 = f32[3,600,600]{2,1,0:T(8,128)S(1)} copy-done((f32[3,600,600]{2,1,0:T(8,128)S(1)}, f32[3,600,600]{2,1,0:T(8,128)}, u32[]{:S(2)}) %copy-start.17) | copy-done | bytes 4320024
  65.2 3.2 %far_factors.1 = (bf16[640,640]{1,0:T(8,128)(2,1)S(1)}, bf16[640,640]{1,0:T(8,128)(2,1)S(1)}) custom-call(f32[600,600]{1,0:T(8,128)S(1)} %copy-done.2, f32[3,600,600]{2,1,0:T(8,128)S(1)} %copy-done.17), custom_call_target="tpu_custom_call" | custom-call | flops 2592000000 | bytes 4320000 | tf_op jit(solution)/shard_map/far_factors/pallas_call | solution.py:235
  68.5 0.0 copy-start.4
  68.5 0.9 copy-done.4
  69.3 0.0 copy-start.6
  69.3 0.9 copy-done.6
  70.2 0.0 all-to-all-done.1
  70.3 0.0 copy-start.5
  70.3 1.1 copy-done.5
  71.4 0.0 copy-start.7
  71.4 1.1 copy-done.7
  72.5 0.0 copy-start.12
  72.5 1.0 copy-done.12
  73.5 0.0 copy-start.14
  73.5 1.0 copy-done.14
  74.5 35.4 %chain.1 = (s16[16,16,640]{2,1,0:T(8,128)(2,1)S(1)}, f32[16,1,640]{2,1,0:T(1,128)}) custom-call(f32[2,600,640]{2,1,0:T(8,128)S(1)} %get-tuple-element.24.near_ref, bf16[256,640]{1,0:T(8,128)(2,1)S(1)} %copy-done.12, bf16[256,640]{1,0:T(8,128)(2,1)S(1)} %copy-done.14, bf16[640,640]{1,0:T(8,128)(2,1)S(1)} %copy-done.5, bf16[640,640]{1,0:T(8,128)(2,1)S(1)} %copy-done.7, ...), custom_call_target="tpu_custom_call" | custom-call | tf_op jit(solution)/shard_map/chain/pallas_call | solution.py:138
  109.9 13.8 %all_to_all.16.own_ref = s16[16,16,640]{2,1,0:T(8,128)(2,1)S(1)} all-to-all(s16[16,16,640]{2,1,0:T(8,128)(2,1)S(1)} %get-tuple-element.36), channel_id=1, replica_groups={{0,16,32,48,64,80,96,112,128,144,160,176,192,208,224,240},{8,24,40,56,7..., dimensions={0} | all-to-all | bytes 655360 | tf_op jit(solution)/shard_map/all_to_all | solution.py:463
  123.7 3.5 %collective-permute-start.2 = (s16[16,16,640]{2,1,0:T(8,128)(2,1)S(1)}, s16[16,16,640]{2,1,0:T(8,128)(2,1)S(1)}, u32[]{:S(2)}, u32[]{:S(2)}) collective-permute-start(s16[16,16,640]{2,1,0:T(8,128)(2,1)S(1)} %all_to_all.16.own_ref), channel_id=1, source_target_pairs={{0,8},{8,0},{16,24},{24,16},{32,40},{40,32},{48,56},{56,48},{64,72... | collective-permute-start | bytes 983048 | tf_op jit(solution)/shard_map/ppermute | solution.py:464
  127.2 1.3 collective-permute-done.2.other_ref
  128.4 1.5 %decode.1 = f32[16,2,16,600]{3,2,1,0:T(8,128)} custom-call(s16[16,16,640]{2,1,0:T(8,128)(2,1)S(1)} %all_to_all.16.own_ref, s16[16,16,640]{2,1,0:T(8,128)(2,1)S(1)} %collective-permute-done.2.other_ref), custom_call_target="tpu_custom_call" | custom-call | tf_op jit(solution)/shard_map/decode/pallas_call | solution.py:383
  (1 shorter events, 0.0 us)
Async XLA Ops:
  1.4 11.2 %collective-permute-start = (bf16[11,32,512]{2,1,0:T(8,128)(2,1)S(1)}, bf16[11,32,512]{2,1,0:T(8,128)(2,1)S(1)}, u32[]{:S(2)}, u32[]{:S(2)}) collective-permute-start(bf16[11,32,512]{2,1,0:T(8,128)(2,1)S(1)} %slice.4), channel_id=1, source_target_pairs={{0,1},{1,2},{2,3},{3,4},{4,5},{5,6},{6,7},{8,9},{9,10},{10,11},{11... | collective-permute-start | bytes 1081352 | tf_op jit(solution)/shard_map/ppermute | solution.py:20
  2.7 1.4 %copy-start = (f32[600,600]{1,0:T(8,128)S(1)}, f32[600,600]{1,0:T(8,128)}, u32[]{:S(2)}) copy-start(f32[600,600]{1,0:T(8,128)} %diag_ref.5) | copy-start | bytes 4320004
  4.1 2.3 %copy-start.16 = (f32[3,600,600]{2,1,0:T(8,128)S(1)}, f32[3,600,600]{2,1,0:T(8,128)}, u32[]{:S(2)}) copy-start(f32[3,600,600]{2,1,0:T(8,128)} %coupling_ref.2) | copy-start | bytes 12960004
  6.4 6.3 %copy-start.15 = (bf16[8,512,600]{1,2,0:T(8,128)(2,1)S(1)}, bf16[8,512,600]{1,2,0:T(8,128)(2,1)}, u32[]{:S(2)}) copy-start(bf16[8,512,600]{1,2,0:T(8,128)(2,1)} %param.7) | copy-start | bytes 14745604
  6.4 6.3 %copy-start.18 = (s32[8]{0:T(128)S(1)}, s32[8]{0:T(128)}, u32[]{:S(2)}) copy-start(s32[8]{0:T(128)} %offsets_ref.1) | copy-start | bytes 100
  12.3 9.4 %copy-start.11 = (bf16[256,640]{1,0:T(8,128)(2,1)}, bf16[256,640]{1,0:T(8,128)(2,1)S(1)}, u32[]{:S(2)}) copy-start(bf16[256,640]{1,0:T(8,128)(2,1)S(1)} %get-tuple-element.25.two_hi) | copy-start | bytes 983044
  12.3 9.4 %copy-start.13 = (bf16[256,640]{1,0:T(8,128)(2,1)}, bf16[256,640]{1,0:T(8,128)(2,1)S(1)}, u32[]{:S(2)}) copy-start(bf16[256,640]{1,0:T(8,128)(2,1)S(1)} %get-tuple-element.26.two_lo) | copy-start | bytes 983044
  21.7 0.8 copy-start.8
  22.5 3.0 %collective-permute-start.1 = (s16[16,16,640]{2,1,0:T(8,128)(2,1)}, s16[16,16,640]{2,1,0:T(8,128)(2,1)S(1)}, u32[]{:S(2)}, u32[]{:S(2)}) collective-permute-start(s16[16,16,640]{2,1,0:T(8,128)(2,1)} %get-tuple-element.29), channel_id=1, source_target_pairs={{0,8},{8,0},{16,24},{24,16},{32,40},{40,32},{48,56},{56,48},{64,72... | collective-permute-start | bytes 983048 | tf_op jit(solution)/shard_map/ppermute | solution.py:453
  25.5 1.1 copy-start.9
  50.1 1.4 %copy-start.1 = (f32[600,600]{1,0:T(8,128)S(1)}, f32[600,600]{1,0:T(8,128)}, u32[]{:S(2)}) copy-start(f32[600,600]{1,0:T(8,128)} %diag_ref.5) | copy-start | bytes 4320004
  51.5 1.1 copy-start.10
  54.1 0.7 copy-start.3
  54.8 15.4 %all-to-all-start.1 = ((f32[8,16,1,640]{3,2,1,0:T(1,128)}), f32[8,16,1,640]{3,2,1,0:T(1,128)S(1)}, u32[]{:S(2)}, u32[]{:S(2)}) async-start(f32[8,16,1,640]{3,2,1,0:T(1,128)} %copy-done.3), calls=%async_computation.1 | async-start | bytes 655360 | tf_op jit(solution)/shard_map/all_to_all | solution.py:460
  61.5 1.4 %copy-start.2 = (f32[600,600]{1,0:T(8,128)S(1)}, f32[600,600]{1,0:T(8,128)}, u32[]{:S(2)}) copy-start(f32[600,600]{1,0:T(8,128)} %diag_ref.5) | copy-start | bytes 4320004
  62.9 2.3 %copy-start.17 = (f32[3,600,600]{2,1,0:T(8,128)S(1)}, f32[3,600,600]{2,1,0:T(8,128)}, u32[]{:S(2)}) copy-start(f32[3,600,600]{2,1,0:T(8,128)} %coupling_ref.2) | copy-start | bytes 12960004
  68.5 0.9 copy-start.4
  69.3 0.9 copy-start.6
  70.3 1.1 copy-start.5
  71.4 1.1 copy-start.7
  72.5 1.0 copy-start.12
  73.5 1.0 copy-start.14
  123.7 4.7 %collective-permute-start.2 = (s16[16,16,640]{2,1,0:T(8,128)(2,1)S(1)}, s16[16,16,640]{2,1,0:T(8,128)(2,1)S(1)}, u32[]{:S(2)}, u32[]{:S(2)}) collective-permute-start(s16[16,16,640]{2,1,0:T(8,128)(2,1)S(1)} %all_to_all.16.own_ref), channel_id=1, source_target_pairs={{0,8},{8,0},{16,24},{24,16},{32,40},{40,32},{48,56},{56,48},{64,72... | collective-permute-start | bytes 983048 | tf_op jit(solution)/shard_map/ppermute | solution.py:464

commit v9 on v6

--- a/solution.py
+++ b/solution.py
@@ -358,6 +358,7 @@
         in_specs=[pl.BlockSpec(memory_space=pltpu.VMEM)] * 2,
         out_specs=pl.BlockSpec(memory_space=pltpu.VMEM),
         name="merge",
+        compiler_params=pltpu.CompilerParams(vmem_limit_bytes=4 << 20),
     )(own, code)
 
 
@@ -381,6 +382,7 @@
         in_specs=[pl.BlockSpec(memory_space=pltpu.VMEM)] * 2,
         out_specs=pl.BlockSpec(memory_space=pltpu.VMEM),
         name="decode",
+        compiler_params=pltpu.CompilerParams(vmem_limit_bytes=6 << 20),
     )(own, other)
     return out.reshape(2 * pairs, steps, sensors)
 

time: 128 us -> 124 us (0.969)
  Pallas kernels: 69.3 us -> 66.3 us
    pallas_call x1, Pallas kernels: 2.74 us -> 0.82 us  [merge(): pl.pallas_call(functools.partial(merge_kernel, sensors), out_shape=jax.Sh...]
    unnamed x9 -> x5, local copies, waits for them, and re-layouts: 3.53 us -> 3.16 us
  transfers between devices with their start and end apart: 4 -> 4, of which waited for: 3 -> 3; matrix products, arithmetic and copies ran while one was open for 0% -> 0% of each run, Pallas kernels for 12% -> 13%
where the time goes in v9:
time: 124 us
  Pallas kernels  66.3 us (53%)
  blocking collectives  37.2 us (30%)
  starting transfers between devices  13.1 us (11%)
  local copies, waits for them, and re-layouts  3.19 us (3%)
  waiting for transfers between devices  2.92 us (2%)
    all_to_all x2, blocking collectives, per_device(): lax.all_to_all(code, 'param', 0, 0, tiled=True, axis_index_groups=chips)  37.2 us
    pallas_call x1, Pallas kernels, run_chain(): pl.pallas_call(functools.partial(chain_kernel, block, sensors), out_shape...  34.9 us
    pallas_call x1, Pallas kernels, prepare_near(): pl.pallas_call(near_kernel, out_shape=(jax.ShapeDtypeStruct((2, sensors,...  9.7 us
    pallas_call x1, Pallas kernels, predict(): pl.pallas_call(predict_kernel, out_shape=(jax.ShapeDtypeStruct((samples /...  9.53 us
    all_to_all x1, starting transfers between devices, per_device(): every = lax.all_to_all(forced, 'tm', 0, 0, tiled=True)  6.84 us
    pallas_call x1, Pallas kernels, prepare_far(): pl.pallas_call(far_kernel, out_shape=(part, part), in_specs=[pl.BlockSpec...  6.12 us
    pallas_call x1, Pallas kernels, force(): pl.pallas_call(forcing_kernel, out_shape=jax.ShapeDtypeStruct((copies, st...  3.72 us
    ppermute x1, starting transfers between devices, per_device(): return decode(code, lax.ppermute(code, 'param', partner), sensors)  3.37 us
  transfers between devices with their start and end apart: 4, of which 3 were waited for; matrix products, arithmetic and copies ran while one was open for 0% of the time, Pallas kernels for 13%

profile of v9, /device:TPU:39, one launch (start us, length us, event | category | flops | bytes accessed | tf_op | source)
XLA Modules:
  0.0 123.8 jit_solution(3690830947745533066)
XLA Ops:
  0.0 1.3 %copy.9 = bf16[32,16,512]{2,0,1:T(8,128)(2,1)S(1)} copy(bf16[32,16,512]{2,1,0:T(8,128)(2,1)} %param.6) | data formatting | bytes 1048576 | tf_op args[0]
  1.4 1.3 %collective-permute-start = (bf16[11,32,512]{2,1,0:T(8,128)(2,1)S(1)}, bf16[11,32,512]{2,1,0:T(8,128)(2,1)S(1)}, u32[]{:S(2)}, u32[]{:S(2)}) collective-permute-start(bf16[11,32,512]{2,1,0:T(8,128)(2,1)S(1)} %slice.4), channel_id=1, source_target_pairs={{0,1},{1,2},{2,3},{3,4},{4,5},{5,6},{6,7},{8,9},{9,10},{10,11},{11... | collective-permute-start | bytes 1081352 | tf_op jit(solution)/shard_map/ppermute | solution.py:20
  2.7 9.7 %near_factors.1 = (f32[2,600,640]{2,1,0:T(8,128)}, bf16[256,640]{1,0:T(8,128)(2,1)}, bf16[256,640]{1,0:T(8,128)(2,1)}) custom-call(f32[600,600]{1,0:T(8,128)} %diag_ref.5, f32[3,600,600]{2,1,0:T(8,128)} %coupling_ref.2), custom_call_target="tpu_custom_call" | custom-call | flops 5184000000 | bytes 5760000 | tf_op jit(solution)/shard_map/near_factors/pallas_call | solution.py:209
  12.4 0.2 collective-permute-done
  12.6 1.0 pad_maximum_fusion.source_ref
  13.5 9.5 %predict.1 = (s16[16,16,640]{2,1,0:T(8,128)(2,1)}, f32[16,16,640]{2,1,0:T(8,128)}) custom-call(s32[8]{0:T(128)} %offsets_ref.1, bf16[27,32,512]{2,1,0:T(8,128)(2,1)} %pad_maximum_fusion.source_ref, bf16[8,600,512]{2,1,0:T(8,128)(2,1)} %bitcast.10), custom_call_target="tpu_custom_call" | custom-call | flops 2516582400 | bytes 4915200 | tf_op jit(solution)/shard_map/predict/pallas_call | solution.py:310
  23.1 1.6 %collective-permute-start.1 = (s16[16,16,640]{2,1,0:T(8,128)(2,1)}, s16[16,16,640]{2,1,0:T(8,128)(2,1)S(1)}, u32[]{:S(2)}, u32[]{:S(2)}) collective-permute-start(s16[16,16,640]{2,1,0:T(8,128)(2,1)} %get-tuple-element.29), channel_id=1, source_target_pairs={{0,8},{8,0},{16,24},{24,16},{32,40},{40,32},{48,56},{56,48},{64,72... | collective-permute-start | bytes 983048 | tf_op jit(solution)/shard_map/ppermute | solution.py:448
  24.7 1.5 %collective-permute-done.1.code_ref = s16[16,16,640]{2,1,0:T(8,128)(2,1)S(1)} collective-permute-done((s16[16,16,640]{2,1,0:T(8,128)(2,1)}, s16[16,16,640]{2,1,0:T(8,128)(2,1)S(1)}, u32[]{:S(2)}, u32[]{:S(2)}) %collective-permute-start.1) | collective-permute-done | bytes 327712 | tf_op jit(solution)/shard_map/ppermute | solution.py:448
  26.2 0.0 copy-start
  26.2 1.1 copy-done
  27.3 0.8 merge.1
  28.1 22.8 %all_to_all.15.code_ref = s16[16,16,640]{2,1,0:T(8,128)(2,1)} all-to-all(s16[16,16,640]{2,1,0:T(8,128)(2,1)S(1)} %merge.1), channel_id=1, replica_groups={{0,16,32,48,64,80,96,112,128,144,160,176,192,208,224,240},{8,24,40,56,7..., dimensions={0} | all-to-all | bytes 655360 | tf_op jit(solution)/shard_map/all_to_all | solution.py:451
  50.9 3.7 %forcing.1 = f32[8,16,1,640]{3,2,1,0:T(1,128)} custom-call(s32[1]{0:T(128)} %bitcast.2.place_ref, s16[16,16,640]{2,1,0:T(8,128)(2,1)} %all_to_all.15.code_ref, bf16[32,16,600]{2,1,0:T(8,128)(2,1)} %observed_ref.1, f32[600,600]{1,0:T(8,128)} %diag_ref.5), custom_call_target="tpu_custom_call" | custom-call | tf_op jit(solution)/shard_map/forcing/pallas_call | solution.py:415
  54.6 6.8 %all-to-all-start.1 = ((f32[8,16,1,640]{3,2,1,0:T(1,128)}), f32[8,16,1,640]{3,2,1,0:T(1,128)S(1)}, u32[]{:S(2)}, u32[]{:S(2)}) async-start(f32[8,16,1,640]{3,2,1,0:T(1,128)} %forcing.1), calls=%async_computation.1 | async-start | bytes 655360 | tf_op jit(solution)/shard_map/all_to_all | solution.py:455
  61.4 6.1 %far_factors.1 = (bf16[640,640]{1,0:T(8,128)(2,1)}, bf16[640,640]{1,0:T(8,128)(2,1)}) custom-call(f32[600,600]{1,0:T(8,128)} %diag_ref.5, f32[3,600,600]{2,1,0:T(8,128)} %coupling_ref.2), custom_call_target="tpu_custom_call" | custom-call | flops 2592000000 | bytes 4320000 | tf_op jit(solution)/shard_map/far_factors/pallas_call | solution.py:233
  67.6 0.0 all-to-all-done.1
  67.6 0.0 copy-start.1
  67.6 0.7 copy-done.1
  68.3 34.9 %chain.1 = (s16[16,16,640]{2,1,0:T(8,128)(2,1)}, f32[16,1,640]{2,1,0:T(1,128)}) custom-call(f32[2,600,640]{2,1,0:T(8,128)} %get-tuple-element.24.near_ref, bf16[256,640]{1,0:T(8,128)(2,1)} %get-tuple-element.25.two_hi, bf16[256,640]{1,0:T(8,128)(2,1)} %get-tuple-element.26.two_lo, bf16[640,640]{1,0:T(8,128)(2,1)} %get-tuple-element.33.three_hi, ...), custom_call_target="tpu_custom_call" | custom-call | tf_op jit(solution)/shard_map/chain/pallas_call | solution.py:138
  103.2 14.5 %all_to_all.16.own_ref = s16[16,16,640]{2,1,0:T(8,128)(2,1)S(1)} all-to-all(s16[16,16,640]{2,1,0:T(8,128)(2,1)} %get-tuple-element.36), channel_id=1, replica_groups={{0,16,32,48,64,80,96,112,128,144,160,176,192,208,224,240},{8,24,40,56,7..., dimensions={0} | all-to-all | bytes 655360 | tf_op jit(solution)/shard_map/all_to_all | solution.py:458
  117.7 3.4 %collective-permute-start.2 = (s16[16,16,640]{2,1,0:T(8,128)(2,1)S(1)}, s16[16,16,640]{2,1,0:T(8,128)(2,1)S(1)}, u32[]{:S(2)}, u32[]{:S(2)}) collective-permute-start(s16[16,16,640]{2,1,0:T(8,128)(2,1)S(1)} %all_to_all.16.own_ref), channel_id=1, source_target_pairs={{0,8},{8,0},{16,24},{24,16},{32,40},{40,32},{48,56},{56,48},{64,72... | collective-permute-start | bytes 983048 | tf_op jit(solution)/shard_map/ppermute | solution.py:459
  121.1 1.3 %collective-permute-done.2.other_ref = s16[16,16,640]{2,1,0:T(8,128)(2,1)S(1)} collective-permute-done((s16[16,16,640]{2,1,0:T(8,128)(2,1)S(1)}, s16[16,16,640]{2,1,0:T(8,128)(2,1)S(1)}, u32[]{:S(2)}, u32[]{:S(2)}) %collective-permute-start.2) | collective-permute-done | bytes 327712 | tf_op jit(solution)/shard_map/ppermute | solution.py:459
  122.3 1.5 %decode.1 = f32[16,2,16,600]{3,2,1,0:T(8,128)} custom-call(s16[16,16,640]{2,1,0:T(8,128)(2,1)S(1)} %all_to_all.16.own_ref, s16[16,16,640]{2,1,0:T(8,128)(2,1)S(1)} %collective-permute-done.2.other_ref), custom_call_target="tpu_custom_call" | custom-call | tf_op jit(solution)/shard_map/decode/pallas_call | solution.py:379
  (1 shorter events, 0.0 us)
Async XLA Ops:
  1.4 11.2 %collective-permute-start = (bf16[11,32,512]{2,1,0:T(8,128)(2,1)S(1)}, bf16[11,32,512]{2,1,0:T(8,128)(2,1)S(1)}, u32[]{:S(2)}, u32[]{:S(2)}) collective-permute-start(bf16[11,32,512]{2,1,0:T(8,128)(2,1)S(1)} %slice.4), channel_id=1, source_target_pairs={{0,1},{1,2},{2,3},{3,4},{4,5},{5,6},{6,7},{8,9},{9,10},{10,11},{11... | collective-permute-start | bytes 1081352 | tf_op jit(solution)/shard_map/ppermute | solution.py:20
  23.1 3.1 %collective-permute-start.1 = (s16[16,16,640]{2,1,0:T(8,128)(2,1)}, s16[16,16,640]{2,1,0:T(8,128)(2,1)S(1)}, u32[]{:S(2)}, u32[]{:S(2)}) collective-permute-start(s16[16,16,640]{2,1,0:T(8,128)(2,1)} %get-tuple-element.29), channel_id=1, source_target_pairs={{0,8},{8,0},{16,24},{24,16},{32,40},{40,32},{48,56},{56,48},{64,72... | collective-permute-start | bytes 983048 | tf_op jit(solution)/shard_map/ppermute | solution.py:448
  26.2 1.1 copy-start
  54.6 13.0 %all-to-all-start.1 = ((f32[8,16,1,640]{3,2,1,0:T(1,128)}), f32[8,16,1,640]{3,2,1,0:T(1,128)S(1)}, u32[]{:S(2)}, u32[]{:S(2)}) async-start(f32[8,16,1,640]{3,2,1,0:T(1,128)} %forcing.1), calls=%async_computation.1 | async-start | bytes 655360 | tf_op jit(solution)/shard_map/all_to_all | solution.py:455
  67.6 0.7 copy-start.1
  117.7 4.6 %collective-permute-start.2 = (s16[16,16,640]{2,1,0:T(8,128)(2,1)S(1)}, s16[16,16,640]{2,1,0:T(8,128)(2,1)S(1)}, u32[]{:S(2)}, u32[]{:S(2)}) collective-permute-start(s16[16,16,640]{2,1,0:T(8,128)(2,1)S(1)} %all_to_all.16.own_ref), channel_id=1, source_target_pairs={{0,8},{8,0},{16,24},{24,16},{32,40},{40,32},{48,56},{56,48},{64,72... | collective-permute-start | bytes 983048 | tf_op jit(solution)/shard_map/ppermute | solution.py:459

commit v10 on v7

--- a/solution.py
+++ b/solution.py
@@ -122,11 +122,11 @@
 
     turns = (lax.axis_index("tm") + 1) * (block // 2)
     def several(group, unused):
-        for member in range(4):
-            unused = pair(4 * group + member, unused)
-        return unused
-
-    lax.fori_loop(0, turns // 4, several, 0)
+        for member in range(8):
+            unused = pair(8 * group + member, unused)
+        return unused
+
+    lax.fori_loop(0, turns // 8, several, 0)
     own = jnp.concatenate([solved_ref[row] for row in range(block)], axis=0)
     code = coded_with_grade(own, sensors)
     for copy in range(code_ref.shape[0]):
@@ -359,19 +359,24 @@
 def merge_kernel(sensors, own_ref, code_ref, merged_ref):
     lane = lax.broadcasted_iota(jnp.int32, own_ref.shape[1:], 1)
 
-    for pair in range(own_ref.shape[0]):
-        other = jnp.where(lane < sensors, decoded(code_ref[pair], sensors), 0.0)
-        merged_ref[pair] = coded_with_grade(own_ref[pair] + other, sensors)
+    def several(group, unused):
+        for member in range(4):
+            pair = 4 * group + member
+            other = jnp.where(lane < sensors, decoded(code_ref[pair], sensors), 0.0)
+            merged_ref[pair] = coded_with_grade(own_ref[pair] + other, sensors)
+        return unused
+
+    lax.fori_loop(0, own_ref.shape[0] // 4, several, 0)
 
 
 def merge(own, code, sensors):
     return pl.pallas_call(
         functools.partial(merge_kernel, sensors),
         out_shape=jax.ShapeDtypeStruct(code.shape, code.dtype),
-        in_specs=[pl.BlockSpec((4, *own.shape[1:]), lambda i: (i, 0, 0))] * 2,
-        out_specs=pl.BlockSpec((4, *own.shape[1:]), lambda i: (i, 0, 0)),
-        grid=(own.shape[0] // 4,),
+        in_specs=[pl.BlockSpec(memory_space=pltpu.VMEM)] * 2,
+        out_specs=pl.BlockSpec(memory_space=pltpu.VMEM),
         name="merge",
+        compiler_params=pltpu.CompilerParams(vmem_limit_bytes=4 << 20),
     )(own, code)
 
 
@@ -379,9 +384,12 @@
     sensors = out_ref.shape[3]
     core = lax.rem(lax.axis_index("param"), 2)
 
-    for pair in range(own_ref.shape[0]):
+    def one(pair, unused):
         out_ref[pair, core] = decoded(own_ref[pair], sensors)[:, :sensors]
         out_ref[pair, 1 - core] = decoded(other_ref[pair], sensors)[:, :sensors]
+        return unused
+
+    lax.fori_loop(0, own_ref.shape[0], one, 0, unroll=4)
 
 
 def decode(own, other, sensors):
@@ -389,10 +397,10 @@
     out = pl.pallas_call(
         decode_kernel,
         out_shape=jax.ShapeDtypeStruct((pairs, 2, steps, sensors), jnp.float32),
-        in_specs=[pl.BlockSpec((4, *own.shape[1:]), lambda i: (i, 0, 0))] * 2,
-        out_specs=pl.BlockSpec((4, 2, steps, sensors), lambda i: (i, 0, 0, 0)),
-        grid=(pairs // 4,),
+        in_specs=[pl.BlockSpec(memory_space=pltpu.VMEM)] * 2,
+        out_specs=pl.BlockSpec(memory_space=pltpu.VMEM),
         name="decode",
+        compiler_params=pltpu.CompilerParams(vmem_limit_bytes=6 << 20),
     )(own, other)
     return out.reshape(2 * pairs, steps, sensors)
 

time: 130 us -> 124 us (0.954)
  Pallas kernels: 71 us -> 65.9 us
    pallas_call x1, Pallas kernels: 3.62 us -> 0.82 us  [merge(): pl.pallas_call(functools.partial(merge_kernel, sensors), out_shape=jax.Sh...]
    pallas_call x1, Pallas kernels: 3.52 us -> 1.47 us  [decode(): pl.pallas_call(decode_kernel, out_shape=jax.ShapeDtypeStruct((pairs, 2, s...]
    unnamed x13 -> x9, local copies, waits for them, and re-layouts: 4.3 us -> 3.92 us
  transfers between devices with their start and end apart: 4 -> 4, of which waited for: 3 -> 3; matrix products, arithmetic and copies ran while one was open for 0% -> 0% of each run, Pallas kernels for 12% -> 13%
where the time goes in v10:
time: 124 us; the launch traced here: 123 us
  Pallas kernels  65.9 us (53%)
  blocking collectives  37.1 us (30%)
  starting transfers between devices  13.3 us (11%)
  local copies, waits for them, and re-layouts  3.94 us (3%)
  waiting for transfers between devices  2.93 us (2%)
    all_to_all x2, blocking collectives, per_device(): lax.all_to_all(code, 'param', 0, 0, tiled=True, axis_index_groups=chips)  37.1 us
    pallas_call x1, Pallas kernels, run_chain(): pl.pallas_call(functools.partial(chain_kernel, block, sensors), out_shape...  34.6 us
    pallas_call x1, Pallas kernels, prepare_near(): pl.pallas_call(near_kernel, out_shape=(jax.ShapeDtypeStruct((2, sensors,...  9.69 us
    pallas_call x1, Pallas kernels, predict(): pl.pallas_call(predict_kernel, out_shape=(jax.ShapeDtypeStruct((samples /...  9.48 us
    all_to_all x1, starting transfers between devices, per_device(): every = lax.all_to_all(forced, 'tm', 0, 0, tiled=True)  6.98 us
    pallas_call x1, Pallas kernels, prepare_far(): pl.pallas_call(far_kernel, out_shape=(part, part), in_specs=[pl.BlockSpec...  6.12 us
    unnamed x9, local copies, waits for them, and re-layouts  3.92 us
    pallas_call x1, Pallas kernels, force(): pl.pallas_call(forcing_kernel, out_shape=jax.ShapeDtypeStruct((copies, st...  3.72 us
  transfers between devices with their start and end apart: 4, of which 3 were waited for; matrix products, arithmetic and copies ran while one was open for 0% of the time, Pallas kernels for 13%

profile of v10, /device:TPU:39, one launch (start us, length us, event | category | flops | bytes accessed | tf_op | source)
XLA Modules:
  0.0 123.3 jit_solution(5025361490396065375)
XLA Ops:
  0.0 1.3 %copy.9 = bf16[32,16,512]{2,0,1:T(8,128)(2,1)S(1)} copy(bf16[32,16,512]{2,1,0:T(8,128)(2,1)} %param.6) | data formatting | bytes 1048576 | tf_op args[0]
  1.3 0.0 copy-start.1
  1.4 1.3 %collective-permute-start = (bf16[11,32,512]{2,1,0:T(8,128)(2,1)S(1)}, bf16[11,32,512]{2,1,0:T(8,128)(2,1)S(1)}, u32[]{:S(2)}, u32[]{:S(2)}) collective-permute-start(bf16[11,32,512]{2,1,0:T(8,128)(2,1)S(1)} %slice.4), channel_id=1, source_target_pairs={{0,1},{1,2},{2,3},{3,4},{4,5},{5,6},{6,7},{8,9},{9,10},{10,11},{11... | collective-permute-start | bytes 1081352 | tf_op jit(solution)/shard_map/ppermute | solution.py:21
  2.7 9.7 %near_factors.1 = (f32[2,600,640]{2,1,0:T(8,128)}, bf16[256,640]{1,0:T(8,128)(2,1)}, bf16[256,640]{1,0:T(8,128)(2,1)}) custom-call(f32[600,600]{1,0:T(8,128)} %diag_ref.5, f32[3,600,600]{2,1,0:T(8,128)} %coupling_ref.2), custom_call_target="tpu_custom_call" | custom-call | flops 5184000000 | bytes 5760000 | tf_op jit(solution)/shard_map/near_factors/pallas_call | solution.py:210
  12.4 0.0 copy-done.1
  12.4 0.2 collective-permute-done.rim_hbm
  12.6 0.0 copy-start.3
  12.6 0.7 copy-done.3
  13.3 9.5 %predict.1 = (s16[16,16,640]{2,1,0:T(8,128)(2,1)}, f32[16,16,640]{2,1,0:T(8,128)}) custom-call(s32[8]{0:T(128)} %offsets_ref.1, bf16[11,32,512]{2,1,0:T(8,128)(2,1)} %copy-done.3, bf16[16,32,512]{2,1,0:T(8,128)(2,1)} %bitcast.8, bf16[8,600,512]{2,1,0:T(8,128)(2,1)} %bitcast.10), custom_call_target="tpu_custom_call" | custom-call | flops 2516582400 | bytes 4915200 | tf_op jit(solution)/shard_map/predict/pallas_call | solution.py:325
  22.8 1.6 %collective-permute-start.1 = (s16[16,16,640]{2,1,0:T(8,128)(2,1)}, s16[16,16,640]{2,1,0:T(8,128)(2,1)S(1)}, u32[]{:S(2)}, u32[]{:S(2)}) collective-permute-start(s16[16,16,640]{2,1,0:T(8,128)(2,1)} %get-tuple-element.29), channel_id=1, source_target_pairs={{0,8},{8,0},{16,24},{24,16},{32,40},{40,32},{48,56},{56,48},{64,72... | collective-permute-start | bytes 983048 | tf_op jit(solution)/shard_map/ppermute | solution.py:464
  24.4 1.5 %collective-permute-done.1.code_ref = s16[16,16,640]{2,1,0:T(8,128)(2,1)S(1)} collective-permute-done((s16[16,16,640]{2,1,0:T(8,128)(2,1)}, s16[16,16,640]{2,1,0:T(8,128)(2,1)S(1)}, u32[]{:S(2)}, u32[]{:S(2)}) %collective-permute-start.1) | collective-permute-done | bytes 327712 | tf_op jit(solution)/shard_map/ppermute | solution.py:464
  25.9 0.0 copy-start
  25.9 1.1 copy-done
  27.0 0.8 merge.1
  27.8 22.7 %all_to_all.15.code_ref = s16[16,16,640]{2,1,0:T(8,128)(2,1)} all-to-all(s16[16,16,640]{2,1,0:T(8,128)(2,1)S(1)} %merge.1), channel_id=1, replica_groups={{0,16,32,48,64,80,96,112,128,144,160,176,192,208,224,240},{8,24,40,56,7..., dimensions={0} | all-to-all | bytes 655360 | tf_op jit(solution)/shard_map/all_to_all | solution.py:467
  50.5 3.7 %forcing.1 = f32[8,16,1,640]{3,2,1,0:T(1,128)} custom-call(s32[1]{0:T(128)} %bitcast.2.place_ref, s16[16,16,640]{2,1,0:T(8,128)(2,1)} %all_to_all.15.code_ref, bf16[32,16,600]{2,1,0:T(8,128)(2,1)} %observed_ref.1, f32[600,600]{1,0:T(8,128)} %diag_ref.5), custom_call_target="tpu_custom_call" | custom-call | tf_op jit(solution)/shard_map/forcing/pallas_call | solution.py:433
  54.2 7.0 %all-to-all-start.1 = ((f32[8,16,1,640]{3,2,1,0:T(1,128)}), f32[8,16,1,640]{3,2,1,0:T(1,128)S(1)}, u32[]{:S(2)}, u32[]{:S(2)}) async-start(f32[8,16,1,640]{3,2,1,0:T(1,128)} %forcing.1), calls=%async_computation.1 | async-start | bytes 655360 | tf_op jit(solution)/shard_map/all_to_all | solution.py:471
  61.2 6.1 %far_factors.1 = (bf16[640,640]{1,0:T(8,128)(2,1)}, bf16[640,640]{1,0:T(8,128)(2,1)}) custom-call(f32[600,600]{1,0:T(8,128)} %diag_ref.5, f32[3,600,600]{2,1,0:T(8,128)} %coupling_ref.2), custom_call_target="tpu_custom_call" | custom-call | flops 2592000000 | bytes 4320000 | tf_op jit(solution)/shard_map/far_factors/pallas_call | solution.py:234
  67.3 0.0 all-to-all-done.1
  67.3 0.0 copy-start.2
  67.3 0.7 copy-done.2
  68.1 34.6 %chain.1 = (s16[16,16,640]{2,1,0:T(8,128)(2,1)}, f32[16,1,640]{2,1,0:T(1,128)}) custom-call(f32[2,600,640]{2,1,0:T(8,128)} %get-tuple-element.24.near_ref, bf16[256,640]{1,0:T(8,128)(2,1)} %get-tuple-element.25.two_hi, bf16[256,640]{1,0:T(8,128)(2,1)} %get-tuple-element.26.two_lo, bf16[640,640]{1,0:T(8,128)(2,1)} %get-tuple-element.33.three_hi, ...), custom_call_target="tpu_custom_call" | custom-call | tf_op jit(solution)/shard_map/chain/pallas_call | solution.py:139
  102.7 14.5 %all_to_all.16.own_ref = s16[16,16,640]{2,1,0:T(8,128)(2,1)S(1)} all-to-all(s16[16,16,640]{2,1,0:T(8,128)(2,1)} %get-tuple-element.36), channel_id=1, replica_groups={{0,16,32,48,64,80,96,112,128,144,160,176,192,208,224,240},{8,24,40,56,7..., dimensions={0} | all-to-all | bytes 655360 | tf_op jit(solution)/shard_map/all_to_all | solution.py:474
  117.2 3.4 %collective-permute-start.2 = (s16[16,16,640]{2,1,0:T(8,128)(2,1)S(1)}, s16[16,16,640]{2,1,0:T(8,128)(2,1)S(1)}, u32[]{:S(2)}, u32[]{:S(2)}) collective-permute-start(s16[16,16,640]{2,1,0:T(8,128)(2,1)S(1)} %all_to_all.16.own_ref), channel_id=1, source_target_pairs={{0,8},{8,0},{16,24},{24,16},{32,40},{40,32},{48,56},{56,48},{64,72... | collective-permute-start | bytes 983048 | tf_op jit(solution)/shard_map/ppermute | solution.py:475
  120.5 1.3 %collective-permute-done.2.other_ref = s16[16,16,640]{2,1,0:T(8,128)(2,1)S(1)} collective-permute-done((s16[16,16,640]{2,1,0:T(8,128)(2,1)S(1)}, s16[16,16,640]{2,1,0:T(8,128)(2,1)S(1)}, u32[]{:S(2)}, u32[]{:S(2)}) %collective-permute-start.2) | collective-permute-done | bytes 327712 | tf_op jit(solution)/shard_map/ppermute | solution.py:475
  121.8 1.5 %decode.1 = f32[16,2,16,600]{3,2,1,0:T(8,128)} custom-call(s16[16,16,640]{2,1,0:T(8,128)(2,1)S(1)} %all_to_all.16.own_ref, s16[16,16,640]{2,1,0:T(8,128)(2,1)S(1)} %collective-permute-done.2.other_ref), custom_call_target="tpu_custom_call" | custom-call | tf_op jit(solution)/shard_map/decode/pallas_call | solution.py:397
  (1 shorter events, 0.0 us)
Async XLA Ops:
  1.3 11.0 %copy-start.1 = (bf16[32,16,512]{2,0,1:T(8,128)(2,1)}, bf16[32,16,512]{2,0,1:T(8,128)(2,1)S(1)}, u32[]{:S(2)}) copy-start(bf16[32,16,512]{2,0,1:T(8,128)(2,1)S(1)} %copy.9) | copy-start | bytes 1572868
  1.4 11.2 %collective-permute-start = (bf16[11,32,512]{2,1,0:T(8,128)(2,1)S(1)}, bf16[11,32,512]{2,1,0:T(8,128)(2,1)S(1)}, u32[]{:S(2)}, u32[]{:S(2)}) collective-permute-start(bf16[11,32,512]{2,1,0:T(8,128)(2,1)S(1)} %slice.4), channel_id=1, source_target_pairs={{0,1},{1,2},{2,3},{3,4},{4,5},{5,6},{6,7},{8,9},{9,10},{10,11},{11... | collective-permute-start | bytes 1081352 | tf_op jit(solution)/shard_map/ppermute | solution.py:21
  12.6 0.7 copy-start.3
  22.8 3.1 %collective-permute-start.1 = (s16[16,16,640]{2,1,0:T(8,128)(2,1)}, s16[16,16,640]{2,1,0:T(8,128)(2,1)S(1)}, u32[]{:S(2)}, u32[]{:S(2)}) collective-permute-start(s16[16,16,640]{2,1,0:T(8,128)(2,1)} %get-tuple-element.29), channel_id=1, source_target_pairs={{0,8},{8,0},{16,24},{24,16},{32,40},{40,32},{48,56},{56,48},{64,72... | collective-permute-start | bytes 983048 | tf_op jit(solution)/shard_map/ppermute | solution.py:464
  25.9 1.1 copy-start
  54.2 13.1 %all-to-all-start.1 = ((f32[8,16,1,640]{3,2,1,0:T(1,128)}), f32[8,16,1,640]{3,2,1,0:T(1,128)S(1)}, u32[]{:S(2)}, u32[]{:S(2)}) async-start(f32[8,16,1,640]{3,2,1,0:T(1,128)} %forcing.1), calls=%async_computation.1 | async-start | bytes 655360 | tf_op jit(solution)/shard_map/all_to_all | solution.py:471
  67.3 0.7 copy-start.2
  117.2 4.6 %collective-permute-start.2 = (s16[16,16,640]{2,1,0:T(8,128)(2,1)S(1)}, s16[16,16,640]{2,1,0:T(8,128)(2,1)S(1)}, u32[]{:S(2)}, u32[]{:S(2)}) collective-permute-start(s16[16,16,640]{2,1,0:T(8,128)(2,1)S(1)} %all_to_all.16.own_ref), channel_id=1, source_target_pairs={{0,8},{8,0},{16,24},{24,16},{32,40},{40,32},{48,56},{56,48},{64,72... | collective-permute-start | bytes 983048 | tf_op jit(solution)/shard_map/ppermute | solution.py:475
